TPU v7x, 32 devices: a whole 2x2x4 slice. The times are simulated.
32 devices in a mesh: seq: 16 (over z, y, core), head: 2 (over x).
Axes of the slice: x: 2, y: 2, z: 4, core: 2. Of those that a mesh axis runs over, the one named last changes fastest.
Arguments:
- query: bfloat16 [16384, 1024], P('seq', 'head'), may hold values from -48 to 48
- key: bfloat16 [16384, 1024], P('seq', 'head'), may hold values from -48 to 48
- value: bfloat16 [16384, 1024], P('seq', 'head'), may hold values from -6 to 6
- out_grad: bfloat16 [16384, 1024], P('seq', 'head'), may hold values from -6 to 6
- pool_group: float32 [16, 64], P('head'), may hold values from -0.75 to 0.75
- pool_global: float32 [16, 256], P('head'), may hold values from -0.375 to 0.375
Outputs:
- query_grad: bfloat16 [16384, 1024], P('seq', 'head')
- key_grad: bfloat16 [16384, 1024], P('seq', 'head')
- value_grad: bfloat16 [16384, 1024], P('seq', 'head')
All inputs are finite; a program needn't handle non-finite values.
Results may differ from a plain program's by a relative error of at most 0.04.
Values may be sent and summed in bfloat16 or wider, within the bound.
No kernel may reach another device: no remote copies, remote signals or barrier semaphores. Data moves between devices by JAX's collectives and lax.ppermute only.
A program may use at most 64 MiB of HBM per device.

v0:
```python
import functools
import math

import jax
import jax.numpy as jnp
from jax import lax
from jax.experimental import pallas as pl
from jax.experimental.pallas import tpu as pltpu
from jax.sharding import PartitionSpec as P

BLOCK = 256
SEG1 = 64
SEG2 = 256
GROUP = 8
NEG = -1e30
F32 = jnp.float32
BF16 = jnp.bfloat16
NT = (((1,), (1,)), ((), ()))
NN = (((1,), (0,)), ((), ()))
VMEM_LIMIT = 48 * 2**20


def dot(a, b, dims):
    return lax.dot_general(a, b, dims, preferred_element_type=F32)


def struct(shape, dtype):
    return jax.ShapeDtypeStruct(shape, dtype)


def call(body, name, flops=0, moved=0, **kwargs):
    cost = pl.CostEstimate(flops=int(flops), bytes_accessed=int(moved), transcendentals=0)
    params = pltpu.CompilerParams(vmem_limit_bytes=VMEM_LIMIT)
    return pl.pallas_call(body, name=name, cost_estimate=cost, compiler_params=params, **kwargs)


def head_masks(width, depth):
    lane = lax.broadcasted_iota(jnp.int32, (1, width), 1)
    return [(lane >= h * depth) & (lane < (h + 1) * depth) for h in range(width // depth)]


def keep_head(rows, mask, scale=None):
    rows = jnp.where(mask, rows, 0)
    if scale is not None:
        rows = rows.astype(F32) * scale
    return rows.astype(BF16)


def near(block, blocks):
    return range(max(block - 1, 0), min(block + 2, blocks))


def pool_body(k, v, group_pool, whole_pool, own, first, last, wide_group, wide_whole):
    rows, cols = k.shape
    heads = group_pool.shape[0]
    depth = cols // heads
    head = lax.broadcasted_iota(jnp.int32, (heads, cols), 0)
    col = lax.broadcasted_iota(jnp.int32, (heads, cols), 1)
    pick = ((col >= head * depth) & (col < (head + 1) * depth)).astype(F32)
    tn = (((0,), (0,)), ((), ()))
    exact = lax.Precision.HIGHEST
    wide_group[...] = lax.dot_general(
        group_pool[...], pick, tn, precision=exact, preferred_element_type=F32
    )
    wide_whole[...] = lax.dot_general(
        whole_pool[...], pick, tn, precision=exact, preferred_element_type=F32
    )
    count1 = rows // SEG1
    for n, src in enumerate((k, v)):
        first[n] = src[:BLOCK]
        last[n] = src[rows - BLOCK :]
        sums = []
        for s in range(count1):
            part = src[s * SEG1 : (s + 1) * SEG1].astype(F32) * wide_group[...]
            sums.append(jnp.sum(part, axis=0, keepdims=True))
        for s in range(rows // SEG2):
            part = src[s * SEG2 : (s + 1) * SEG2].astype(F32) * wide_whole[...]
            sums.append(jnp.sum(part, axis=0, keepdims=True))
        pad = own.shape[2] - len(sums)
        if pad:
            sums.append(jnp.zeros((pad, cols), F32))
        own[0, n] = jnp.concatenate(sums, axis=0).astype(BF16)


def pool(k, v, group_pool, whole_pool):
    rows, cols = k.shape
    count = rows // SEG1 + rows // SEG2
    padded = -(-count // 8) * 8
    return call(
        pool_body,
        "pool",
        moved=k.size * 8,
        out_shape=[
            struct((1, 2, padded, cols), BF16),
            struct((2, BLOCK, cols), BF16),
            struct((2, BLOCK, cols), BF16),
            struct((SEG1, cols), F32),
            struct((SEG2, cols), F32),
        ],
    )(k, v, group_pool, whole_pool)


def pack_body(count1, count2, comb, whole, out):
    slots1, slots2 = comb.shape[0], whole.shape[0]
    for n in range(2):
        parts = [comb[s, n, :count1] for s in range(slots1)]
        parts += [whole[s, n] for s in range(slots2)]
        out[n] = jnp.concatenate([p.astype(F32) for p in parts], axis=0).astype(BF16)


def pack(comb, whole, count1, count2):
    cols = comb.shape[-1]
    rows = comb.shape[0] * count1 + whole.shape[0] * count2
    return call(
        functools.partial(pack_body, count1, count2),
        "pack",
        moved=comb.size * 4,
        out_shape=struct((2, rows, cols), BF16),
    )(comb, whole)


def stats_body(depth, scale, q, k, v, g, out):
    rows, width = q.shape
    blocks = rows // BLOCK
    chunk = 64
    for h, mask in enumerate(head_masks(width, depth)):
        for b in range(blocks):
            r = slice(b * BLOCK, (b + 1) * BLOCK)
            qs = keep_head(q[r], mask, scale)
            gs = keep_head(g[r], mask)
            lo, hi = near(b, blocks)[0] * BLOCK, (near(b, blocks)[-1] + 1) * BLOCK
            s_all = dot(k[lo:hi], qs, NT)
            d_all = dot(v[lo:hi], gs, NT)
            top = total = inner = None
            for c in range(0, hi - lo, chunk):
                s = s_all[c : c + chunk].reshape(chunk // 8, 8, BLOCK)
                d = d_all[c : c + chunk].reshape(chunk // 8, 8, BLOCK)
                here = jnp.max(s, axis=0)
                if top is None:
                    new = here
                else:
                    new = jnp.maximum(top, here)
                e = jnp.exp(s - new[None])
                sum_e = jnp.sum(e, axis=0)
                sum_d = jnp.sum(e * d, axis=0)
                if top is not None:
                    fade = jnp.exp(top - new)
                    sum_e = sum_e + total * fade
                    sum_d = sum_d + inner * fade
                top, total, inner = new, sum_e, sum_d
            most = jnp.max(top, axis=0, keepdims=True)
            fade = jnp.exp(top - most)
            out[0, h : h + 1, r] = most
            out[1, h : h + 1, r] = jnp.sum(total * fade, axis=0, keepdims=True)
            out[2, h : h + 1, r] = jnp.sum(inner * fade, axis=0, keepdims=True)


def stats(q, k, v, g, width, depth, scale, pair):
    rows = q.shape[0]
    hp = width // depth
    cols = pl.BlockSpec((rows, width), lambda i: (0, pair))
    return call(
        functools.partial(stats_body, depth, scale),
        f"stats{pair}",
        flops=2 * 2 * 3 * BLOCK * rows * width,
        moved=rows * width * 8,
        grid=(1,),
        in_specs=[cols] * 4,
        out_specs=pl.BlockSpec((3, hp, rows), lambda i: (0, 0, 0)),
        out_shape=struct((3, hp, rows), F32),
    )(q, k, v, g)


def remote_body(
    depth, scale, pairs, ends, q, g, before, after, mine, theirs, *rest
):
    partial = rest[:pairs]
    kept, sent, to_prev, to_next, dq_t, final, far_k, far_v = rest[pairs : pairs + 8]
    far_kt, near_t, q_t, g_t, dk_t, dv_t = rest[pairs + 8 :]
    rows, width = q.shape
    blocks = rows // BLOCK
    half = mine.shape[1]
    far = 2 * half
    pair = pl.program_id(0)
    far_k[:half] = mine[0]
    far_k[half:] = theirs[0]
    far_v[:half] = mine[1]
    far_v[half:] = theirs[1]
    far_kt[...] = (far_k[...].astype(F32) * scale).astype(BF16).T
    near_t[0] = (before[0].astype(F32) * scale).astype(BF16).T
    near_t[1] = (after[0].astype(F32) * scale).astype(BF16).T
    q_t[...] = (q[...].astype(F32) * scale).astype(BF16).T
    g_t[...] = g[...].T
    low = jnp.where(ends[0] == 1, NEG, 0.0)
    high = jnp.where(ends[1] == 1, NEG, 0.0)
    for h, mask in enumerate(head_masks(width, depth)):
        hr = slice(h * depth, (h + 1) * depth)
        for b in range(blocks):
            r = slice(b * BLOCK, (b + 1) * BLOCK)
            qs = keep_head(q[r], mask, scale)
            gs = keep_head(g[r], mask)
            scores = [dot(far_k[...], qs, NT)]
            values = [dot(far_v[...], gs, NT)]
            if b == 0:
                scores.append(dot(before[0], qs, NT) + low)
                values.append(dot(before[1], gs, NT))
            if b == blocks - 1:
                scores.append(dot(after[0], qs, NT) + high)
                values.append(dot(after[1], gs, NT))
            old = [partial[0][n, h : h + 1, r] for n in range(3)]
            for n in range(1, pairs):
                old = [
                    jnp.where(pair == n, partial[n][m, h : h + 1, r], old[m]) for m in range(3)
                ]
            top = old[0]
            for s in scores:
                top = jnp.maximum(top, jnp.max(s, axis=0, keepdims=True))
            fade = jnp.exp(old[0] - top)
            total = old[1] * fade
            inner = old[2] * fade
            exps = []
            for s, d in zip(scores, values):
                e = jnp.exp(s - top)
                exps.append(e)
                total = total + jnp.sum(e, axis=0, keepdims=True)
                inner = inner + jnp.sum(e * d, axis=0, keepdims=True)
            share = 1.0 / total
            delta = inner * share
            final[0, h : h + 1, r] = top + jnp.log(total)
            final[1, h : h + 1, r] = delta
            probs = [e * share for e in exps]
            grads = [(p * (d - delta)).astype(BF16) for p, d in zip(probs, values)]
            weights = [p.astype(BF16) for p in probs]
            qt, gt = q_t[hr, r], g_t[hr, r]
            dv = dot(gt, weights[0], NT)
            dk = dot(qt, grads[0], NT)
            if b == 0:
                dv_t[hr, :far] = dv
                dk_t[hr, :far] = dk
            else:
                dv_t[hr, :far] += dv
                dk_t[hr, :far] += dk
            dq = dot(far_kt[hr], grads[0], NN)
            at = 1
            if b == 0:
                dv_t[hr, far : far + BLOCK] = dot(gt, weights[at], NT)
                dk_t[hr, far : far + BLOCK] = dot(qt, grads[at], NT)
                dq = dq + dot(near_t[0, hr], grads[at], NN)
                at += 1
            if b == blocks - 1:
                dv_t[hr, far + BLOCK :] = dot(gt, weights[at], NT)
                dk_t[hr, far + BLOCK :] = dot(qt, grads[at], NT)
                dq = dq + dot(near_t[1, hr], grads[at], NN)
            dq_t[hr, r] = dq
    for n, grad in enumerate((dk_t, dv_t)):
        whole = grad[...].T
        kept[n] = whole[:half]
        sent[n] = whole[half:far].astype(BF16)
        to_prev[n] = whole[far : far + BLOCK].astype(BF16)
        to_next[n] = whole[far + BLOCK :].astype(BF16)


def remote(q, g, before, after, mine, theirs, partial, ends, width, depth, scale):
    rows, cols = q.shape
    pairs = cols // width
    hp = width // depth
    half = mine.shape[1]
    far = 2 * half
    wide = lambda n: pl.BlockSpec((n, width), lambda i, *_: (0, i))
    both = lambda n: pl.BlockSpec((2, n, width), lambda i, *_: (0, 0, i))
    fixed = pl.BlockSpec((3, hp, rows), lambda i, *_: (0, 0, 0))
    grid_spec = pltpu.PrefetchScalarGridSpec(
        num_scalar_prefetch=1,
        grid=(pairs,),
        in_specs=[wide(rows)] * 2 + [both(BLOCK)] * 2 + [both(half)] * 2 + [fixed] * pairs,
        out_specs=[
            both(half),
            both(half),
            both(BLOCK),
            both(BLOCK),
            pl.BlockSpec((width, rows), lambda i, *_: (i, 0)),
            pl.BlockSpec((None, 2, hp, rows), lambda i, *_: (i, 0, 0, 0)),
        ],
        scratch_shapes=[
            pltpu.VMEM((far, width), BF16),
            pltpu.VMEM((far, width), BF16),
            pltpu.VMEM((width, far), BF16),
            pltpu.VMEM((2, width, BLOCK), BF16),
            pltpu.VMEM((width, rows), BF16),
            pltpu.VMEM((width, rows), BF16),
            pltpu.VMEM((width, far + 2 * BLOCK), F32),
            pltpu.VMEM((width, far + 2 * BLOCK), F32),
        ],
    )
    return call(
        functools.partial(remote_body, depth, scale, pairs),
        "remote",
        flops=10 * (far * rows + 2 * BLOCK * BLOCK) * cols,
        moved=rows * cols * 8,
        grid_spec=grid_spec,
        out_shape=[
            struct((2, half, cols), F32),
            struct((2, half, cols), BF16),
            struct((2, BLOCK, cols), BF16),
            struct((2, BLOCK, cols), BF16),
            struct((cols, rows), F32),
            struct((pairs, 2, hp, rows), F32),
        ],
    )(ends, q, g, before, after, mine, theirs, *partial)


def local_body(depth, scale, chained, q, k, v, g, part, final, *rest):
    dq, dk, dv, k_t, q_t, g_t, dq_t, dk_t, dv_t = rest[3 if chained else 0 :]
    rows, width = q.shape
    blocks = rows // BLOCK
    k_t[...] = (k[...].astype(F32) * scale).astype(BF16).T
    q_t[...] = (q[...].astype(F32) * scale).astype(BF16).T
    g_t[...] = g[...].T
    for h, mask in enumerate(head_masks(width, depth)):
        hr = slice(h * depth, (h + 1) * depth)
        for b in range(blocks):
            r = slice(b * BLOCK, (b + 1) * BLOCK)
            qs = keep_head(q[r], mask, scale)
            gs = keep_head(g[r], mask)
            qt, gt = q_t[hr, r], g_t[hr, r]
            lse = final[0, h : h + 1, r]
            delta = final[1, h : h + 1, r]
            total = part[hr, r]
            for j in near(b, blocks):
                c = slice(j * BLOCK, (j + 1) * BLOCK)
                p = jnp.exp(dot(k[c], qs, NT) - lse)
                ds = (p * (dot(v[c], gs, NT) - delta)).astype(BF16)
                v_part = dot(gt, p.astype(BF16), NT)
                k_part = dot(qt, ds, NT)
                if b == near(j, blocks)[0]:
                    dv_t[hr, c] = v_part
                    dk_t[hr, c] = k_part
                else:
                    dv_t[hr, c] += v_part
                    dk_t[hr, c] += k_part
                total = total + dot(k_t[hr, c], ds, NN)
            dq_t[hr, r] = total
    dq[...] = dq_t[...].T.astype(BF16)
    dk[...] = dk_t[...].T
    dv[...] = dv_t[...].T


def local(q, k, v, g, part, final, before, width, depth, scale, pair):
    rows, cols = q.shape
    hp = width // depth
    column = pl.BlockSpec((rows, width), lambda i: (0, pair))
    chained = before is not None
    extra = list(before) if chained else []
    return call(
        functools.partial(local_body, depth, scale, chained),
        f"local{pair}",
        flops=10 * 3 * BLOCK * rows * width,
        moved=rows * width * 24,
        grid=(1,),
        in_specs=[column] * 4
        + [
            pl.BlockSpec((width, rows), lambda i: (pair, 0)),
            pl.BlockSpec((None, 2, hp, rows), lambda i: (pair, 0, 0, 0)),
        ]
        + [pl.BlockSpec(memory_space=pl.ANY)] * len(extra),
        out_specs=[column] * 3,
        out_shape=[struct((rows, cols), BF16), struct((rows, cols), F32), struct((rows, cols), F32)],
        scratch_shapes=[pltpu.VMEM((width, rows), BF16)] * 3 + [pltpu.VMEM((width, rows), F32)] * 3,
        input_output_aliases={6 + n: n for n in range(len(extra))},
    )(q, k, v, g, part, final, *extra)


def fold_body(rows1, rows2, only_whole, split_both, kept, got, next_kept, next_sent):
    for n in range(2):
        first = kept[n, :rows1]
        second = kept[n, rows1:]
        if only_whole:
            second = second + got[n].astype(F32)
        else:
            first = first + got[n, :rows1].astype(F32)
            second = second + got[n, rows1:].astype(F32)
        keep2 = rows2 // 2
        if split_both:
            keep1 = rows1 // 2
            next_kept[n] = jnp.concatenate([first[:keep1], second[:keep2]], axis=0)
            next_sent[n] = jnp.concatenate([first[keep1:], second[keep2:]], axis=0).astype(BF16)
        else:
            next_kept[n] = jnp.concatenate([first, second[:keep2]], axis=0)
            next_sent[n] = second[keep2:].astype(BF16)


def fold(kept, got, rows1, rows2, only_whole, split_both):
    cols = kept.shape[-1]
    if split_both:
        stay, go = (rows1 + rows2) // 2, (rows1 + rows2) // 2
    else:
        stay, go = rows1 + rows2 // 2, rows2 // 2
    return call(
        functools.partial(fold_body, rows1, rows2, only_whole, split_both),
        "fold",
        moved=kept.size * 8,
        out_shape=[struct((2, stay, cols), F32), struct((2, go, cols), BF16)],
    )(kept, got)


def finish_body(dk, dv, from_prev, from_next, kept, got, wide_group, wide_whole, out_k, out_v):
    block = pl.program_id(0)
    blocks = pl.num_programs(0)
    per = BLOCK // SEG1
    count1 = kept.shape[1] * SEG2 // (SEG1 + SEG2)
    low = jnp.where(block == 0, 1.0, 0.0)
    high = jnp.where(block == blocks - 1, 1.0, 0.0)
    for n, (src, dst) in enumerate(((dk, out_k), (dv, out_v))):
        sums = kept[n] + got[n].astype(F32)
        index = lax.broadcasted_iota(jnp.int32, (kept.shape[1], 1), 0)
        pieces = []
        whole = jnp.sum(jnp.where(index == count1 + block, sums, 0.0), axis=0, keepdims=True)
        for s in range(per):
            at = jnp.where(index == block * per + s, sums, 0.0)
            group = jnp.sum(at, axis=0, keepdims=True)
            c = slice(s * SEG1, (s + 1) * SEG1)
            piece = src[c] + group * wide_group[...] + whole * wide_whole[c]
            piece = piece + low * from_prev[n, c].astype(F32) + high * from_next[n, c].astype(F32)
            dst[c] = piece.astype(BF16)


def finish(dk, dv, from_prev, from_next, kept, got, wide_group, wide_whole):
    rows, cols = dk.shape
    tile = pl.BlockSpec((BLOCK, cols), lambda i: (i, 0))
    full = lambda x: pl.BlockSpec(x.shape, lambda i: (0,) * x.ndim)
    return call(
        finish_body,
        "finish",
        moved=rows * cols * 12,
        grid=(rows // BLOCK,),
        in_specs=[tile, tile]
        + [full(x) for x in (from_prev, from_next, kept, got, wide_group, wide_whole)],
        out_specs=[tile, tile],
        out_shape=[struct((rows, cols), BF16)] * 2,
    )(dk, dv, from_prev, from_next, kept, got, wide_group, wide_whole)


def shards(query, key, value, out_grad, pool_group, pool_global):
    rows, cols = query.shape
    heads = pool_group.shape[0]
    depth = cols // heads
    scale = 1.0 / math.sqrt(depth)
    width = 128 if cols % 128 == 0 and 128 % depth == 0 else cols
    pairs = cols // width
    devices = lax.axis_size("seq")
    position = lax.axis_index("seq")
    count1, count2 = rows // SEG1, rows // SEG2
    group_bits = list(range(1, GROUP.bit_length() - 1))
    other_bits = list(range(GROUP.bit_length() - 1, devices.bit_length() - 1))

    def swap(array, bit):
        return lax.ppermute(array, "seq", [(i, i ^ (1 << bit)) for i in range(devices)])

    def shift(array, by):
        pairs_ = [(i, i + by) for i in range(devices) if 0 <= i + by < devices]
        return lax.ppermute(array, "seq", pairs_)

    comb, first, last, wide_group, wide_whole = pool(key, value, pool_group, pool_global)
    ends = jnp.stack([position == 0, position == devices - 1]).astype(jnp.int32)

    before = after = None
    for bit in group_bits:
        got = swap(comb, bit)
        if before is None:
            before = shift(last, 1)
            after = shift(first, -1)
        comb = jnp.concatenate([comb, got], axis=0)
    whole = comb[:, :, count1 : count1 + count2]
    for bit in other_bits:
        whole = jnp.concatenate([whole, swap(whole, bit)], axis=0)
    slots1, slots2 = comb.shape[0], whole.shape[0]
    mine = pack(comb, whole, count1, count2)
    theirs = swap(mine, 0)

    partial = [stats(query, key, value, out_grad, width, depth, scale, p) for p in range(pairs)]
    kept, sent, to_prev, to_next, dq_t, final = remote(
        query, out_grad, before, after, mine, theirs, partial, ends, width, depth, scale
    )
    got = swap(sent, 0)
    from_next = shift(to_prev, -1)
    from_prev = shift(to_next, 1)

    rows1, rows2 = slots1 * count1, slots2 * count2
    only_whole = False
    for bit in reversed(other_bits):
        kept, sent = fold(kept, got, rows1, rows2, only_whole, False)
        rows2 //= 2
        got = swap(sent, bit)
        only_whole = True
    for bit in reversed(group_bits):
        kept, sent = fold(kept, got, rows1, rows2, only_whole, True)
        rows1 //= 2
        rows2 //= 2
        got = swap(sent, bit)
        only_whole = False

    grads = None
    for p in range(pairs):
        grads = local(
            query, key, value, out_grad, dq_t, final, grads, width, depth, scale, p
        )
    query_grad, dk, dv = grads
    key_grad, value_grad = finish(
        dk, dv, from_prev, from_next, kept, got, wide_group, wide_whole
    )
    return (query_grad, key_grad, value_grad)


def solution(mesh):
    rows = P("seq", "head")
    in_specs = (rows, rows, rows, rows, P("head", None), P("head", None))
    return jax.shard_map(
        shards, mesh=mesh, in_specs=in_specs, out_specs=(rows, rows, rows), check_vma=False
    )
```

profile of v0, /device:TPU:1, one launch (start us, length us, event | category | flops | bytes accessed | tf_op | source)
XLA Modules:
  0.0 105.6 jit_solution(14990610297423313304)
XLA Ops:
  0.6 1.2 %copy-done = bf16[1024,512]{1,0:T(8,128)(2,1)S(1)} copy-done((bf16[1024,512]{1,0:T(8,128)(2,1)S(1)}, bf16[1024,512]{1,0:T(8,128)(2,1)}, u32[]{:S(2)}) %copy-start) | copy-done | bytes 1048600
  1.9 1.2 %copy-done.2 = bf16[1024,512]{1,0:T(8,128)(2,1)S(1)} copy-done((bf16[1024,512]{1,0:T(8,128)(2,1)S(1)}, bf16[1024,512]{1,0:T(8,128)(2,1)}, u32[]{:S(2)}) %copy-start.2) | copy-done | bytes 1048600
  3.1 0.7 copy-done.12
  3.8 0.7 copy-done.13
  4.5 2.2 %pool.1 = (bf16[1,2,24,512]{3,2,1,0:T(8,128)(2,1)S(1)}, bf16[2,256,512]{2,1,0:T(8,128)(2,1)}, bf16[2,256,512]{2,1,0:T(8,128)(2,1)}, f32[64,512]{1,0:T(8,128)S(1)}, f32[256,512]{1,0:T(8,128)S(1)}) custom-call(bf16[1024,512]{1,0:T(8,128)(2,1)S(1)} %copy-done, bf16[1024,512]{1,0:T(8,128)(2,1)S(1)} %copy-done.2, f32[8,64]{1,0:T(8,128)S(1)} %copy-done.13, ...), custom_call_target="tpu_custom_call" | custom-call | bytes 4194304 | tf_op jit(solution)/shard_map/pool/pallas_call | solution.py:89
  6.7 2.1 %collective-permute-start.2 = (bf16[1,2,24,512]{3,2,1,0:T(8,128)(2,1)S(1)}, bf16[1,2,24,512]{3,2,1,0:T(8,128)(2,1)S(1)}, u32[]{:S(2)}, u32[]{:S(2)}) collective-permute-start(bf16[1,2,24,512]{3,2,1,0:T(8,128)(2,1)S(1)} %get-tuple-element.36), channel_id=1, source_target_pairs={{0,4},{2,6},{4,0},{6,2},{8,12},{10,14},{12,8},{14,10},{16,20},{18,... | collective-permute-start | bytes 147464 | tf_op jit(solution)/shard_map/ppermute | solution.py:457
  8.8 2.5 %collective-permute-start = (bf16[2,256,512]{2,1,0:T(8,128)(2,1)}, bf16[2,256,512]{2,1,0:T(8,128)(2,1)}, u32[]{:S(2)}, u32[]{:S(2)}) collective-permute-start(bf16[2,256,512]{2,1,0:T(8,128)(2,1)} %get-tuple-element.34), channel_id=1, source_target_pairs={{0,2},{2,4},{4,6},{6,8},{8,10},{10,12},{12,14},{14,16},{16,18},{18... | collective-permute-start | bytes 1572872 | tf_op jit(solution)/shard_map/ppermute | solution.py:461
  11.2 2.7 %collective-permute-start.1 = (bf16[2,256,512]{2,1,0:T(8,128)(2,1)}, bf16[2,256,512]{2,1,0:T(8,128)(2,1)}, u32[]{:S(2)}, u32[]{:S(2)}) collective-permute-start(bf16[2,256,512]{2,1,0:T(8,128)(2,1)} %get-tuple-element.35), channel_id=1, source_target_pairs={{2,0},{4,2},{6,4},{8,6},{10,8},{12,10},{14,12},{16,14},{18,16},{20... | collective-permute-start | bytes 1572872 | tf_op jit(solution)/shard_map/ppermute | solution.py:461
  13.9 1.1 %collective-permute-start.3 = (bf16[2,2,24,512]{3,2,1,0:T(8,128)(2,1)S(1)}, bf16[2,2,24,512]{3,2,1,0:T(8,128)(2,1)S(1)}, u32[]{:S(2)}, u32[]{:S(2)}) collective-permute-start(bf16[2,2,24,512]{3,2,1,0:T(8,128)(2,1)S(1)} %pad_maximum_fusion), channel_id=1, source_target_pairs={{0,8},{2,10},{4,12},{6,14},{8,0},{10,2},{12,4},{14,6},{16,24},{18,... | collective-permute-start | bytes 294920 | tf_op jit(solution)/shard_map/ppermute | solution.py:457
  15.1 2.4 %collective-permute-done.3 = bf16[2,2,24,512]{3,2,1,0:T(8,128)(2,1)S(1)} collective-permute-done((bf16[2,2,24,512]{3,2,1,0:T(8,128)(2,1)S(1)}, bf16[2,2,24,512]{3,2,1,0:T(8,128)(2,1)S(1)}, u32[]{:S(2)}, u32[]{:S(2)}) %collective-permute-start.3) | collective-permute-done | bytes 98336 | tf_op jit(solution)/shard_map/ppermute | solution.py:457
  17.5 2.5 %collective-permute-start.4 = (bf16[4,2,4,512]{3,2,1,0:T(4,128)(2,1)S(1)}, bf16[4,2,4,512]{3,2,1,0:T(4,128)(2,1)S(1)}, u32[]{:S(2)}, u32[]{:S(2)}) collective-permute-start(bf16[4,2,4,512]{3,2,1,0:T(4,128)(2,1)S(1)} %slice.4), channel_id=1, source_target_pairs={{0,16},{2,18},{4,20},{6,22},{8,24},{10,26},{12,28},{14,30},{16,0},... | collective-permute-start | bytes 98312 | tf_op jit(solution)/shard_map/ppermute | solution.py:457
  20.0 1.8 %stats3.1.rest_3_ = f32[3,2,1024]{2,1,0:T(2,128)S(1)} custom-call(bf16[1024,512]{1,0:T(8,128)(2,1)S(1)} %copy-done.4, bf16[1024,512]{1,0:T(8,128)(2,1)S(1)} %copy-done, bf16[1024,512]{1,0:T(8,128)(2,1)S(1)} %copy-done.2, bf16[1024,512]{1,0:T(8,128)(2,1)S(1)} %copy-done.5), custom_call_target="tpu_custom_call" | custom-call | flops 402653184 | bytes 1048576 | tf_op jit(solution)/shard_map/stats3/pallas_call | solution.py:162
  21.9 9.7 %collective-permute-start.5 = (bf16[2,96,512]{2,1,0:T(8,128)(2,1)S(1)}, bf16[2,96,512]{2,1,0:T(8,128)(2,1)}, u32[]{:S(2)}, u32[]{:S(2)}) collective-permute-start(bf16[2,96,512]{2,1,0:T(8,128)(2,1)S(1)} %pack.1.mine), channel_id=1, source_target_pairs={{0,2},{2,0},{4,6},{6,4},{8,10},{10,8},{12,14},{14,12},{16,18},{18,... | collective-permute-start | bytes 589832 | tf_op jit(solution)/shard_map/ppermute | solution.py:457
  31.6 1.8 %stats2.1.rest_2_ = f32[3,2,1024]{2,1,0:T(2,128)S(1)} custom-call(bf16[1024,512]{1,0:T(8,128)(2,1)S(1)} %copy-done.4, bf16[1024,512]{1,0:T(8,128)(2,1)S(1)} %copy-done.1, bf16[1024,512]{1,0:T(8,128)(2,1)S(1)} %copy-done.2, bf16[1024,512]{1,0:T(8,128)(2,1)S(1)} %copy-done.5), custom_call_target="tpu_custom_call" | custom-call | flops 402653184 | bytes 1048576 | tf_op jit(solution)/shard_map/stats2/pallas_call | solution.py:162
  33.4 1.2 %copy-done.6 = bf16[1024,512]{1,0:T(8,128)(2,1)S(1)} copy-done((bf16[1024,512]{1,0:T(8,128)(2,1)S(1)}, bf16[1024,512]{1,0:T(8,128)(2,1)}, u32[]{:S(2)}) %copy-start.6) | copy-done | bytes 1048600
  34.6 1.7 %stats1.1.rest_1_ = f32[3,2,1024]{2,1,0:T(2,128)S(1)} custom-call(bf16[1024,512]{1,0:T(8,128)(2,1)S(1)} %copy-done.4, bf16[1024,512]{1,0:T(8,128)(2,1)S(1)} %copy-done.1, bf16[1024,512]{1,0:T(8,128)(2,1)S(1)} %copy-done.3, bf16[1024,512]{1,0:T(8,128)(2,1)S(1)} %copy-done.6), custom_call_target="tpu_custom_call" | custom-call | flops 402653184 | bytes 1048576 | tf_op jit(solution)/shard_map/stats1/pallas_call | solution.py:162
  36.3 1.7 %stats0.1.rest_0_ = f32[3,2,1024]{2,1,0:T(2,128)S(1)} custom-call(bf16[1024,512]{1,0:T(8,128)(2,1)S(1)} %copy-done.4, bf16[1024,512]{1,0:T(8,128)(2,1)S(1)} %copy-done.1, bf16[1024,512]{1,0:T(8,128)(2,1)S(1)} %copy-done.3, bf16[1024,512]{1,0:T(8,128)(2,1)S(1)} %copy-done.6), custom_call_target="tpu_custom_call" | custom-call | flops 402653184 | bytes 1048576 | tf_op jit(solution)/shard_map/stats0/pallas_call | solution.py:162
  38.1 0.1 add_convert_fusion.ends
  38.2 19.5 %remote.1 = (f32[2,96,512]{2,1,0:T(8,128)S(1)}, bf16[2,96,512]{2,1,0:T(8,128)(2,1)S(1)}, bf16[2,256,512]{2,1,0:T(8,128)(2,1)S(1)}, bf16[2,256,512]{2,1,0:T(8,128...) custom-call(s32[2]{0:T(128)S(1)} %add_convert_fusion.ends, bf16[1024,512]{1,0:T(8,128)(2,1)S(1)} %copy-done.4, ...), custom_call_target="tpu_custom_call" | custom-call | flops 1677721600 | bytes 4194304 | tf_op jit(solution)/shard_map/remote/pallas_call | solution.py:295
  57.7 1.9 %collective-permute-start.6 = (bf16[2,256,512]{2,1,0:T(8,128)(2,1)S(1)}, bf16[2,256,512]{2,1,0:T(8,128)(2,1)S(1)}, u32[]{:S(2)}, u32[]{:S(2)}) collective-permute-start(bf16[2,256,512]{2,1,0:T(8,128)(2,1)S(1)} %get-tuple-element.51), channel_id=1, source_target_pairs={{0,2},{2,4},{4,6},{6,8},{8,10},{10,12},{12,14},{14,16},{16,18},{18... | collective-permute-start | bytes 1572872 | tf_op jit(solution)/shard_map/ppermute | solution.py:461
  59.6 2.6 %collective-permute-start.7 = (bf16[2,256,512]{2,1,0:T(8,128)(2,1)S(1)}, bf16[2,256,512]{2,1,0:T(8,128)(2,1)S(1)}, u32[]{:S(2)}, u32[]{:S(2)}) collective-permute-start(bf16[2,256,512]{2,1,0:T(8,128)(2,1)S(1)} %get-tuple-element.52), channel_id=1, source_target_pairs={{2,0},{4,2},{6,4},{8,6},{10,8},{12,10},{14,12},{16,14},{18,16},{20... | collective-permute-start | bytes 1572872 | tf_op jit(solution)/shard_map/ppermute | solution.py:461
  62.3 0.1 collective-permute-start.8
  62.3 8.1 %local0.1 = (bf16[1024,512]{1,0:T(8,128)(2,1)}, f32[1024,512]{1,0:T(8,128)}, f32[1024,512]{1,0:T(8,128)}) custom-call(bf16[1024,512]{1,0:T(8,128)(2,1)S(1)} %copy-done.4, bf16[1024,512]{1,0:T(8,128)(2,1)S(1)} %copy-done.1, bf16[1024,512]{1,0:T(8,128)(2,1)S(1)} %copy-done.3, bf16[1024,512]{1,0:T(8,128)(2,1)S(1)} %copy-done.7, ...), custom_call_target="tpu_custom_call" | custom-call | flops 1006632960 | bytes 3145728 | tf_op jit(solution)/shard_map/local0/pallas_call | solution.py:354
  70.5 4.5 %collective-permute-start.9 = (bf16[2,16,512]{2,1,0:T(8,128)(2,1)S(1)}, bf16[2,16,512]{2,1,0:T(8,128)(2,1)S(1)}, u32[]{:S(2)}, u32[]{:S(2)}) collective-permute-start(bf16[2,16,512]{2,1,0:T(8,128)(2,1)S(1)} %get-tuple-element.56), channel_id=1, source_target_pairs={{0,16},{2,18},{4,20},{6,22},{8,24},{10,26},{12,28},{14,30},{16,0},... | collective-permute-start | bytes 98312 | tf_op jit(solution)/shard_map/ppermute | solution.py:457
  74.9 8.1 %local1.1 = (bf16[1024,512]{1,0:T(8,128)(2,1)}, f32[1024,512]{1,0:T(8,128)}, f32[1024,512]{1,0:T(8,128)}) custom-call(bf16[1024,512]{1,0:T(8,128)(2,1)S(1)} %copy-done.4, bf16[1024,512]{1,0:T(8,128)(2,1)S(1)} %copy-done.1, bf16[1024,512]{1,0:T(8,128)(2,1)S(1)} %copy-done.3, ...), custom_call_target="tpu_custom_call", output_to_operand_aliasing={{0}: (6, {}), {1}: (7, {}), {2}: (8, {})} | custom-call | flops 1006632960 | bytes 3145728 | tf_op jit(solution)/shard_map/local1/pallas_call | solution.py:354
  83.1 0.1 collective-permute-start.10
  83.2 8.3 %local2.1 = (bf16[1024,512]{1,0:T(8,128)(2,1)}, f32[1024,512]{1,0:T(8,128)}, f32[1024,512]{1,0:T(8,128)}) custom-call(bf16[1024,512]{1,0:T(8,128)(2,1)S(1)} %copy-done.4, bf16[1024,512]{1,0:T(8,128)(2,1)S(1)} %copy-done.1, bf16[1024,512]{1,0:T(8,128)(2,1)S(1)} %copy-done.3, ...), custom_call_target="tpu_custom_call", output_to_operand_aliasing={{0}: (6, {}), {1}: (7, {}), {2}: (8, {})} | custom-call | flops 1006632960 | bytes 3145728 | tf_op jit(solution)/shard_map/local2/pallas_call | solution.py:354
  91.5 0.1 collective-permute-start.11
  91.6 8.1 %local3.1 = (bf16[1024,512]{1,0:T(8,128)(2,1)}, f32[1024,512]{1,0:T(8,128)}, f32[1024,512]{1,0:T(8,128)}) custom-call(bf16[1024,512]{1,0:T(8,128)(2,1)S(1)} %copy-done.4, bf16[1024,512]{1,0:T(8,128)(2,1)S(1)} %copy-done.1, bf16[1024,512]{1,0:T(8,128)(2,1)S(1)} %copy-done.3, ...), custom_call_target="tpu_custom_call", output_to_operand_aliasing={{0}: (6, {}), {1}: (7, {}), {2}: (8, {})} | custom-call | flops 1006632960 | bytes 3145728 | tf_op jit(solution)/shard_map/local3/pallas_call | solution.py:354
  99.7 1.6 %copy-done.8 = f32[1024,512]{1,0:T(8,128)S(1)} copy-done((f32[1024,512]{1,0:T(8,128)S(1)}, f32[1024,512]{1,0:T(8,128)}, u32[]{:S(2)}) %copy-start.8) | copy-done | bytes 2097176
  101.3 1.6 %copy-done.9 = f32[1024,512]{1,0:T(8,128)S(1)} copy-done((f32[1024,512]{1,0:T(8,128)S(1)}, f32[1024,512]{1,0:T(8,128)}, u32[]{:S(2)}) %copy-start.9) | copy-done | bytes 2097176
  102.9 2.7 %finish.1 = (bf16[1024,512]{1,0:T(8,128)(2,1)}, bf16[1024,512]{1,0:T(8,128)(2,1)}) custom-call(f32[1024,512]{1,0:T(8,128)S(1)} %copy-done.8, f32[1024,512]{1,0:T(8,128)S(1)} %copy-done.9, bf16[2,256,512]{2,1,0:T(8,128)(2,1)S(1)} %collective-permute-done.6.from_prev, bf16[2,256,512]{2,1,0:T(8,128)(2,1)S(1)} %collective-permute-done.7.from_next, ...), custom_call_target="tpu_custom_call" | custom-call | bytes 6291456 | tf_op jit(solution)/shard_map/finish/pallas_call | solution.py:431
  (42 shorter events, 0.3 us)
Async XLA Ops:
  0.6 1.2 %copy-start = (bf16[1024,512]{1,0:T(8,128)(2,1)S(1)}, bf16[1024,512]{1,0:T(8,128)(2,1)}, u32[]{:S(2)}) copy-start(bf16[1024,512]{1,0:T(8,128)(2,1)} %k.17) | copy-start | bytes 3145732
  1.9 1.2 %copy-start.2 = (bf16[1024,512]{1,0:T(8,128)(2,1)S(1)}, bf16[1024,512]{1,0:T(8,128)(2,1)}, u32[]{:S(2)}) copy-start(bf16[1024,512]{1,0:T(8,128)(2,1)} %v.17) | copy-start | bytes 3145732
  3.1 0.7 copy-start.12
  3.8 0.7 copy-start.13
  4.5 15.6 %copy-start.4 = (bf16[1024,512]{1,0:T(8,128)(2,1)S(1)}, bf16[1024,512]{1,0:T(8,128)(2,1)}, u32[]{:S(2)}) copy-start(bf16[1024,512]{1,0:T(8,128)(2,1)} %q.17) | copy-start | bytes 3145732
  4.5 15.6 %copy-start.5 = (bf16[1024,512]{1,0:T(8,128)(2,1)S(1)}, bf16[1024,512]{1,0:T(8,128)(2,1)}, u32[]{:S(2)}) copy-start(bf16[1024,512]{1,0:T(8,128)(2,1)} %g.17) | copy-start | bytes 3145732
  6.7 15.1 %copy-start.10 = (f32[256,512]{1,0:T(8,128)}, f32[256,512]{1,0:T(8,128)S(1)}, u32[]{:S(2)}) copy-start(f32[256,512]{1,0:T(8,128)S(1)} %get-tuple-element.62.wide_whole) | copy-start | bytes 1572868
  6.7 7.2 %collective-permute-start.2 = (bf16[1,2,24,512]{3,2,1,0:T(8,128)(2,1)S(1)}, bf16[1,2,24,512]{3,2,1,0:T(8,128)(2,1)S(1)}, u32[]{:S(2)}, u32[]{:S(2)}) collective-permute-start(bf16[1,2,24,512]{3,2,1,0:T(8,128)(2,1)S(1)} %get-tuple-element.36), channel_id=1, source_target_pairs={{0,4},{2,6},{4,0},{6,2},{8,12},{10,14},{12,8},{14,10},{16,20},{18,... | collective-permute-start | bytes 147464 | tf_op jit(solution)/shard_map/ppermute | solution.py:457
  8.8 29.4 %collective-permute-start = (bf16[2,256,512]{2,1,0:T(8,128)(2,1)}, bf16[2,256,512]{2,1,0:T(8,128)(2,1)}, u32[]{:S(2)}, u32[]{:S(2)}) collective-permute-start(bf16[2,256,512]{2,1,0:T(8,128)(2,1)} %get-tuple-element.34), channel_id=1, source_target_pairs={{0,2},{2,4},{4,6},{6,8},{8,10},{10,12},{12,14},{14,16},{16,18},{18... | collective-permute-start | bytes 1572872 | tf_op jit(solution)/shard_map/ppermute | solution.py:461
  11.2 26.9 %collective-permute-start.1 = (bf16[2,256,512]{2,1,0:T(8,128)(2,1)}, bf16[2,256,512]{2,1,0:T(8,128)(2,1)}, u32[]{:S(2)}, u32[]{:S(2)}) collective-permute-start(bf16[2,256,512]{2,1,0:T(8,128)(2,1)} %get-tuple-element.35), channel_id=1, source_target_pairs={{2,0},{4,2},{6,4},{8,6},{10,8},{12,10},{14,12},{16,14},{18,16},{20... | collective-permute-start | bytes 1572872 | tf_op jit(solution)/shard_map/ppermute | solution.py:461
  13.9 3.5 %collective-permute-start.3 = (bf16[2,2,24,512]{3,2,1,0:T(8,128)(2,1)S(1)}, bf16[2,2,24,512]{3,2,1,0:T(8,128)(2,1)S(1)}, u32[]{:S(2)}, u32[]{:S(2)}) collective-permute-start(bf16[2,2,24,512]{3,2,1,0:T(8,128)(2,1)S(1)} %pad_maximum_fusion), channel_id=1, source_target_pairs={{0,8},{2,10},{4,12},{6,14},{8,0},{10,2},{12,4},{14,6},{16,24},{18,... | collective-permute-start | bytes 294920 | tf_op jit(solution)/shard_map/ppermute | solution.py:457
  17.5 14.1 %copy-start.1 = (bf16[1024,512]{1,0:T(8,128)(2,1)S(1)}, bf16[1024,512]{1,0:T(8,128)(2,1)}, u32[]{:S(2)}) copy-start(bf16[1024,512]{1,0:T(8,128)(2,1)} %k.17) | copy-start | bytes 3145732
  17.5 4.3 %collective-permute-start.4 = (bf16[4,2,4,512]{3,2,1,0:T(4,128)(2,1)S(1)}, bf16[4,2,4,512]{3,2,1,0:T(4,128)(2,1)S(1)}, u32[]{:S(2)}, u32[]{:S(2)}) collective-permute-start(bf16[4,2,4,512]{3,2,1,0:T(4,128)(2,1)S(1)} %slice.4), channel_id=1, source_target_pairs={{0,16},{2,18},{4,20},{6,22},{8,24},{10,26},{12,28},{14,30},{16,0},... | collective-permute-start | bytes 98312 | tf_op jit(solution)/shard_map/ppermute | solution.py:457
  21.9 11.4 %copy-start.3 = (bf16[1024,512]{1,0:T(8,128)(2,1)S(1)}, bf16[1024,512]{1,0:T(8,128)(2,1)}, u32[]{:S(2)}) copy-start(bf16[1024,512]{1,0:T(8,128)(2,1)} %v.17) | copy-start | bytes 3145732
  21.9 16.2 %collective-permute-start.5 = (bf16[2,96,512]{2,1,0:T(8,128)(2,1)S(1)}, bf16[2,96,512]{2,1,0:T(8,128)(2,1)}, u32[]{:S(2)}, u32[]{:S(2)}) collective-permute-start(bf16[2,96,512]{2,1,0:T(8,128)(2,1)S(1)} %pack.1.mine), channel_id=1, source_target_pairs={{0,2},{2,0},{4,6},{6,4},{8,10},{10,8},{12,14},{14,12},{16,18},{18,... | collective-permute-start | bytes 589832 | tf_op jit(solution)/shard_map/ppermute | solution.py:457
  33.4 1.2 %copy-start.6 = (bf16[1024,512]{1,0:T(8,128)(2,1)S(1)}, bf16[1024,512]{1,0:T(8,128)(2,1)}, u32[]{:S(2)}) copy-start(bf16[1024,512]{1,0:T(8,128)(2,1)} %g.17) | copy-start | bytes 3145732
  36.3 1.8 %copy-start.7 = (bf16[1024,512]{1,0:T(8,128)(2,1)S(1)}, bf16[1024,512]{1,0:T(8,128)(2,1)}, u32[]{:S(2)}) copy-start(bf16[1024,512]{1,0:T(8,128)(2,1)} %g.17) | copy-start | bytes 3145732
  57.7 41.9 %collective-permute-start.6 = (bf16[2,256,512]{2,1,0:T(8,128)(2,1)S(1)}, bf16[2,256,512]{2,1,0:T(8,128)(2,1)S(1)}, u32[]{:S(2)}, u32[]{:S(2)}) collective-permute-start(bf16[2,256,512]{2,1,0:T(8,128)(2,1)S(1)} %get-tuple-element.51), channel_id=1, source_target_pairs={{0,2},{2,4},{4,6},{6,8},{8,10},{10,12},{12,14},{14,16},{16,18},{18... | collective-permute-start | bytes 1572872 | tf_op jit(solution)/shard_map/ppermute | solution.py:461
  59.6 40.0 %collective-permute-start.7 = (bf16[2,256,512]{2,1,0:T(8,128)(2,1)S(1)}, bf16[2,256,512]{2,1,0:T(8,128)(2,1)S(1)}, u32[]{:S(2)}, u32[]{:S(2)}) collective-permute-start(bf16[2,256,512]{2,1,0:T(8,128)(2,1)S(1)} %get-tuple-element.52), channel_id=1, source_target_pairs={{2,0},{4,2},{6,4},{8,6},{10,8},{12,10},{14,12},{16,14},{18,16},{20... | collective-permute-start | bytes 1572872 | tf_op jit(solution)/shard_map/ppermute | solution.py:461
  62.3 8.2 %collective-permute-start.8 = (bf16[2,96,512]{2,1,0:T(8,128)(2,1)S(1)}, bf16[2,96,512]{2,1,0:T(8,128)(2,1)S(1)}, u32[]{:S(2)}, u32[]{:S(2)}) collective-permute-start(bf16[2,96,512]{2,1,0:T(8,128)(2,1)S(1)} %get-tuple-element.54), channel_id=1, source_target_pairs={{0,2},{2,0},{4,6},{6,4},{8,10},{10,8},{12,14},{14,12},{16,18},{18,... | collective-permute-start | bytes 589832 | tf_op jit(solution)/shard_map/ppermute | solution.py:457
  70.5 12.6 %collective-permute-start.9 = (bf16[2,16,512]{2,1,0:T(8,128)(2,1)S(1)}, bf16[2,16,512]{2,1,0:T(8,128)(2,1)S(1)}, u32[]{:S(2)}, u32[]{:S(2)}) collective-permute-start(bf16[2,16,512]{2,1,0:T(8,128)(2,1)S(1)} %get-tuple-element.56), channel_id=1, source_target_pairs={{0,16},{2,18},{4,20},{6,22},{8,24},{10,26},{12,28},{14,30},{16,0},... | collective-permute-start | bytes 98312 | tf_op jit(solution)/shard_map/ppermute | solution.py:457
  83.1 8.4 %collective-permute-start.10 = (bf16[2,40,512]{2,1,0:T(8,128)(2,1)S(1)}, bf16[2,40,512]{2,1,0:T(8,128)(2,1)S(1)}, u32[]{:S(2)}, u32[]{:S(2)}) collective-permute-start(bf16[2,40,512]{2,1,0:T(8,128)(2,1)S(1)} %get-tuple-element.58), channel_id=1, source_target_pairs={{0,8},{2,10},{4,12},{6,14},{8,0},{10,2},{12,4},{14,6},{16,24},{18,... | collective-permute-start | bytes 245768 | tf_op jit(solution)/shard_map/ppermute | solution.py:457
  91.5 8.2 %collective-permute-start.11 = (bf16[2,20,512]{2,1,0:T(8,128)(2,1)S(1)}, bf16[2,20,512]{2,1,0:T(8,128)(2,1)S(1)}, u32[]{:S(2)}, u32[]{:S(2)}) collective-permute-start(bf16[2,20,512]{2,1,0:T(8,128)(2,1)S(1)} %get-tuple-element.60), channel_id=1, source_target_pairs={{0,4},{2,6},{4,0},{6,2},{8,12},{10,14},{12,8},{14,10},{16,20},{18,... | collective-permute-start | bytes 122888 | tf_op jit(solution)/shard_map/ppermute | solution.py:457
  91.5 8.1 %copy-start.11 = (f32[256,512]{1,0:T(8,128)S(1)}, f32[256,512]{1,0:T(8,128)}, u32[]{:S(2)}) copy-start(f32[256,512]{1,0:T(8,128)} %copy-done.10) | copy-start | bytes 1572868
  99.7 1.6 %copy-start.8 = (f32[1024,512]{1,0:T(8,128)S(1)}, f32[1024,512]{1,0:T(8,128)}, u32[]{:S(2)}) copy-start(f32[1024,512]{1,0:T(8,128)} %get-tuple-element.49.dk) | copy-start | bytes 6291460
  101.3 1.6 %copy-start.9 = (f32[1024,512]{1,0:T(8,128)S(1)}, f32[1024,512]{1,0:T(8,128)}, u32[]{:S(2)}) copy-start(f32[1024,512]{1,0:T(8,128)} %get-tuple-element.50.dv) | copy-start | bytes 6291460
where the time goes:
time: 106 us
  Pallas kernels  64.1 us (60%)
  starting transfers between devices  29.7 us (28%)
  local copies, waits for them, and re-layouts  8.29 us (8%)
  waiting for transfers between devices  2.42 us (2%)
    pallas_call x4, Pallas kernels, local(): call(functools.partial(local_body, depth, scale, chained), f'local{pair}'...  32.6 us
    ppermute x8, starting transfers between devices, swap(): lax.ppermute(array, 'seq', [(i, i ^ 1 << bit) for i in range(devices)])  20.1 us
    pallas_call x1, Pallas kernels, remote(): call(functools.partial(remote_body, depth, scale, pairs), 'remote', flops...  19.5 us
    ppermute x4, starting transfers between devices, shift(): return lax.ppermute(array, 'seq', pairs_)  9.64 us
    unnamed x30, local copies, waits for them, and re-layouts  8.27 us
    pallas_call x4, Pallas kernels, stats(): call(functools.partial(stats_body, depth, scale), f'stats{pair}', flops=2...  6.98 us
    pallas_call x1, Pallas kernels, finish(): call(finish_body, 'finish', moved=rows * cols * 12, grid=(rows // BLOCK,)...  2.71 us
    ppermute x8, waiting for transfers between devices, swap(): lax.ppermute(array, 'seq', [(i, i ^ 1 << bit) for i in range(devices)])  2.41 us
  transfers between devices with their start and end apart: 12, of which 1 were waited for; matrix products, arithmetic and copies ran while one was open for 0% of the time, Pallas kernels for 38%

commit v1 on v0

v1 whole, which is shorter than its diff:
```python
import functools
import math

import jax
import jax.numpy as jnp
from jax import lax
from jax.experimental import pallas as pl
from jax.experimental.pallas import tpu as pltpu
from jax.sharding import PartitionSpec as P

BLOCK = 256
SEG1 = 64
SEG2 = 256
GROUP = 8
NEG = -1e30
F32 = jnp.float32
BF16 = jnp.bfloat16
NT = (((1,), (1,)), ((), ()))
NN = (((1,), (0,)), ((), ()))
VMEM_LIMIT = 32 * 2**20
VMEM_ALL = 60 * 2**20
ANY = pl.BlockSpec(memory_space=pl.ANY)


def dot(a, b, dims):
    return lax.dot_general(a, b, dims, preferred_element_type=F32)


def struct(shape, dtype):
    return jax.ShapeDtypeStruct(shape, dtype)


def call(body, name, flops=0, moved=0, vmem=VMEM_LIMIT, **kwargs):
    cost = pl.CostEstimate(flops=int(flops), bytes_accessed=int(moved), transcendentals=0)
    params = pltpu.CompilerParams(vmem_limit_bytes=vmem)
    return pl.pallas_call(body, name=name, cost_estimate=cost, compiler_params=params, **kwargs)


def head_masks(width, depth):
    lane = lax.broadcasted_iota(jnp.int32, (1, width), 1)
    return [(lane >= h * depth) & (lane < (h + 1) * depth) for h in range(width // depth)]


def keep_head(rows, mask, scale=None):
    rows = jnp.where(mask, rows, 0)
    if scale is not None:
        rows = rows.astype(F32) * scale
    return rows.astype(BF16)


def near(block, blocks):
    return range(max(block - 1, 0), min(block + 2, blocks))


def edge_body(k, v, out):
    out[0] = k[...]
    out[1] = v[...]


def edge(k, v, block):
    cols = k.shape[1]
    spec = pl.BlockSpec((BLOCK, cols), lambda i: (block, 0))
    return call(
        edge_body,
        "edge",
        moved=8 * BLOCK * cols,
        vmem=VMEM_ALL,
        grid=(1,),
        in_specs=[spec, spec],
        out_specs=pl.BlockSpec((2, BLOCK, cols), lambda i: (0, 0, 0)),
        out_shape=struct((2, BLOCK, cols), BF16),
    )(k, v)


def pool_body(depth, k, v, group_pool, whole_pool, groups, wholes, first, wide_group, wide_whole):
    rows, width = k.shape
    heads = group_pool.shape[0]
    start = pl.program_id(0) * width
    head = lax.broadcasted_iota(jnp.int32, (heads, width), 0)
    col = lax.broadcasted_iota(jnp.int32, (heads, width), 1) + start
    pick = ((col >= head * depth) & (col < (head + 1) * depth)).astype(F32)
    for src, dst in ((group_pool, wide_group), (whole_pool, wide_whole)):
        dst[...] = lax.dot_general(
            src[...],
            pick,
            (((0,), (0,)), ((), ())),
            precision=lax.Precision.HIGHEST,
            preferred_element_type=F32,
        )
    for n, src in enumerate((k, v)):
        first[n] = src[:BLOCK]
        for segment, wide, dst in ((SEG1, wide_group, groups), (SEG2, wide_whole, wholes)):
            sums = []
            for s in range(rows // segment):
                part = src[s * segment : (s + 1) * segment].astype(F32) * wide[...]
                sums.append(jnp.sum(part, axis=0, keepdims=True))
            dst[n] = jnp.concatenate(sums, axis=0).astype(BF16)


def pool(k, v, group_pool, whole_pool, width):
    rows, cols = k.shape
    heads = group_pool.shape[0]
    count1, count2 = rows // SEG1, rows // SEG2
    column = lambda n: pl.BlockSpec((n, width), lambda i: (0, i))
    both = lambda n: pl.BlockSpec((2, n, width), lambda i: (0, 0, i))
    full = lambda x: pl.BlockSpec(x.shape, lambda i: (0, 0))
    return call(
        functools.partial(pool_body, cols // heads),
        "pool",
        moved=k.size * 6,
        vmem=VMEM_ALL,
        grid=(cols // width,),
        in_specs=[column(rows), column(rows), full(group_pool), full(whole_pool)],
        out_specs=[both(count1), both(count2), both(BLOCK), column(SEG1), column(SEG2)],
        out_shape=[
            struct((2, count1, cols), BF16),
            struct((2, count2, cols), BF16),
            struct((2, BLOCK, cols), BF16),
            struct((SEG1, cols), F32),
            struct((SEG2, cols), F32),
        ],
    )(k, v, group_pool, whole_pool)


def join_body(axis, has_token, *refs):
    parts, out = refs[: len(refs) - 1 - has_token], refs[-1]
    at = 0
    for part in parts:
        size = part.shape[axis]
        if axis == 0:
            out[at : at + size] = part[...]
            at += size
    if axis == 1:
        for n in range(2):
            rows = [part[n].astype(F32) for part in parts]
            out[n] = jnp.concatenate(rows, axis=0).astype(BF16)


def join(parts, axis, token=None):
    shape = list(parts[0].shape)
    shape[axis] = sum(part.shape[axis] for part in parts)
    tokens = [] if token is None else [token]
    return call(
        functools.partial(join_body, axis, len(tokens)),
        "join",
        moved=4 * math.prod(shape),
        in_specs=[pl.BlockSpec(memory_space=pltpu.VMEM)] * len(parts) + [ANY] * len(tokens),
        out_shape=struct(tuple(shape), BF16),
    )(*parts, *tokens)


def stats_body(depth, scale, q, k, v, g, out):
    rows, width = q.shape
    blocks = rows // BLOCK
    chunk = 64
    for h, mask in enumerate(head_masks(width, depth)):
        for b in range(blocks):
            r = slice(b * BLOCK, (b + 1) * BLOCK)
            qs = keep_head(q[r], mask, scale)
            gs = keep_head(g[r], mask)
            lo, hi = near(b, blocks)[0] * BLOCK, (near(b, blocks)[-1] + 1) * BLOCK
            s_all = dot(k[lo:hi], qs, NT)
            d_all = dot(v[lo:hi], gs, NT)
            top = total = inner = None
            for c in range(0, hi - lo, chunk):
                s = s_all[c : c + chunk].reshape(chunk // 8, 8, BLOCK)
                d = d_all[c : c + chunk].reshape(chunk // 8, 8, BLOCK)
                here = jnp.max(s, axis=0)
                if top is None:
                    new = here
                else:
                    new = jnp.maximum(top, here)
                e = jnp.exp(s - new[None])
                sum_e = jnp.sum(e, axis=0)
                sum_d = jnp.sum(e * d, axis=0)
                if top is not None:
                    fade = jnp.exp(top - new)
                    sum_e = sum_e + total * fade
                    sum_d = sum_d + inner * fade
                top, total, inner = new, sum_e, sum_d
            most = jnp.max(top, axis=0, keepdims=True)
            fade = jnp.exp(top - most)
            out[0, h : h + 1, r] = most
            out[1, h : h + 1, r] = jnp.sum(total * fade, axis=0, keepdims=True)
            out[2, h : h + 1, r] = jnp.sum(inner * fade, axis=0, keepdims=True)


def stats(q, k, v, g, width, depth, scale, pair):
    rows = q.shape[0]
    hp = width // depth
    cols = pl.BlockSpec((rows, width), lambda i: (0, pair))
    return call(
        functools.partial(stats_body, depth, scale),
        f"stats{pair}",
        flops=2 * 2 * 3 * BLOCK * rows * width,
        moved=rows * width * 8,
        grid=(1,),
        in_specs=[cols] * 4,
        out_specs=pl.BlockSpec((3, hp, rows), lambda i: (0, 0, 0)),
        out_shape=struct((3, hp, rows), F32),
    )(q, k, v, g)


def remote_body(depth, scale, pairs, ends, q, g, before, after, mine, theirs, *rest):
    partial = rest[:pairs]
    kept, sent, to_prev, to_next, dq_t, final, far_k, far_v = rest[pairs : pairs + 8]
    far_kt, near_t, far_dk, far_dv, near_d = rest[pairs + 8 :]
    rows, width = q.shape
    blocks = rows // BLOCK
    slots, _, per, _ = mine.shape
    half = slots * per
    pair = pl.program_id(0)
    for n, far in enumerate((far_k, far_v)):
        pieces = [src[s, n].astype(F32) for src in (mine, theirs) for s in range(slots)]
        far[...] = jnp.concatenate(pieces, axis=0).astype(BF16)
    far_kt[...] = (far_k[...].astype(F32) * scale).astype(BF16).T
    near_t[0] = (before[0].astype(F32) * scale).astype(BF16).T
    near_t[1] = (after[0].astype(F32) * scale).astype(BF16).T
    low = jnp.where(ends[0] == 1, NEG, 0.0)
    high = jnp.where(ends[1] == 1, NEG, 0.0)
    for h, mask in enumerate(head_masks(width, depth)):
        hr = slice(h * depth, (h + 1) * depth)
        for b in range(blocks):
            r = slice(b * BLOCK, (b + 1) * BLOCK)
            qs = keep_head(q[r], mask, scale)
            gs = keep_head(g[r], mask)
            scores = [dot(far_k[...], qs, NT)]
            values = [dot(far_v[...], gs, NT)]
            turned = [far_kt[hr]]
            sinks = [(far_dk, far_dv)]
            if b == 0:
                scores.append(dot(before[0], qs, NT) + low)
                values.append(dot(before[1], gs, NT))
                turned.append(near_t[0, hr])
                sinks.append((near_d.at[0], near_d.at[1]))
            if b == blocks - 1:
                scores.append(dot(after[0], qs, NT) + high)
                values.append(dot(after[1], gs, NT))
                turned.append(near_t[1, hr])
                sinks.append((near_d.at[2], near_d.at[3]))
            old = [partial[0][n, h : h + 1, r] for n in range(3)]
            for n in range(1, pairs):
                old = [
                    jnp.where(pair == n, partial[n][m, h : h + 1, r], old[m]) for m in range(3)
                ]
            top = old[0]
            for s in scores:
                top = jnp.maximum(top, jnp.max(s, axis=0, keepdims=True))
            fade = jnp.exp(old[0] - top)
            total = old[1] * fade
            inner = old[2] * fade
            exps = []
            for s, d in zip(scores, values):
                e = jnp.exp(s - top)
                exps.append(e)
                total = total + jnp.sum(e, axis=0, keepdims=True)
                inner = inner + jnp.sum(e * d, axis=0, keepdims=True)
            share = 1.0 / total
            delta = inner * share
            final[0, h : h + 1, r] = top + jnp.log(total)
            final[1, h : h + 1, r] = delta
            dq = None
            for n, (e, d, kt, (dk, dv)) in enumerate(zip(exps, values, turned, sinks)):
                p = e * share
                ds = (p * (d - delta)).astype(BF16)
                v_part = dot(p.astype(BF16), gs, NN)
                k_part = dot(ds, qs, NN)
                if h == 0 and (n or b == 0):
                    dv[...] = v_part
                    dk[...] = k_part
                else:
                    dv[...] += v_part
                    dk[...] += k_part
                part = dot(kt, ds, NN)
                dq = part if dq is None else dq + part
            dq_t[hr, r] = dq
    for n, far in enumerate((far_dk, far_dv)):
        kept[n] = far[:half]
        sent[n] = far[half:].astype(BF16)
        to_prev[n] = near_d[n].astype(BF16)
        to_next[n] = near_d[2 + n].astype(BF16)


def remote(q, g, before, after, mine, theirs, partial, ends, width, depth, scale):
    rows, cols = q.shape
    pairs = cols // width
    hp = width // depth
    slots, _, per, _ = mine.shape
    half = slots * per
    far = 2 * half
    wide = lambda n: pl.BlockSpec((n, width), lambda i, *_: (0, i))
    both = lambda n: pl.BlockSpec((2, n, width), lambda i, *_: (0, 0, i))
    slot = pl.BlockSpec((slots, 2, per, width), lambda i, *_: (0, 0, 0, i))
    fixed = pl.BlockSpec((3, hp, rows), lambda i, *_: (0, 0, 0))
    grid_spec = pltpu.PrefetchScalarGridSpec(
        num_scalar_prefetch=1,
        grid=(pairs,),
        in_specs=[wide(rows)] * 2 + [both(BLOCK)] * 2 + [slot] * 2 + [fixed] * pairs,
        out_specs=[
            both(half),
            both(half),
            both(BLOCK),
            both(BLOCK),
            pl.BlockSpec((width, rows), lambda i, *_: (i, 0)),
            pl.BlockSpec((None, 2, hp, rows), lambda i, *_: (i, 0, 0, 0)),
        ],
        scratch_shapes=[
            pltpu.VMEM((far, width), BF16),
            pltpu.VMEM((far, width), BF16),
            pltpu.VMEM((width, far), BF16),
            pltpu.VMEM((2, width, BLOCK), BF16),
            pltpu.VMEM((far, width), F32),
            pltpu.VMEM((far, width), F32),
            pltpu.VMEM((4, BLOCK, width), F32),
        ],
    )
    return call(
        functools.partial(remote_body, depth, scale, pairs),
        "remote",
        flops=10 * (far * rows + 2 * BLOCK * BLOCK) * cols,
        moved=rows * cols * 8,
        grid_spec=grid_spec,
        out_shape=[
            struct((2, half, cols), F32),
            struct((2, half, cols), BF16),
            struct((2, BLOCK, cols), BF16),
            struct((2, BLOCK, cols), BF16),
            struct((cols, rows), F32),
            struct((pairs, 2, hp, rows), F32),
        ],
    )(ends, q, g, before, after, mine, theirs, *partial)


def local_body(depth, scale, chained, q, k, v, g, part, final, *rest):
    dq, dk, dv, k_t, dq_t = rest[chained:]
    rows, width = q.shape
    blocks = rows // BLOCK
    k_t[...] = (k[...].astype(F32) * scale).astype(BF16).T
    for h, mask in enumerate(head_masks(width, depth)):
        hr = slice(h * depth, (h + 1) * depth)
        for b in range(blocks):
            r = slice(b * BLOCK, (b + 1) * BLOCK)
            qs = keep_head(q[r], mask, scale)
            gs = keep_head(g[r], mask)
            reach = near(b, blocks)
            c = slice(reach[0] * BLOCK, (reach[-1] + 1) * BLOCK)
            p = jnp.exp(dot(k[c], qs, NT) - final[0, h : h + 1, r])
            ds = (p * (dot(v[c], gs, NT) - final[1, h : h + 1, r])).astype(BF16)
            v_part = dot(p.astype(BF16), gs, NN)
            k_part = dot(ds, qs, NN)
            for n, j in enumerate(reach):
                rj = slice(j * BLOCK, (j + 1) * BLOCK)
                here = slice(n * BLOCK, (n + 1) * BLOCK)
                if h == 0 and b == near(j, blocks)[0]:
                    dv[rj] = v_part[here]
                    dk[rj] = k_part[here]
                else:
                    dv[rj] += v_part[here]
                    dk[rj] += k_part[here]
            dq_t[hr, r] = part[hr, r] + dot(k_t[hr, c], ds, NN)
    dq[...] = dq_t[...].T.astype(BF16)


def local(q, k, v, g, part, final, before, width, depth, scale, pair):
    rows, cols = q.shape
    hp = width // depth
    column = pl.BlockSpec((rows, width), lambda i: (0, pair))
    alone = pl.BlockSpec((rows, width), lambda i: (0, 0))
    extra = [] if before is None else [before]
    return call(
        functools.partial(local_body, depth, scale, len(extra)),
        f"local{pair}",
        flops=10 * 3 * BLOCK * rows * width,
        moved=rows * width * 24,
        grid=(1,),
        in_specs=[column] * 4
        + [
            pl.BlockSpec((width, rows), lambda i: (pair, 0)),
            pl.BlockSpec((None, 2, hp, rows), lambda i: (pair, 0, 0, 0)),
        ]
        + [ANY] * len(extra),
        out_specs=[column, alone, alone],
        out_shape=[struct((rows, cols), BF16)] + [struct((rows, width), F32)] * 2,
        scratch_shapes=[pltpu.VMEM((width, rows), BF16), pltpu.VMEM((width, rows), F32)],
        input_output_aliases={6: 0} if extra else {},
    )(q, k, v, g, part, final, *extra)


def fold_body(at, cut, kept, got, *rest):
    next_kept, next_sent = rest[-2:]
    for n in range(2):
        rows = kept[n, at:] + got[n].astype(F32)
        if at:
            rows = jnp.concatenate([kept[n, :at], rows], axis=0)
        next_kept[n] = rows[:cut]
        next_sent[n] = rows[cut:].astype(BF16)


def fold(kept, got, cut, tokens=(), passed=()):
    cols = kept.shape[-1]
    rows = kept.shape[1]
    at = rows - got.shape[1]
    vmem = pl.BlockSpec(memory_space=pltpu.VMEM)
    extra = list(passed) + list(tokens)

    def body(kept, got, *rest):
        fold_body(at, cut, kept, got, *rest[len(extra) : len(extra) + 2])

    return call(
        body,
        "fold",
        moved=kept.size * 8,
        in_specs=[vmem, vmem] + [ANY] * len(extra),
        out_specs=[vmem, vmem] + [ANY] * len(passed),
        out_shape=[struct((2, cut, cols), F32), struct((2, rows - cut, cols), BF16)]
        + [struct(x.shape, x.dtype) for x in passed],
        input_output_aliases={2 + n: 2 + n for n in range(len(passed))},
    )(kept, got, *extra)


def finish_body(pairs, *refs):
    dk, dv = refs[:pairs], refs[pairs : 2 * pairs]
    from_prev, from_next, kept, got, wide_group, wide_whole, out_k, out_v = refs[2 * pairs :]
    block = pl.program_id(0)
    blocks = pl.num_programs(0)
    width = dk[0].shape[1]
    per = BLOCK // SEG1
    rows = kept.shape[1]
    at = rows - got.shape[1]
    count1 = rows * SEG2 // (SEG1 + SEG2)
    low = jnp.where(block == 0, 1.0, 0.0)
    high = jnp.where(block == blocks - 1, 1.0, 0.0)
    index = lax.broadcasted_iota(jnp.int32, (rows, 1), 0)
    for n, (src, dst) in enumerate(((dk, out_k), (dv, out_v))):
        sums = kept[n, at:] + got[n].astype(F32)
        if at:
            sums = jnp.concatenate([kept[n, :at], sums], axis=0)
        whole = jnp.sum(jnp.where(index == count1 + block, sums, 0.0), axis=0, keepdims=True)
        for s in range(per):
            mine = jnp.where(index == block * per + s, sums, 0.0)
            group = jnp.sum(mine, axis=0, keepdims=True)
            c = slice(s * SEG1, (s + 1) * SEG1)
            piece = group * wide_group[...] + whole * wide_whole[c]
            piece = piece + low * from_prev[n, c].astype(F32) + high * from_next[n, c].astype(F32)
            for p in range(pairs):
                lanes = slice(p * width, (p + 1) * width)
                dst[c, lanes] = (piece[:, lanes] + src[p][c]).astype(BF16)


def finish(dk, dv, from_prev, from_next, kept, got, wide_group, wide_whole):
    rows, width = dk[0].shape
    pairs = len(dk)
    cols = width * pairs
    tile = pl.BlockSpec((BLOCK, cols), lambda i: (i, 0))
    narrow = pl.BlockSpec((BLOCK, width), lambda i: (i, 0))
    full = lambda x: pl.BlockSpec(x.shape, lambda i: (0,) * x.ndim)
    return call(
        functools.partial(finish_body, pairs),
        "finish",
        moved=rows * cols * 12,
        grid=(rows // BLOCK,),
        in_specs=[narrow] * (2 * pairs)
        + [full(x) for x in (from_prev, from_next, kept, got, wide_group, wide_whole)],
        out_specs=[tile, tile],
        out_shape=[struct((rows, cols), BF16)] * 2,
    )(*dk, *dv, from_prev, from_next, kept, got, wide_group, wide_whole)


def shards(query, key, value, out_grad, pool_group, pool_global):
    rows, cols = query.shape
    heads = pool_group.shape[0]
    depth = cols // heads
    scale = 1.0 / math.sqrt(depth)
    width = 128 if cols % 128 == 0 and 128 % depth == 0 else cols
    pairs = cols // width
    devices = lax.axis_size("seq")
    position = lax.axis_index("seq")
    count1, count2 = rows // SEG1, rows // SEG2
    group_bits = list(range(1, GROUP.bit_length() - 1))
    other_bits = list(range(GROUP.bit_length() - 1, devices.bit_length() - 1))

    def swap(array, bit):
        return lax.ppermute(array, "seq", [(i, i ^ (1 << bit)) for i in range(devices)])

    def shift(array, by):
        route = [(i, i + by) for i in range(devices) if 0 <= i + by < devices]
        return lax.ppermute(array, "seq", route)

    before = shift(edge(key, value, rows // BLOCK - 1), 1)
    groups, wholes, first, wide_group, wide_whole = pool(
        key, value, pool_group, pool_global, width
    )
    ends = jnp.stack([position == 0, position == devices - 1]).astype(jnp.int32)
    partial = [
        stats(query, key, value, out_grad, width, depth, scale, p) for p in range(pairs)
    ]
    waiting = list(partial)

    def token():
        return waiting.pop(0) if waiting else None

    for n, bit in enumerate(other_bits):
        got = swap(wholes, bit)
        if n < len(other_bits) - 1:
            wholes = join([wholes, got], 1)
    parts = [groups, wholes] + ([got] if other_bits else [])
    comb = join(parts, 1, token())[None]
    after = None
    for bit in group_bits:
        got = swap(comb, bit)
        if after is None:
            after = shift(first, -1)
        comb = join([comb, got], 0, token())
    theirs = swap(comb, 0)

    kept, sent, to_prev, to_next, dq_t, final = remote(
        query, out_grad, before, after, comb, theirs, partial, ends, width, depth, scale
    )
    got = swap(sent, 0)
    from_next = shift(to_prev, -1)

    query_grad, dk, dv = None, [], []

    def step():
        nonlocal query_grad
        if len(dk) == pairs:
            return []
        query_grad, a, b = local(
            query, key, value, out_grad, dq_t, final, query_grad, width, depth, scale, len(dk)
        )
        dk.append(a)
        dv.append(b)
        return [a]

    from_prev = None
    for bit in list(reversed(group_bits)) + list(reversed(other_bits)):
        size = kept.shape[1]
        if bit in group_bits:
            cut = size // 2
        else:
            cut = count1 + (size - count1) // 2
        if from_prev is None:
            kept, sent, to_next = fold(kept, got, cut, step(), [to_next])
            got = swap(sent, bit)
            from_prev = shift(to_next, 1)
        else:
            kept, sent = fold(kept, got, cut, step())
            got = swap(sent, bit)
    while len(dk) < pairs:
        step()
    key_grad, value_grad = finish(
        dk, dv, from_prev, from_next, kept, got, wide_group, wide_whole
    )
    return (query_grad, key_grad, value_grad)


def solution(mesh):
    rows = P("seq", "head")
    in_specs = (rows, rows, rows, rows, P("head", None), P("head", None))
    return jax.shard_map(
        shards, mesh=mesh, in_specs=in_specs, out_specs=(rows, rows, rows), check_vma=False
    )
```

time: 106 us -> 85.6 us (0.81)
  Pallas kernels: 64.1 us -> 50.3 us
  local copies, waits for them, and re-layouts: 8.29 us -> 2.48 us
    pallas_call x10 -> x13, Pallas kernels: 37.6 us -> 26.3 us  [the longest x4 16.9 us: local(): call(functools.partial(local_body, depth, scale, len(extra)), f'local{pai...]
    unnamed x30 -> x22, local copies, waits for them, and re-layouts: 8.27 us -> 2.48 us
    ppermute x4, starting transfers between devices: 9.64 us -> 12.3 us  [shift(): return lax.ppermute(array, 'seq', route)]
    pallas_call x1, Pallas kernels: 19.5 us -> 17 us  [remote(): call(functools.partial(remote_body, depth, scale, pairs), 'remote', flops...]
    ppermute x8, starting transfers between devices: 20.1 us -> 17.8 us  [swap(): lax.ppermute(array, 'seq', [(i, i ^ 1 << bit) for i in range(devices)])]
  transfers between devices with their start and end apart: 12 -> 12, of which waited for: 1 -> 2; matrix products, arithmetic and copies ran while one was open for 0% -> 0% of each run, Pallas kernels for 38% -> 33%
where the time goes in v1:
time: 85.6 us; the launch traced here: 85.2 us
  Pallas kernels  50.3 us (59%)
  starting transfers between devices  30.1 us (35%)
  local copies, waits for them, and re-layouts  2.48 us (3%)
  waiting for transfers between devices  1.54 us (2%)
    ppermute x8, starting transfers between devices, swap(): lax.ppermute(array, 'seq', [(i, i ^ 1 << bit) for i in range(devices)])  17.8 us
    pallas_call x1, Pallas kernels, remote(): call(functools.partial(remote_body, depth, scale, pairs), 'remote', flops...  17 us
    pallas_call x4, Pallas kernels, local(): call(functools.partial(local_body, depth, scale, len(extra)), f'local{pai...  16.9 us
    ppermute x4, starting transfers between devices, shift(): return lax.ppermute(array, 'seq', route)  12.3 us
    pallas_call x4, Pallas kernels, stats(): call(functools.partial(stats_body, depth, scale), f'stats{pair}', flops=2...  6.96 us
    pallas_call x1, Pallas kernels, pool(): call(functools.partial(pool_body, cols // heads), 'pool', moved=k.size *...  4.38 us
    pallas_call x1, Pallas kernels, finish(): call(functools.partial(finish_body, pairs), 'finish', moved=rows * cols *...  2.92 us
    unnamed x22, local copies, waits for them, and re-layouts  2.48 us
  transfers between devices with their start and end apart: 12, of which 2 were waited for; matrix products, arithmetic and copies ran while one was open for 0% of the time, Pallas kernels for 33%

profile of v1, /device:TPU:1, one launch (start us, length us, event | category | flops | bytes accessed | tf_op | source)
XLA Modules:
  0.0 85.2 jit_solution(8070448994734928828)
XLA Ops:
  0.6 0.0 copy-start.1
  0.6 0.0 copy-start
  0.7 2.0 %edge.1 = bf16[2,256,512]{2,1,0:T(8,128)(2,1)} custom-call(bf16[1024,512]{1,0:T(8,128)(2,1)} %k.19, bf16[1024,512]{1,0:T(8,128)(2,1)} %v.19), custom_call_target="tpu_custom_call" | custom-call | bytes 1048576 | tf_op jit(solution)/shard_map/edge/pallas_call | solution.py:63
  2.7 4.5 %collective-permute-start = (bf16[2,256,512]{2,1,0:T(8,128)(2,1)}, bf16[2,256,512]{2,1,0:T(8,128)(2,1)}, u32[]{:S(2)}, u32[]{:S(2)}) collective-permute-start(bf16[2,256,512]{2,1,0:T(8,128)(2,1)} %edge.1), channel_id=1, source_target_pairs={{0,2},{2,4},{4,6},{6,8},{8,10},{10,12},{12,14},{14,16},{16,18},{18... | collective-permute-start | bytes 1572872 | tf_op jit(solution)/shard_map/ppermute | solution.py:487
  7.2 4.4 %pool.1 = (bf16[2,16,512]{2,1,0:T(8,128)(2,1)}, bf16[2,4,512]{2,1,0:T(4,128)(2,1)}, bf16[2,256,512]{2,1,0:T(8,128)(2,1)}, f32[64,512]{1,0:T(8,128)}, f32[256,512]{1,0:T(8,128)}) custom-call(bf16[1024,512]{1,0:T(8,128)(2,1)} %k.19, bf16[1024,512]{1,0:T(8,128)(2,1)} %v.19, f32[8,64]{1,0:T(8,128)} %group_pool.1, f32[8,256]{1,0:T(8,128)} %whole_pool.1), custom_call_target="tpu_custom_call" | custom-call | bytes 3145728 | tf_op jit(solution)/shard_map/pool/pallas_call | solution.py:107
  11.6 1.9 %collective-permute-start.1 = (bf16[2,256,512]{2,1,0:T(8,128)(2,1)}, bf16[2,256,512]{2,1,0:T(8,128)(2,1)}, u32[]{:S(2)}, u32[]{:S(2)}) collective-permute-start(bf16[2,256,512]{2,1,0:T(8,128)(2,1)} %get-tuple-element.35), channel_id=1, source_target_pairs={{2,0},{4,2},{6,4},{8,6},{10,8},{12,10},{14,12},{16,14},{18,16},{20... | collective-permute-start | bytes 1572872 | tf_op jit(solution)/shard_map/ppermute | solution.py:487
  13.5 2.4 %collective-permute-start.2 = (bf16[2,4,512]{2,1,0:T(4,128)(2,1)}, bf16[2,4,512]{2,1,0:T(4,128)(2,1)S(1)}, u32[]{:S(2)}, u32[]{:S(2)}) collective-permute-start(bf16[2,4,512]{2,1,0:T(4,128)(2,1)} %get-tuple-element.37.refs_1_), channel_id=1, source_target_pairs={{0,16},{2,18},{4,20},{6,22},{8,24},{10,26},{12,28},{14,30},{16,0},... | collective-permute-start | bytes 24584 | tf_op jit(solution)/shard_map/ppermute | solution.py:483
  15.9 1.2 %copy-done.3 = bf16[1024,512]{1,0:T(8,128)(2,1)S(1)} copy-done((bf16[1024,512]{1,0:T(8,128)(2,1)S(1)}, bf16[1024,512]{1,0:T(8,128)(2,1)}, u32[]{:S(2)}) %copy-start.3) | copy-done | bytes 1048600
  17.1 1.7 %stats0.1.refs_3_.rest_0_ = f32[3,2,1024]{2,1,0:T(2,128)S(1)} custom-call(bf16[1024,512]{1,0:T(8,128)(2,1)S(1)} %copy-done.2, bf16[1024,512]{1,0:T(8,128)(2,1)S(1)} %copy-done, bf16[1024,512]{1,0:T(8,128)(2,1)S(1)} %copy-done.1, bf16[1024,512]{1,0:T(8,128)(2,1)S(1)} %copy-done.3), custom_call_target="tpu_custom_call" | custom-call | flops 402653184 | bytes 1048576 | tf_op jit(solution)/shard_map/stats0/pallas_call | solution.py:192
  18.9 0.0 collective-permute-done.2.refs_2_
  18.9 1.3 %collective-permute-start.3 = (bf16[1,2,24,512]{3,2,1,0:T(8,128)(2,1)S(1)}, bf16[1,2,24,512]{3,2,1,0:T(8,128)(2,1)S(1)}, u32[]{:S(2)}, u32[]{:S(2)}) collective-permute-start(bf16[1,2,24,512]{3,2,1,0:T(8,128)(2,1)S(1)} %bitcast.3), channel_id=1, source_target_pairs={{0,4},{2,6},{4,0},{6,2},{8,12},{10,14},{12,8},{14,10},{16,20},{18,... | collective-permute-start | bytes 147464 | tf_op jit(solution)/shard_map/ppermute | solution.py:483
  20.2 1.7 %stats1.1.refs_2_.rest_1_ = f32[3,2,1024]{2,1,0:T(2,128)S(1)} custom-call(bf16[1024,512]{1,0:T(8,128)(2,1)S(1)} %copy-done.2, bf16[1024,512]{1,0:T(8,128)(2,1)S(1)} %copy-done, bf16[1024,512]{1,0:T(8,128)(2,1)S(1)} %copy-done.1, bf16[1024,512]{1,0:T(8,128)(2,1)S(1)} %copy-done.4), custom_call_target="tpu_custom_call" | custom-call | flops 402653184 | bytes 1048576 | tf_op jit(solution)/shard_map/stats1/pallas_call | solution.py:192
  22.0 1.1 %collective-permute-done.3.refs_1_ = bf16[1,2,24,512]{3,2,1,0:T(8,128)(2,1)S(1)} collective-permute-done((bf16[1,2,24,512]{3,2,1,0:T(8,128)(2,1)S(1)}, bf16[1,2,24,512]{3,2,1,0:T(8,128)(2,1)S(1)}, u32[]{:S(2)}, u32[]{:S(2)}) %collective-permute-start.3) | collective-permute-done | bytes 49184 | tf_op jit(solution)/shard_map/ppermute | solution.py:483
  23.1 1.3 %collective-permute-start.4 = (bf16[2,2,24,512]{3,2,1,0:T(8,128)(2,1)S(1)}, bf16[2,2,24,512]{3,2,1,0:T(8,128)(2,1)S(1)}, u32[]{:S(2)}, u32[]{:S(2)}) collective-permute-start(bf16[2,2,24,512]{3,2,1,0:T(8,128)(2,1)S(1)} %join.4.refs_0_), channel_id=1, source_target_pairs={{0,8},{2,10},{4,12},{6,14},{8,0},{10,2},{12,4},{14,6},{16,24},{18,... | collective-permute-start | bytes 294920 | tf_op jit(solution)/shard_map/ppermute | solution.py:483
  24.3 1.7 %stats2.1.refs_2_.rest_2_ = f32[3,2,1024]{2,1,0:T(2,128)S(1)} custom-call(bf16[1024,512]{1,0:T(8,128)(2,1)S(1)} %copy-done.2, bf16[1024,512]{1,0:T(8,128)(2,1)S(1)} %copy-done, bf16[1024,512]{1,0:T(8,128)(2,1)S(1)} %copy-done.1, bf16[1024,512]{1,0:T(8,128)(2,1)S(1)} %copy-done.4), custom_call_target="tpu_custom_call" | custom-call | flops 402653184 | bytes 1048576 | tf_op jit(solution)/shard_map/stats2/pallas_call | solution.py:192
  26.1 0.4 collective-permute-done.4.refs_1_
  26.5 7.5 %collective-permute-start.5 = (bf16[4,2,24,512]{3,2,1,0:T(8,128)(2,1)S(1)}, bf16[4,2,24,512]{3,2,1,0:T(8,128)(2,1)}, u32[]{:S(2)}, u32[]{:S(2)}) collective-permute-start(bf16[4,2,24,512]{3,2,1,0:T(8,128)(2,1)S(1)} %join.5.mine), channel_id=1, source_target_pairs={{0,2},{2,0},{4,6},{6,4},{8,10},{10,8},{12,14},{14,12},{16,18},{18,... | collective-permute-start | bytes 589832 | tf_op jit(solution)/shard_map/ppermute | solution.py:483
  34.0 1.2 %copy-done.5 = bf16[1024,512]{1,0:T(8,128)(2,1)S(1)} copy-done((bf16[1024,512]{1,0:T(8,128)(2,1)S(1)}, bf16[1024,512]{1,0:T(8,128)(2,1)}, u32[]{:S(2)}) %copy-start.5) | copy-done | bytes 1048600
  35.2 1.7 %stats3.1.rest_3_ = f32[3,2,1024]{2,1,0:T(2,128)S(1)} custom-call(bf16[1024,512]{1,0:T(8,128)(2,1)S(1)} %copy-done.2, bf16[1024,512]{1,0:T(8,128)(2,1)S(1)} %copy-done, bf16[1024,512]{1,0:T(8,128)(2,1)S(1)} %copy-done.1, bf16[1024,512]{1,0:T(8,128)(2,1)S(1)} %copy-done.5), custom_call_target="tpu_custom_call" | custom-call | flops 402653184 | bytes 1048576 | tf_op jit(solution)/shard_map/stats3/pallas_call | solution.py:192
  37.0 0.1 add_convert_fusion.ends
  37.1 17.0 %remote.1 = (f32[2,96,512]{2,1,0:T(8,128)S(1)}, bf16[2,96,512]{2,1,0:T(8,128)(2,1)S(1)}, bf16[2,256,512]{2,1,0:T(8,128)(2,1)S(1)}, bf16[2,256,512]{2,1,0:T(8,128...) custom-call(s32[2]{0:T(128)S(1)} %add_convert_fusion.ends, bf16[1024,512]{1,0:T(8,128)(2,1)S(1)} %copy-done.2, ...), custom_call_target="tpu_custom_call" | custom-call | flops 1677721600 | bytes 4194304 | tf_op jit(solution)/shard_map/remote/pallas_call | solution.py:317
  54.1 0.1 collective-permute-start.6
  54.2 2.6 %collective-permute-start.8 = (bf16[2,256,512]{2,1,0:T(8,128)(2,1)S(1)}, bf16[2,256,512]{2,1,0:T(8,128)(2,1)S(1)}, u32[]{:S(2)}, u32[]{:S(2)}) collective-permute-start(bf16[2,256,512]{2,1,0:T(8,128)(2,1)S(1)} %get-tuple-element.56), channel_id=1, source_target_pairs={{2,0},{4,2},{6,4},{8,6},{10,8},{12,10},{14,12},{16,14},{18,16},{20... | collective-permute-start | bytes 1572872 | tf_op jit(solution)/shard_map/ppermute | solution.py:487
  56.8 4.2 %local0.1 = (bf16[1024,512]{1,0:T(8,128)(2,1)}, f32[1024,128]{1,0:T(8,128)S(1)}, f32[1024,128]{1,0:T(8,128)S(1)}) custom-call(bf16[1024,512]{1,0:T(8,128)(2,1)S(1)} %copy-done.2, bf16[1024,512]{1,0:T(8,128)(2,1)S(1)} %copy-done, bf16[1024,512]{1,0:T(8,128)(2,1)S(1)} %copy-done.1, bf16[1024,512]{1,0:T(8,128)(2,1)S(1)} %copy-done.5, ...), custom_call_target="tpu_custom_call" | custom-call | flops 1006632960 | bytes 3145728 | tf_op jit(solution)/shard_map/local0/pallas_call | solution.py:370
  61.0 3.3 %collective-permute-start.7 = (bf16[2,256,512]{2,1,0:T(8,128)(2,1)S(1)}, bf16[2,256,512]{2,1,0:T(8,128)(2,1)S(1)}, u32[]{:S(2)}, u32[]{:S(2)}) collective-permute-start(bf16[2,256,512]{2,1,0:T(8,128)(2,1)S(1)} %get-tuple-element.55), channel_id=1, source_target_pairs={{0,2},{2,4},{4,6},{6,8},{8,10},{10,12},{12,14},{14,16},{16,18},{18... | collective-permute-start | bytes 1572872 | tf_op jit(solution)/shard_map/ppermute | solution.py:487
  64.3 1.4 %collective-permute-start.9 = (bf16[2,48,512]{2,1,0:T(8,128)(2,1)S(1)}, bf16[2,48,512]{2,1,0:T(8,128)(2,1)S(1)}, u32[]{:S(2)}, u32[]{:S(2)}) collective-permute-start(bf16[2,48,512]{2,1,0:T(8,128)(2,1)S(1)} %get-tuple-element.58), channel_id=1, source_target_pairs={{0,8},{2,10},{4,12},{6,14},{8,0},{10,2},{12,4},{14,6},{16,24},{18,... | collective-permute-start | bytes 294920 | tf_op jit(solution)/shard_map/ppermute | solution.py:483
  65.7 4.2 %local1.1 = (bf16[1024,512]{1,0:T(8,128)(2,1)}, f32[1024,128]{1,0:T(8,128)S(1)}, f32[1024,128]{1,0:T(8,128)S(1)}) custom-call(bf16[1024,512]{1,0:T(8,128)(2,1)S(1)} %copy-done.2, bf16[1024,512]{1,0:T(8,128)(2,1)S(1)} %copy-done, bf16[1024,512]{1,0:T(8,128)(2,1)S(1)} %copy-done.1, bf16[1024,512]{1,0:T(8,128)(2,1)S(1)} %copy-done.6, ...), custom_call_target="tpu_custom_call", output_to_operand_aliasing={{0}: (6, {})} | custom-call | flops 1006632960 | bytes 3145728 | tf_op jit(solution)/shard_map/local1/pallas_call | solution.py:370
  70.0 3.8 %collective-permute-start.10 = (bf16[2,24,512]{2,1,0:T(8,128)(2,1)S(1)}, bf16[2,24,512]{2,1,0:T(8,128)(2,1)S(1)}, u32[]{:S(2)}, u32[]{:S(2)}) collective-permute-start(bf16[2,24,512]{2,1,0:T(8,128)(2,1)S(1)} %get-tuple-element.60), channel_id=1, source_target_pairs={{0,4},{2,6},{4,0},{6,2},{8,12},{10,14},{12,8},{14,10},{16,20},{18,... | collective-permute-start | bytes 147464 | tf_op jit(solution)/shard_map/ppermute | solution.py:483
  73.8 4.2 %local2.1 = (bf16[1024,512]{1,0:T(8,128)(2,1)}, f32[1024,128]{1,0:T(8,128)S(1)}, f32[1024,128]{1,0:T(8,128)S(1)}) custom-call(bf16[1024,512]{1,0:T(8,128)(2,1)S(1)} %copy-done.2, bf16[1024,512]{1,0:T(8,128)(2,1)S(1)} %copy-done, bf16[1024,512]{1,0:T(8,128)(2,1)S(1)} %copy-done.1, bf16[1024,512]{1,0:T(8,128)(2,1)S(1)} %copy-done.6, ...), custom_call_target="tpu_custom_call", output_to_operand_aliasing={{0}: (6, {})} | custom-call | flops 1006632960 | bytes 3145728 | tf_op jit(solution)/shard_map/local2/pallas_call | solution.py:370
  78.0 0.1 collective-permute-start.11
  78.1 4.2 %local3.1 = (bf16[1024,512]{1,0:T(8,128)(2,1)}, f32[1024,128]{1,0:T(8,128)S(1)}, f32[1024,128]{1,0:T(8,128)S(1)}) custom-call(bf16[1024,512]{1,0:T(8,128)(2,1)S(1)} %copy-done.2, bf16[1024,512]{1,0:T(8,128)(2,1)S(1)} %copy-done, bf16[1024,512]{1,0:T(8,128)(2,1)S(1)} %copy-done.1, bf16[1024,512]{1,0:T(8,128)(2,1)S(1)} %copy-done.6, ...), custom_call_target="tpu_custom_call", output_to_operand_aliasing={{0}: (6, {})} | custom-call | flops 1006632960 | bytes 3145728 | tf_op jit(solution)/shard_map/local3/pallas_call | solution.py:370
  82.3 2.9 %finish.1 = (bf16[1024,512]{1,0:T(8,128)(2,1)}, bf16[1024,512]{1,0:T(8,128)(2,1)}) custom-call(f32[1024,128]{1,0:T(8,128)S(1)} %get-tuple-element.44.rest_1_.refs_0_, f32[1024,128]{1,0:T(8,128)S(1)} %get-tuple-element.45.rest_0_.refs_1_, f32[1024,128]{1,0:T(8,128)S(1)} %get-tuple-element.46.rest_0_.refs_2_, f32[1024,128]{1,0:T(8,128)S(1)} %get-tuple-element.47.refs_3_, ...), custom_call_target="tpu_custom_call" | custom-call | bytes 6291456 | tf_op jit(solution)/shard_map/finish/pallas_call | solution.py:457
  (33 shorter events, 0.2 us)
Async XLA Ops:
  0.6 15.2 %copy-start.1 = (bf16[1024,512]{1,0:T(8,128)(2,1)S(1)}, bf16[1024,512]{1,0:T(8,128)(2,1)}, u32[]{:S(2)}) copy-start(bf16[1024,512]{1,0:T(8,128)(2,1)} %v.19) | copy-start | bytes 3145732
  0.6 15.2 %copy-start = (bf16[1024,512]{1,0:T(8,128)(2,1)S(1)}, bf16[1024,512]{1,0:T(8,128)(2,1)}, u32[]{:S(2)}) copy-start(bf16[1024,512]{1,0:T(8,128)(2,1)} %k.19) | copy-start | bytes 3145732
  0.7 15.2 %copy-start.2 = (bf16[1024,512]{1,0:T(8,128)(2,1)S(1)}, bf16[1024,512]{1,0:T(8,128)(2,1)}, u32[]{:S(2)}) copy-start(bf16[1024,512]{1,0:T(8,128)(2,1)} %q.17) | copy-start | bytes 3145732
  2.7 34.4 %collective-permute-start = (bf16[2,256,512]{2,1,0:T(8,128)(2,1)}, bf16[2,256,512]{2,1,0:T(8,128)(2,1)}, u32[]{:S(2)}, u32[]{:S(2)}) collective-permute-start(bf16[2,256,512]{2,1,0:T(8,128)(2,1)} %edge.1), channel_id=1, source_target_pairs={{0,2},{2,4},{4,6},{6,8},{8,10},{10,12},{12,14},{14,16},{16,18},{18... | collective-permute-start | bytes 1572872 | tf_op jit(solution)/shard_map/ppermute | solution.py:487
  11.6 25.5 %collective-permute-start.1 = (bf16[2,256,512]{2,1,0:T(8,128)(2,1)}, bf16[2,256,512]{2,1,0:T(8,128)(2,1)}, u32[]{:S(2)}, u32[]{:S(2)}) collective-permute-start(bf16[2,256,512]{2,1,0:T(8,128)(2,1)} %get-tuple-element.35), channel_id=1, source_target_pairs={{2,0},{4,2},{6,4},{8,6},{10,8},{12,10},{14,12},{16,14},{18,16},{20... | collective-permute-start | bytes 1572872 | tf_op jit(solution)/shard_map/ppermute | solution.py:487
  13.5 5.4 %collective-permute-start.2 = (bf16[2,4,512]{2,1,0:T(4,128)(2,1)}, bf16[2,4,512]{2,1,0:T(4,128)(2,1)S(1)}, u32[]{:S(2)}, u32[]{:S(2)}) collective-permute-start(bf16[2,4,512]{2,1,0:T(4,128)(2,1)} %get-tuple-element.37.refs_1_), channel_id=1, source_target_pairs={{0,16},{2,18},{4,20},{6,22},{8,24},{10,26},{12,28},{14,30},{16,0},... | collective-permute-start | bytes 24584 | tf_op jit(solution)/shard_map/ppermute | solution.py:483
  15.9 1.2 %copy-start.3 = (bf16[1024,512]{1,0:T(8,128)(2,1)S(1)}, bf16[1024,512]{1,0:T(8,128)(2,1)}, u32[]{:S(2)}) copy-start(bf16[1024,512]{1,0:T(8,128)(2,1)} %g.17) | copy-start | bytes 3145732
  17.1 1.8 %copy-start.9 = (bf16[2,16,512]{2,1,0:T(8,128)(2,1)S(1)}, bf16[2,16,512]{2,1,0:T(8,128)(2,1)}, u32[]{:S(2)}) copy-start(bf16[2,16,512]{2,1,0:T(8,128)(2,1)} %get-tuple-element.36.refs_0_) | copy-start | bytes 98308
  17.1 1.8 %copy-start.10 = (bf16[2,4,512]{2,1,0:T(4,128)(2,1)S(1)}, bf16[2,4,512]{2,1,0:T(4,128)(2,1)}, u32[]{:S(2)}) copy-start(bf16[2,4,512]{2,1,0:T(4,128)(2,1)} %get-tuple-element.37.refs_1_) | copy-start | bytes 24580
  17.1 3.1 %copy-start.4 = (bf16[1024,512]{1,0:T(8,128)(2,1)S(1)}, bf16[1024,512]{1,0:T(8,128)(2,1)}, u32[]{:S(2)}) copy-start(bf16[1024,512]{1,0:T(8,128)(2,1)} %g.17) | copy-start | bytes 3145732
  18.9 4.1 %collective-permute-start.3 = (bf16[1,2,24,512]{3,2,1,0:T(8,128)(2,1)S(1)}, bf16[1,2,24,512]{3,2,1,0:T(8,128)(2,1)S(1)}, u32[]{:S(2)}, u32[]{:S(2)}) collective-permute-start(bf16[1,2,24,512]{3,2,1,0:T(8,128)(2,1)S(1)} %bitcast.3), channel_id=1, source_target_pairs={{0,4},{2,6},{4,0},{6,2},{8,12},{10,14},{12,8},{14,10},{16,20},{18,... | collective-permute-start | bytes 147464 | tf_op jit(solution)/shard_map/ppermute | solution.py:483
  23.1 3.5 %collective-permute-start.4 = (bf16[2,2,24,512]{3,2,1,0:T(8,128)(2,1)S(1)}, bf16[2,2,24,512]{3,2,1,0:T(8,128)(2,1)S(1)}, u32[]{:S(2)}, u32[]{:S(2)}) collective-permute-start(bf16[2,2,24,512]{3,2,1,0:T(8,128)(2,1)S(1)} %join.4.refs_0_), channel_id=1, source_target_pairs={{0,8},{2,10},{4,12},{6,14},{8,0},{10,2},{12,4},{14,6},{16,24},{18,... | collective-permute-start | bytes 294920 | tf_op jit(solution)/shard_map/ppermute | solution.py:483
  26.5 10.5 %collective-permute-start.5 = (bf16[4,2,24,512]{3,2,1,0:T(8,128)(2,1)S(1)}, bf16[4,2,24,512]{3,2,1,0:T(8,128)(2,1)}, u32[]{:S(2)}, u32[]{:S(2)}) collective-permute-start(bf16[4,2,24,512]{3,2,1,0:T(8,128)(2,1)S(1)} %join.5.mine), channel_id=1, source_target_pairs={{0,2},{2,0},{4,6},{6,4},{8,10},{10,8},{12,14},{14,12},{16,18},{18,... | collective-permute-start | bytes 589832 | tf_op jit(solution)/shard_map/ppermute | solution.py:483
  34.0 1.2 %copy-start.5 = (bf16[1024,512]{1,0:T(8,128)(2,1)S(1)}, bf16[1024,512]{1,0:T(8,128)(2,1)}, u32[]{:S(2)}) copy-start(bf16[1024,512]{1,0:T(8,128)(2,1)} %g.17) | copy-start | bytes 3145732
  54.1 6.9 %collective-permute-start.6 = (bf16[2,96,512]{2,1,0:T(8,128)(2,1)S(1)}, bf16[2,96,512]{2,1,0:T(8,128)(2,1)S(1)}, u32[]{:S(2)}, u32[]{:S(2)}) collective-permute-start(bf16[2,96,512]{2,1,0:T(8,128)(2,1)S(1)} %get-tuple-element.53), channel_id=1, source_target_pairs={{0,2},{2,0},{4,6},{6,4},{8,10},{10,8},{12,14},{14,12},{16,18},{18,... | collective-permute-start | bytes 589832 | tf_op jit(solution)/shard_map/ppermute | solution.py:483
  54.2 28.1 %collective-permute-start.8 = (bf16[2,256,512]{2,1,0:T(8,128)(2,1)S(1)}, bf16[2,256,512]{2,1,0:T(8,128)(2,1)S(1)}, u32[]{:S(2)}, u32[]{:S(2)}) collective-permute-start(bf16[2,256,512]{2,1,0:T(8,128)(2,1)S(1)} %get-tuple-element.56), channel_id=1, source_target_pairs={{2,0},{4,2},{6,4},{8,6},{10,8},{12,10},{14,12},{16,14},{18,16},{20... | collective-permute-start | bytes 1572872 | tf_op jit(solution)/shard_map/ppermute | solution.py:487
  61.0 4.7 %copy-start.6 = (bf16[1024,512]{1,0:T(8,128)(2,1)S(1)}, bf16[1024,512]{1,0:T(8,128)(2,1)}, u32[]{:S(2)}) copy-start(bf16[1024,512]{1,0:T(8,128)(2,1)} %g.17) | copy-start | bytes 3145732
  61.0 21.3 %collective-permute-start.7 = (bf16[2,256,512]{2,1,0:T(8,128)(2,1)S(1)}, bf16[2,256,512]{2,1,0:T(8,128)(2,1)S(1)}, u32[]{:S(2)}, u32[]{:S(2)}) collective-permute-start(bf16[2,256,512]{2,1,0:T(8,128)(2,1)S(1)} %get-tuple-element.55), channel_id=1, source_target_pairs={{0,2},{2,4},{4,6},{6,8},{8,10},{10,12},{12,14},{14,16},{16,18},{18... | collective-permute-start | bytes 1572872 | tf_op jit(solution)/shard_map/ppermute | solution.py:487
  64.3 5.6 %collective-permute-start.9 = (bf16[2,48,512]{2,1,0:T(8,128)(2,1)S(1)}, bf16[2,48,512]{2,1,0:T(8,128)(2,1)S(1)}, u32[]{:S(2)}, u32[]{:S(2)}) collective-permute-start(bf16[2,48,512]{2,1,0:T(8,128)(2,1)S(1)} %get-tuple-element.58), channel_id=1, source_target_pairs={{0,8},{2,10},{4,12},{6,14},{8,0},{10,2},{12,4},{14,6},{16,24},{18,... | collective-permute-start | bytes 294920 | tf_op jit(solution)/shard_map/ppermute | solution.py:483
  70.0 8.0 %collective-permute-start.10 = (bf16[2,24,512]{2,1,0:T(8,128)(2,1)S(1)}, bf16[2,24,512]{2,1,0:T(8,128)(2,1)S(1)}, u32[]{:S(2)}, u32[]{:S(2)}) collective-permute-start(bf16[2,24,512]{2,1,0:T(8,128)(2,1)S(1)} %get-tuple-element.60), channel_id=1, source_target_pairs={{0,4},{2,6},{4,0},{6,2},{8,12},{10,14},{12,8},{14,10},{16,20},{18,... | collective-permute-start | bytes 147464 | tf_op jit(solution)/shard_map/ppermute | solution.py:483
  78.0 4.3 %collective-permute-start.11 = (bf16[2,4,512]{2,1,0:T(4,128)(2,1)S(1)}, bf16[2,4,512]{2,1,0:T(4,128)(2,1)S(1)}, u32[]{:S(2)}, u32[]{:S(2)}) collective-permute-start(bf16[2,4,512]{2,1,0:T(4,128)(2,1)S(1)} %get-tuple-element.62), channel_id=1, source_target_pairs={{0,16},{2,18},{4,20},{6,22},{8,24},{10,26},{12,28},{14,30},{16,0},... | collective-permute-start | bytes 24584 | tf_op jit(solution)/shard_map/ppermute | solution.py:483
  78.1 4.3 %copy-start.7 = (f32[256,512]{1,0:T(8,128)S(1)}, f32[256,512]{1,0:T(8,128)}, u32[]{:S(2)}) copy-start(f32[256,512]{1,0:T(8,128)} %get-tuple-element.64.refs_13_) | copy-start | bytes 1572868
  78.1 4.3 %copy-start.8 = (f32[64,512]{1,0:T(8,128)S(1)}, f32[64,512]{1,0:T(8,128)}, u32[]{:S(2)}) copy-start(f32[64,512]{1,0:T(8,128)} %get-tuple-element.63.refs_12_) | copy-start | bytes 393220

commit v2 on v1

v2 whole, which is shorter than its diff:
```python
import functools
import math

import jax
import jax.numpy as jnp
from jax import lax
from jax.experimental import pallas as pl
from jax.experimental.pallas import tpu as pltpu
from jax.sharding import PartitionSpec as P


BLOCK = 256
SEG1 = 64
SEG2 = 256
GROUP = 8
NEG = -1e30
F32 = jnp.float32
BF16 = jnp.bfloat16
NT = (((1,), (1,)), ((), ()))
NN = (((1,), (0,)), ((), ()))
VMEM_LIMIT = 32 * 2**20
VMEM_ALL = 60 * 2**20
ANY = pl.BlockSpec(memory_space=pl.ANY)


def dot(a, b, dims):
    return lax.dot_general(a, b, dims, preferred_element_type=F32)


def struct(shape, dtype):
    return jax.ShapeDtypeStruct(shape, dtype)


def call(body, flops=0, moved=0, vmem=VMEM_LIMIT, **kwargs):
    cost = pl.CostEstimate(flops=int(flops), bytes_accessed=int(moved), transcendentals=0)
    params = pltpu.CompilerParams(vmem_limit_bytes=vmem)
    return pl.pallas_call(body, cost_estimate=cost, compiler_params=params, **kwargs)


def head_masks(width, depth):
    lane = lax.broadcasted_iota(jnp.int32, (1, width), 1)
    return [(lane >= h * depth) & (lane < (h + 1) * depth) for h in range(width // depth)]


def keep_head(rows, mask, scale=None):
    rows = jnp.where(mask, rows, 0)
    if scale is not None:
        rows = rows.astype(F32) * scale
    return rows.astype(BF16)


def near(block, blocks):
    return range(max(block - 1, 0), min(block + 2, blocks))


def pool_body(
    depth, ends, k, v, group_pool, whole_pool, groups, wholes, inner, outer, wide_group, wide_whole
):
    rows, width = k.shape
    heads = group_pool.shape[0]
    start = pl.program_id(0) * width
    head = lax.broadcasted_iota(jnp.int32, (heads, width), 0)
    col = lax.broadcasted_iota(jnp.int32, (heads, width), 1) + start
    pick = ((col >= head * depth) & (col < (head + 1) * depth)).astype(F32)
    for src, dst in ((group_pool, wide_group), (whole_pool, wide_whole)):
        dst[...] = lax.dot_general(
            src[...],
            pick,
            (((0,), (0,)), ((), ())),
            precision=lax.Precision.HIGHEST,
            preferred_element_type=F32,
        )
    odd = ends[2]
    low = pl.multiple_of(odd * (rows - BLOCK), BLOCK)
    high = pl.multiple_of((1 - odd) * (rows - BLOCK), BLOCK)
    for n, src in enumerate((k, v)):
        inner[n] = src[pl.ds(high, BLOCK)]
        outer[n] = src[pl.ds(low, BLOCK)]
        for segment, wide, dst in ((SEG1, wide_group, groups), (SEG2, wide_whole, wholes)):
            sums = []
            for s in range(rows // segment):
                part = src[s * segment : (s + 1) * segment].astype(F32) * wide[...]
                sums.append(jnp.sum(part, axis=0, keepdims=True))
            dst[n] = jnp.concatenate(sums, axis=0).astype(BF16)


def pool(k, v, group_pool, whole_pool, ends, width):
    rows, cols = k.shape
    heads = group_pool.shape[0]
    count1, count2 = rows // SEG1, rows // SEG2
    column = lambda n: pl.BlockSpec((n, width), lambda i, *_: (0, i))
    both = lambda n: pl.BlockSpec((2, n, width), lambda i, *_: (0, 0, i))
    full = lambda x: pl.BlockSpec(x.shape, lambda i, *_: (0, 0))
    return call(
        functools.partial(pool_body, cols // heads),
        moved=k.size * 6,
        vmem=VMEM_ALL,
        grid_spec=pltpu.PrefetchScalarGridSpec(
            num_scalar_prefetch=1,
            grid=(cols // width,),
            in_specs=[column(rows), column(rows), full(group_pool), full(whole_pool)],
            out_specs=[both(count1), both(count2), both(BLOCK), both(BLOCK)]
            + [column(SEG1), column(SEG2)],
        ),
        out_shape=[
            struct((2, count1, cols), BF16),
            struct((2, count2, cols), BF16),
            struct((2, BLOCK, cols), BF16),
            struct((2, BLOCK, cols), BF16),
            struct((SEG1, cols), F32),
            struct((SEG2, cols), F32),
        ],
    )(ends, k, v, group_pool, whole_pool)


def join(slots, tokens=(), passed=()):
    flat, plan, count, rows = [], [], 0, 0
    for slot in slots:
        if isinstance(slot, list):
            plan.append((count, len(slot)))
            flat += slot
            rows = sum(part.shape[1] for part in slot)
            count += 1
        else:
            plan.append((count, 0))
            flat.append(slot)
            rows = slot.shape[2]
            count += slot.shape[0]
    cols = flat[0].shape[-1]
    extra = list(passed) + list(tokens)

    def body(*refs):
        out = refs[len(flat) + len(extra)]
        at = 0
        for start, parts in plan:
            if not parts:
                out[start : start + refs[at].shape[0]] = refs[at][...]
                at += 1
                continue
            for n in range(2):
                pieces = [refs[at + i][n].astype(F32) for i in range(parts)]
                out[start, n] = jnp.concatenate(pieces, axis=0).astype(BF16)
            at += parts

    vmem = pl.BlockSpec(memory_space=pltpu.VMEM)
    return call(
        body,
        moved=4 * count * 2 * rows * cols,
        in_specs=[vmem] * len(flat) + [ANY] * len(extra),
        out_specs=[vmem] + [ANY] * len(passed),
        out_shape=[struct((count, 2, rows, cols), BF16)]
        + [struct(x.shape, x.dtype) for x in passed],
        input_output_aliases={len(flat) + n: 1 + n for n in range(len(passed))},
    )(*flat, *extra)


def merge(state, s_all, d_all, chunk=64):
    for c in range(0, s_all.shape[0], chunk):
        s = s_all[c : c + chunk]
        count = s.shape[0] // 8
        s = s.reshape(count, 8, s.shape[1])
        d = d_all[c : c + chunk].reshape(s.shape)
        here = jnp.max(s, axis=0)
        top = here if state is None else jnp.maximum(state[0], here)
        e = jnp.exp(s - top[None])
        total = jnp.sum(e, axis=0)
        inner = jnp.sum(e * d, axis=0)
        if state is not None:
            fade = jnp.exp(state[0] - top)
            total = total + state[1] * fade
            inner = inner + state[2] * fade
        state = (top, total, inner)
    return state


def stats_body(depth, scale, q, k, v, g, out):
    rows, width = q.shape
    blocks = rows // BLOCK
    for h, mask in enumerate(head_masks(width, depth)):
        for b in range(blocks):
            r = slice(b * BLOCK, (b + 1) * BLOCK)
            qs = keep_head(q[r], mask, scale)
            gs = keep_head(g[r], mask)
            c = slice(near(b, blocks)[0] * BLOCK, (near(b, blocks)[-1] + 1) * BLOCK)
            top, total, inner = merge(None, dot(k[c], qs, NT), dot(v[c], gs, NT))
            most = jnp.max(top, axis=0, keepdims=True)
            fade = jnp.exp(top - most)
            out[0, h : h + 1, r] = most
            out[1, h : h + 1, r] = jnp.sum(total * fade, axis=0, keepdims=True)
            out[2, h : h + 1, r] = jnp.sum(inner * fade, axis=0, keepdims=True)


def stats(q, k, v, g, width, depth, scale, pair):
    rows = q.shape[0]
    hp = width // depth
    cols = pl.BlockSpec((rows, width), lambda i: (0, pair))
    return call(
        functools.partial(stats_body, depth, scale),
        flops=2 * 2 * 3 * BLOCK * rows * width,
        moved=rows * width * 8,
        grid=(1,),
        in_specs=[cols] * 4,
        out_specs=pl.BlockSpec((3, hp, rows), lambda i: (0, 0, 0)),
        out_shape=struct((3, hp, rows), F32),
    )(q, k, v, g)


def remote_body(depth, scale, pairs, ends, q, g, inner, outer, mine, theirs, *rest):
    partial = rest[:pairs]
    kept, sent, inner_d, outer_d, dq_t, final = rest[pairs : pairs + 6]
    far_k, far_v, far_kt, near_t, far_dk, far_dv, near_d, qs, gs, s_all, d_all = rest[pairs + 6 :]
    rows, width = q.shape
    blocks = rows // BLOCK
    slots, _, per, _ = mine.shape
    half = slots * per
    pair = pl.program_id(0)
    masks = head_masks(width, depth)
    for n, far in enumerate((far_k, far_v)):
        for m, src in enumerate((mine, theirs)):
            for s in range(slots):
                at = m * half + s * per
                far[at : at + per] = src[s, n]
    far_kt[...] = (far_k[...].astype(F32) * scale).astype(BF16).T
    near_t[0] = (inner[0].astype(F32) * scale).astype(BF16).T
    near_t[1] = (outer[0].astype(F32) * scale).astype(BF16).T
    scaled = (q[...].astype(F32) * scale).astype(BF16)
    for h, mask in enumerate(masks):
        qs[h] = jnp.where(mask, scaled, 0).astype(BF16)
        gs[h] = jnp.where(mask, g[...], 0).astype(BF16)
    odd = ends[2]
    missing = jnp.where((ends[0] == 1) | (ends[1] == 1), NEG, 0.0)
    first = (1 - odd) * (blocks - 1)
    last = odd * (blocks - 1)
    middle = list(range(1, blocks - 1))
    order = [first, last] + middle if blocks > 1 else [0]

    def place(n):
        return pl.ds(pl.multiple_of(order[n] * BLOCK, BLOCK), BLOCK)

    def sets(n):
        out = [(0, far_k, far_v, None, far_kt, far_dk, far_dv)]
        if n == 0:
            out.append(
                (2 * half, inner.at[0], inner.at[1], None, near_t.at[0], near_d.at[0], near_d.at[1])
            )
        if n == (1 if blocks > 1 else 0):
            out.append(
                (
                    2 * half + BLOCK,
                    outer.at[0],
                    outer.at[1],
                    missing,
                    near_t.at[1],
                    near_d.at[2],
                    near_d.at[3],
                )
            )
        return out

    for h in range(len(masks)):
        for b in range(blocks):
            r = place(b)
            old = [partial[0][m, h : h + 1, r] for m in range(3)]
            for n in range(1, pairs):
                old = [
                    jnp.where(pair == n, partial[n][m, h : h + 1, r], old[m]) for m in range(3)
                ]
            state = None
            for at, keys, vals, bias, *_ in sets(b):
                size = keys.shape[0]
                s = dot(keys[...], qs[h, r], NT)
                d = dot(vals[...], gs[h, r], NT)
                if bias is not None:
                    s = s + bias
                s_all[h * blocks + b, at : at + size] = s
                d_all[h * blocks + b, at : at + size] = d
                state = merge(state, s, d)
            top8, total8, inner8 = state
            top = jnp.maximum(old[0], jnp.max(top8, axis=0, keepdims=True))
            fade = jnp.exp(old[0] - top)
            fade8 = jnp.exp(top8 - top)
            total = old[1] * fade + jnp.sum(total8 * fade8, axis=0, keepdims=True)
            dots = old[2] * fade + jnp.sum(inner8 * fade8, axis=0, keepdims=True)
            final[0, h : h + 1, r] = top + jnp.log(total)
            final[1, h : h + 1, r] = dots / total
    for h in range(len(masks)):
        hr = slice(h * depth, (h + 1) * depth)
        for b in range(blocks):
            r = place(b)
            lse = final[0, h : h + 1, r]
            delta = final[1, h : h + 1, r]
            dq = None
            for n, (at, keys, _, _, turned, dk, dv) in enumerate(sets(b)):
                size = keys.shape[0]
                p = jnp.exp(s_all[h * blocks + b, at : at + size] - lse)
                ds = (p * (d_all[h * blocks + b, at : at + size] - delta)).astype(BF16)
                v_part = dot(p.astype(BF16), gs[h, r], NN)
                k_part = dot(ds, qs[h, r], NN)
                if h == 0 and (n or b == 0):
                    dv[...] = v_part
                    dk[...] = k_part
                else:
                    dv[...] += v_part
                    dk[...] += k_part
                part = dot(turned[hr], ds, NN)
                dq = part if dq is None else dq + part
            dq_t[hr, r] = dq
    for n, far in enumerate((far_dk, far_dv)):
        kept[n] = far[:half]
        sent[n] = far[half:].astype(BF16)
        inner_d[n] = near_d[n].astype(BF16)
        outer_d[n] = near_d[2 + n].astype(BF16)


def remote(q, g, inner, outer, mine, theirs, partial, ends, width, depth, scale):
    rows, cols = q.shape
    pairs = cols // width
    hp = width // depth
    slots, _, per, _ = mine.shape
    half = slots * per
    far = 2 * half
    wide = lambda n: pl.BlockSpec((n, width), lambda i, *_: (0, i))
    both = lambda n: pl.BlockSpec((2, n, width), lambda i, *_: (0, 0, i))
    slot = pl.BlockSpec((slots, 2, per, width), lambda i, *_: (0, 0, 0, i))
    fixed = pl.BlockSpec((3, hp, rows), lambda i, *_: (0, 0, 0))
    held = pltpu.VMEM((hp * rows // BLOCK, far + 2 * BLOCK, BLOCK), F32)
    grid_spec = pltpu.PrefetchScalarGridSpec(
        num_scalar_prefetch=1,
        grid=(pairs,),
        in_specs=[wide(rows)] * 2 + [both(BLOCK)] * 2 + [slot] * 2 + [fixed] * pairs,
        out_specs=[
            both(half),
            both(half),
            both(BLOCK),
            both(BLOCK),
            pl.BlockSpec((width, rows), lambda i, *_: (i, 0)),
            pl.BlockSpec((None, 2, hp, rows), lambda i, *_: (i, 0, 0, 0)),
        ],
        scratch_shapes=[
            pltpu.VMEM((far, width), BF16),
            pltpu.VMEM((far, width), BF16),
            pltpu.VMEM((width, far), BF16),
            pltpu.VMEM((2, width, BLOCK), BF16),
            pltpu.VMEM((far, width), F32),
            pltpu.VMEM((far, width), F32),
            pltpu.VMEM((4, BLOCK, width), F32),
            pltpu.VMEM((hp, rows, width), BF16),
            pltpu.VMEM((hp, rows, width), BF16),
            held,
            held,
        ],
    )
    return call(
        functools.partial(remote_body, depth, scale, pairs),
        flops=10 * (far * rows + 2 * BLOCK * BLOCK) * cols,
        moved=rows * cols * 8,
        grid_spec=grid_spec,
        out_shape=[
            struct((2, half, cols), F32),
            struct((2, half, cols), BF16),
            struct((2, BLOCK, cols), BF16),
            struct((2, BLOCK, cols), BF16),
            struct((cols, rows), F32),
            struct((pairs, 2, hp, rows), F32),
        ],
    )(ends, q, g, inner, outer, mine, theirs, *partial)


def local_body(depth, scale, chained, q, k, v, g, part, final, *rest):
    dq, dk, dv, k_t, dq_t = rest[chained:]
    rows, width = q.shape
    blocks = rows // BLOCK
    k_t[...] = (k[...].astype(F32) * scale).astype(BF16).T
    for h, mask in enumerate(head_masks(width, depth)):
        hr = slice(h * depth, (h + 1) * depth)
        for b in range(blocks):
            r = slice(b * BLOCK, (b + 1) * BLOCK)
            qs = keep_head(q[r], mask, scale)
            gs = keep_head(g[r], mask)
            reach = near(b, blocks)
            c = slice(reach[0] * BLOCK, (reach[-1] + 1) * BLOCK)
            p = jnp.exp(dot(k[c], qs, NT) - final[0, h : h + 1, r])
            ds = (p * (dot(v[c], gs, NT) - final[1, h : h + 1, r])).astype(BF16)
            v_part = dot(p.astype(BF16), gs, NN)
            k_part = dot(ds, qs, NN)
            for n, j in enumerate(reach):
                rj = slice(j * BLOCK, (j + 1) * BLOCK)
                here = slice(n * BLOCK, (n + 1) * BLOCK)
                if h == 0 and b == near(j, blocks)[0]:
                    dv[rj] = v_part[here]
                    dk[rj] = k_part[here]
                else:
                    dv[rj] += v_part[here]
                    dk[rj] += k_part[here]
            dq_t[hr, r] = part[hr, r] + dot(k_t[hr, c], ds, NN)
    dq[...] = dq_t[...].T.astype(BF16)


def local(q, k, v, g, part, final, before, width, depth, scale, pair):
    rows, cols = q.shape
    hp = width // depth
    column = pl.BlockSpec((rows, width), lambda i: (0, pair))
    alone = pl.BlockSpec((rows, width), lambda i: (0, 0))
    extra = [] if before is None else [before]
    return call(
        functools.partial(local_body, depth, scale, len(extra)),
        flops=10 * 3 * BLOCK * rows * width,
        moved=rows * width * 24,
        grid=(1,),
        in_specs=[column] * 4
        + [
            pl.BlockSpec((width, rows), lambda i: (pair, 0)),
            pl.BlockSpec((None, 2, hp, rows), lambda i: (pair, 0, 0, 0)),
        ]
        + [ANY] * len(extra),
        out_specs=[column, alone, alone],
        out_shape=[struct((rows, cols), BF16)] + [struct((rows, width), F32)] * 2,
        scratch_shapes=[pltpu.VMEM((width, rows), BF16), pltpu.VMEM((width, rows), F32)],
        input_output_aliases={6: 0} if extra else {},
    )(q, k, v, g, part, final, *extra)


def gathered(kept, got, n):
    rows = kept.shape[1]
    total = kept[n]
    for part in got:
        at = rows - part.shape[1]
        more = part[n].astype(F32)
        if at:
            more = jnp.concatenate([jnp.zeros((at, more.shape[1]), F32), more], axis=0)
        total = total + more
    return total


def fold(kept, got, cuts, tokens=(), passed=()):
    cols = kept.shape[-1]
    vmem = pl.BlockSpec(memory_space=pltpu.VMEM)
    extra = list(passed) + list(tokens)
    count = len(got)
    sizes = [b - a for a, b in zip(cuts, cuts[1:])]

    def body(kept, *rest):
        arrived = rest[:count]
        outs = rest[count + len(extra) :]
        for n in range(2):
            total = gathered(kept, arrived, n)
            outs[0][n] = total[: cuts[0]]
            for a, b, out in zip(cuts, cuts[1:], outs[1:]):
                out[n] = total[a:b].astype(BF16)

    return call(
        body,
        moved=kept.size * 8,
        in_specs=[vmem] * (1 + count) + [ANY] * len(extra),
        out_specs=[vmem] * len(cuts) + [ANY] * len(passed),
        out_shape=[struct((2, cuts[0], cols), F32)]
        + [struct((2, size, cols), BF16) for size in sizes]
        + [struct(x.shape, x.dtype) for x in passed],
        input_output_aliases={1 + count + n: len(cuts) + n for n in range(len(passed))},
    )(kept, *got, *extra)


def finish_body(pairs, ends, *refs):
    dk, dv = refs[:pairs], refs[pairs : 2 * pairs]
    from_inner, from_outer, wide_group, wide_whole, kept = refs[2 * pairs : 2 * pairs + 5]
    got, (out_k, out_v) = refs[2 * pairs + 5 : -2], refs[-2:]
    block = pl.program_id(0)
    blocks = pl.num_programs(0)
    width = dk[0].shape[1]
    per = BLOCK // SEG1
    rows = kept.shape[1]
    count1 = rows * SEG2 // (SEG1 + SEG2)
    odd = ends[2]
    from_in = jnp.where(block == (1 - odd) * (blocks - 1), 1.0, 0.0)
    from_out = jnp.where(block == odd * (blocks - 1), 1.0, 0.0)
    index = lax.broadcasted_iota(jnp.int32, (rows, 1), 0)
    for n, (src, dst) in enumerate(((dk, out_k), (dv, out_v))):
        sums = gathered(kept, got, n)
        whole = jnp.sum(jnp.where(index == count1 + block, sums, 0.0), axis=0, keepdims=True)
        for s in range(per):
            mine = jnp.where(index == block * per + s, sums, 0.0)
            group = jnp.sum(mine, axis=0, keepdims=True)
            c = slice(s * SEG1, (s + 1) * SEG1)
            piece = group * wide_group[...] + whole * wide_whole[c]
            piece = piece + from_in * from_inner[n, c].astype(F32)
            piece = piece + from_out * from_outer[n, c].astype(F32)
            for p in range(pairs):
                lanes = slice(p * width, (p + 1) * width)
                dst[c, lanes] = (piece[:, lanes] + src[p][c]).astype(BF16)


def finish(dk, dv, from_inner, from_outer, kept, got, wide_group, wide_whole, ends):
    rows, width = dk[0].shape
    pairs = len(dk)
    cols = width * pairs
    tile = pl.BlockSpec((BLOCK, cols), lambda i, *_: (i, 0))
    narrow = pl.BlockSpec((BLOCK, width), lambda i, *_: (i, 0))
    full = lambda x: pl.BlockSpec(x.shape, lambda i, *_: (0,) * x.ndim)
    fixed = [from_inner, from_outer, wide_group, wide_whole, kept] + list(got)
    return call(
        functools.partial(finish_body, pairs),
        moved=rows * cols * 12,
        grid_spec=pltpu.PrefetchScalarGridSpec(
            num_scalar_prefetch=1,
            grid=(rows // BLOCK,),
            in_specs=[narrow] * (2 * pairs) + [full(x) for x in fixed],
            out_specs=[tile, tile],
        ),
        out_shape=[struct((rows, cols), BF16)] * 2,
    )(ends, *dk, *dv, *fixed)


def shards(query, key, value, out_grad, pool_group, pool_global):
    rows, cols = query.shape
    heads = pool_group.shape[0]
    depth = cols // heads
    scale = 1.0 / math.sqrt(depth)
    width = 128 if cols % 128 == 0 and 128 % depth == 0 else cols
    pairs = cols // width
    devices = lax.axis_size("seq")
    position = lax.axis_index("seq")
    count1 = rows // SEG1
    group_bits = list(range(1, GROUP.bit_length() - 1))
    other_bits = list(range(GROUP.bit_length() - 1, devices.bit_length() - 1))

    def swap(array, *bits):
        mask = sum(1 << bit for bit in bits)
        return lax.ppermute(array, "seq", [(i, i ^ mask) for i in range(devices)])

    def cross(array):
        route = [(i, i + 1) for i in range(1, devices - 1, 2)]
        return lax.ppermute(array, "seq", route + [(b, a) for a, b in route])

    ends = jnp.stack([position == 0, position == devices - 1, position % 2 == 1])
    ends = ends.astype(jnp.int32)
    groups, wholes, inner, outer, wide_group, wide_whole = pool(
        key, value, pool_group, pool_global, ends, width
    )
    partial = [
        stats(query, key, value, out_grad, width, depth, scale, p) for p in range(pairs)
    ]
    waiting = list(partial)

    def token():
        return [waiting.pop(0)] if waiting else []

    for bit in other_bits[:-1]:
        got = swap(wholes, bit)
        wholes = join([[wholes, got]])[0][0]
    base, far_bit = group_bits[0], other_bits[-1:]
    (pair,) = join([[groups, wholes]])
    here, there = [groups, wholes], []
    there = [swap(pair[0], base)]
    for bit in far_bit:
        here.append(swap(wholes, bit))
        there.append(swap(wholes, base, bit))
    comb, outer, inner = join([here, there], token(), [outer, inner])
    for bit in group_bits[1:]:
        got = swap(comb, bit)
        (comb,) = join([comb, got], token())
    theirs = swap(comb, 0)
    outer = cross(outer)
    inner = swap(inner, 0)

    kept, sent, inner_d, outer_d, dq_t, final = remote(
        query, out_grad, inner, outer, comb, theirs, partial, ends, width, depth, scale
    )
    got = [swap(sent, 0)]

    query_grad, dk, dv = None, [], []

    def step():
        nonlocal query_grad
        if len(dk) == pairs:
            return []
        query_grad, a, b = local(
            query, key, value, out_grad, dq_t, final, query_grad, width, depth, scale, len(dk)
        )
        dk.append(a)
        dv.append(b)
        return [a]

    from_inner = from_outer = None
    for bit in reversed(group_bits[1:]):
        size = kept.shape[1]
        if from_outer is None:
            kept, sent, inner_d, outer_d = fold(
                kept, got, [size // 2, size], step(), [inner_d, outer_d]
            )
            got = [swap(sent, bit)]
            from_outer = cross(outer_d)
            from_inner = swap(inner_d, 0)
        else:
            kept, sent = fold(kept, got, [size // 2, size], step())
            got = [swap(sent, bit)]
    slot = kept.shape[1] // 2
    own = slot - (slot - count1) // 2 if far_bit else slot
    last = []
    while len(dk) < pairs - 1:
        last = step()
    if far_bit:
        kept, far_here, to_base, far_there = fold(kept, got, [own, slot, slot + own, 2 * slot], last)
        got = [swap(to_base, base), swap(far_here, far_bit[0]), swap(far_there, base, far_bit[0])]
    else:
        kept, to_base = fold(kept, got, [slot, 2 * slot], last)
        got = [swap(to_base, base)]
    for bit in reversed(other_bits[:-1]):
        size = kept.shape[1]
        cut = count1 + (size - count1) // 2
        kept, sent = fold(kept, got, [cut, size])
        got = [swap(sent, bit)]
    while len(dk) < pairs:
        step()
    key_grad, value_grad = finish(
        dk, dv, from_inner, from_outer, kept, got, wide_group, wide_whole, ends
    )
    return (query_grad, key_grad, value_grad)


def solution(mesh):
    rows = P("seq", "head")
    in_specs = (rows, rows, rows, rows, P("head", None), P("head", None))
    return jax.shard_map(
        shards, mesh=mesh, in_specs=in_specs, out_specs=(rows, rows, rows), check_vma=False
    )
```

time: 85.6 us -> 78.8 us (0.921)
  starting transfers between devices: 30.1 us -> 25.7 us
  Pallas kernels: 50.3 us -> 46.4 us
    ppermute x12 -> x14, starting transfers between devices: 30.1 us -> 25.7 us  [the longest x12 20.4 us: swap(): return lax.ppermute(array, 'seq', [(i, i ^ mask) for i in range(devices)])]
    pallas_call x18 -> x16, Pallas kernels: 50.3 us -> 46.4 us  [the longest x4 16.9 us: local(): call(functools.partial(local_body, depth, scale, len(extra)), flops=10 *...]
    unnamed x22 -> x26, local copies, waits for them, and re-layouts: 2.48 us -> 3.25 us
  transfers between devices with their start and end apart: 12 -> 14, of which waited for: 2 -> 1; matrix products, arithmetic and copies ran while one was open for 0% -> 0% of each run, Pallas kernels for 33% -> 31%
where the time goes in v2:
time: 78.8 us; the launch traced here: 78.2 us
  Pallas kernels  46.4 us (59%)
  starting transfers between devices  25.7 us (33%)
  local copies, waits for them, and re-layouts  3.25 us (4%)
  waiting for transfers between devices  1.38 us (2%)
  between operations  0.85 us (1%)
    ppermute x12, starting transfers between devices, swap(): return lax.ppermute(array, 'seq', [(i, i ^ mask) for i in range(devices)])  20.4 us
    pallas_call x4, Pallas kernels, local(): call(functools.partial(local_body, depth, scale, len(extra)), flops=10 *...  16.9 us
    pallas_call x1, Pallas kernels, remote(): call(functools.partial(remote_body, depth, scale, pairs), flops=10 * (far...  12.2 us
    pallas_call x4, Pallas kernels, stats(): call(functools.partial(stats_body, depth, scale), flops=2 * 2 * 3 * BLOCK...  7 us
    ppermute x2, starting transfers between devices, cross(): return lax.ppermute(array, 'seq', route + [(b, a) for a, b in route])  5.36 us
    pallas_call x1, Pallas kernels, pool(): call(functools.partial(pool_body, cols // heads), moved=k.size * 6, vmem=...  5.25 us
    pallas_call x1, Pallas kernels, finish(): call(functools.partial(finish_body, pairs), moved=rows * cols * 12, grid_...  3.45 us
    unnamed x26, local copies, waits for them, and re-layouts  3.25 us
  transfers between devices with their start and end apart: 14, of which 1 were waited for; matrix products, arithmetic and copies ran while one was open for 0% of the time, Pallas kernels for 31%

profile of v2, /device:TPU:1, one launch (start us, length us, event | category | flops | bytes accessed | tf_op | source)
XLA Modules:
  0.0 78.2 jit_solution(15992058958575727761)
XLA Ops:
  0.6 0.0 copy-start
  0.7 0.6 add_convert_fusion.ends
  1.2 5.2 %shard_map.85 = (bf16[2,16,512]{2,1,0:T(8,128)(2,1)}, bf16[2,4,512]{2,1,0:T(4,128)(2,1)}, bf16[2,256,512]{2,1,0:T(8,128)(2,1)}, bf16[2,256,512]{2,1,0:T(8,128)(2...) custom-call(s32[3]{0:T(128)} %add_convert_fusion.ends, bf16[1024,512]{1,0:T(8,128)(2,1)} %k.17, bf16[1024,512]{1,0:T(8,128)(2,1)} %v.17, ...), custom_call_target="tpu_custom_call" | custom-call | bytes 3145728 | tf_op jit(solution)/shard_map/pallas_call | solution.py:94
  6.5 0.8 copy-done.10
  7.3 0.7 shard_map.86
  8.0 2.1 %collective-permute-start.1 = (bf16[2,20,512]{2,1,0:T(8,128)(2,1)S(1)}, bf16[2,20,512]{2,1,0:T(8,128)(2,1)S(1)}, u32[]{:S(2)}, u32[]{:S(2)}) collective-permute-start(bf16[2,20,512]{2,1,0:T(8,128)(2,1)S(1)} %bitcast.4), channel_id=1, source_target_pairs={{0,4},{2,6},{4,0},{6,2},{8,12},{10,14},{12,8},{14,10},{16,20},{18,... | collective-permute-start | bytes 122888 | tf_op jit(solution)/shard_map/ppermute | solution.py:528
  10.0 2.3 %collective-permute-start.2 = (bf16[2,4,512]{2,1,0:T(4,128)(2,1)}, bf16[2,4,512]{2,1,0:T(4,128)(2,1)S(1)}, u32[]{:S(2)}, u32[]{:S(2)}) collective-permute-start(bf16[2,4,512]{2,1,0:T(4,128)(2,1)} %get-tuple-element.41.refs_1_), channel_id=1, source_target_pairs={{0,20},{2,22},{4,16},{6,18},{8,28},{10,30},{12,24},{14,26},{16,4},... | collective-permute-start | bytes 24584 | tf_op jit(solution)/shard_map/ppermute | solution.py:528
  12.3 0.1 collective-permute-start
  12.3 1.2 %copy-done.2 = bf16[1024,512]{1,0:T(8,128)(2,1)S(1)} copy-done((bf16[1024,512]{1,0:T(8,128)(2,1)S(1)}, bf16[1024,512]{1,0:T(8,128)(2,1)}, u32[]{:S(2)}) %copy-start.2) | copy-done | bytes 1048600
  13.6 1.2 %copy-done.4 = bf16[1024,512]{1,0:T(8,128)(2,1)S(1)} copy-done((bf16[1024,512]{1,0:T(8,128)(2,1)S(1)}, bf16[1024,512]{1,0:T(8,128)(2,1)}, u32[]{:S(2)}) %copy-start.4) | copy-done | bytes 1048600
  14.8 1.7 %shard_map.87.refs_7_.rest_0_ = f32[3,2,1024]{2,1,0:T(2,128)S(1)} custom-call(bf16[1024,512]{1,0:T(8,128)(2,1)S(1)} %copy-done.2, bf16[1024,512]{1,0:T(8,128)(2,1)S(1)} %copy-done, bf16[1024,512]{1,0:T(8,128)(2,1)S(1)} %copy-done.1, bf16[1024,512]{1,0:T(8,128)(2,1)S(1)} %copy-done.4), custom_call_target="tpu_custom_call" | custom-call | flops 402653184 | bytes 1048576 | tf_op jit(solution)/shard_map/pallas_call | solution.py:197
  16.6 0.7 shard_map.88
  17.3 1.7 %collective-permute-start.3 = (bf16[2,256,512]{2,1,0:T(8,128)(2,1)S(1)}, bf16[2,256,512]{2,1,0:T(8,128)(2,1)S(1)}, u32[]{:S(2)}, u32[]{:S(2)}) collective-permute-start(bf16[2,256,512]{2,1,0:T(8,128)(2,1)S(1)} %get-tuple-element.44), channel_id=1, source_target_pairs={{0,2},{2,0},{4,6},{6,4},{8,10},{10,8},{12,14},{14,12},{16,18},{18,... | collective-permute-start | bytes 1572872 | tf_op jit(solution)/shard_map/ppermute | solution.py:528
  19.1 3.2 %collective-permute-start.4 = (bf16[2,256,512]{2,1,0:T(8,128)(2,1)S(1)}, bf16[2,256,512]{2,1,0:T(8,128)(2,1)S(1)}, u32[]{:S(2)}, u32[]{:S(2)}) collective-permute-start(bf16[2,256,512]{2,1,0:T(8,128)(2,1)S(1)} %get-tuple-element.45), channel_id=1, source_target_pairs={{2,4},{6,8},{10,12},{14,16},{18,20},{22,24},{26,28},{4,2},{8,6},{1... | collective-permute-start | bytes 1572872 | tf_op jit(solution)/shard_map/ppermute | solution.py:532
  22.3 1.4 %collective-permute-start.5 = (bf16[2,2,24,512]{3,2,1,0:T(8,128)(2,1)S(1)}, bf16[2,2,24,512]{3,2,1,0:T(8,128)(2,1)S(1)}, u32[]{:S(2)}, u32[]{:S(2)}) collective-permute-start(bf16[2,2,24,512]{3,2,1,0:T(8,128)(2,1)S(1)} %get-tuple-element.46.refs_0_), channel_id=1, source_target_pairs={{0,8},{2,10},{4,12},{6,14},{8,0},{10,2},{12,4},{14,6},{16,24},{18,... | collective-permute-start | bytes 294920 | tf_op jit(solution)/shard_map/ppermute | solution.py:528
  23.7 1.8 %shard_map.89.refs_2_.rest_1_ = f32[3,2,1024]{2,1,0:T(2,128)S(1)} custom-call(bf16[1024,512]{1,0:T(8,128)(2,1)S(1)} %copy-done.3, bf16[1024,512]{1,0:T(8,128)(2,1)S(1)} %copy-done, bf16[1024,512]{1,0:T(8,128)(2,1)S(1)} %copy-done.1, bf16[1024,512]{1,0:T(8,128)(2,1)S(1)} %copy-done.5), custom_call_target="tpu_custom_call" | custom-call | flops 402653184 | bytes 1048576 | tf_op jit(solution)/shard_map/pallas_call | solution.py:197
  25.4 1.4 %collective-permute-done.5.refs_1_ = bf16[2,2,24,512]{3,2,1,0:T(8,128)(2,1)S(1)} collective-permute-done((bf16[2,2,24,512]{3,2,1,0:T(8,128)(2,1)S(1)}, bf16[2,2,24,512]{3,2,1,0:T(8,128)(2,1)S(1)}, u32[]{:S(2)}, u32[]{:S(2)}) %collective-permute-start.5) | collective-permute-done | bytes 98336 | tf_op jit(solution)/shard_map/ppermute | solution.py:528
  26.8 6.5 %collective-permute-start.6 = (bf16[4,2,24,512]{3,2,1,0:T(8,128)(2,1)S(1)}, bf16[4,2,24,512]{3,2,1,0:T(8,128)(2,1)S(1)}, u32[]{:S(2)}, u32[]{:S(2)}) collective-permute-start(bf16[4,2,24,512]{3,2,1,0:T(8,128)(2,1)S(1)} %shard_map.90.mine), channel_id=1, source_target_pairs={{0,2},{2,0},{4,6},{6,4},{8,10},{10,8},{12,14},{14,12},{16,18},{18,... | collective-permute-start | bytes 589832 | tf_op jit(solution)/shard_map/ppermute | solution.py:528
  33.3 1.8 %shard_map.92.rest_3_ = f32[3,2,1024]{2,1,0:T(2,128)S(1)} custom-call(bf16[1024,512]{1,0:T(8,128)(2,1)S(1)} %copy-done.3, bf16[1024,512]{1,0:T(8,128)(2,1)S(1)} %copy-done, bf16[1024,512]{1,0:T(8,128)(2,1)S(1)} %copy-done.1, bf16[1024,512]{1,0:T(8,128)(2,1)S(1)} %copy-done.5), custom_call_target="tpu_custom_call" | custom-call | flops 402653184 | bytes 1048576 | tf_op jit(solution)/shard_map/pallas_call | solution.py:197
  35.1 1.8 %shard_map.91.rest_2_ = f32[3,2,1024]{2,1,0:T(2,128)S(1)} custom-call(bf16[1024,512]{1,0:T(8,128)(2,1)S(1)} %copy-done.3, bf16[1024,512]{1,0:T(8,128)(2,1)S(1)} %copy-done, bf16[1024,512]{1,0:T(8,128)(2,1)S(1)} %copy-done.1, bf16[1024,512]{1,0:T(8,128)(2,1)S(1)} %copy-done.5), custom_call_target="tpu_custom_call" | custom-call | flops 402653184 | bytes 1048576 | tf_op jit(solution)/shard_map/pallas_call | solution.py:197
  36.9 12.2 %shard_map.93 = (f32[2,96,512]{2,1,0:T(8,128)S(1)}, bf16[2,96,512]{2,1,0:T(8,128)(2,1)S(1)}, bf16[2,256,512]{2,1,0:T(8,128)(2,1)S(1)}, bf16[2,256,512]{2,1,0:T(8...) custom-call(s32[3]{0:T(128)S(1)} %copy-done.12, bf16[1024,512]{1,0:T(8,128)(2,1)S(1)} %copy-done.3, ...), custom_call_target="tpu_custom_call" | custom-call | flops 1677721600 | bytes 4194304 | tf_op jit(solution)/shard_map/pallas_call | solution.py:353
  49.1 0.1 collective-permute-start.7
  49.2 4.2 %shard_map.94 = (bf16[1024,512]{1,0:T(8,128)(2,1)}, f32[1024,128]{1,0:T(8,128)S(1)}, f32[1024,128]{1,0:T(8,128)S(1)}) custom-call(bf16[1024,512]{1,0:T(8,128)(2,1)S(1)} %copy-done.3, bf16[1024,512]{1,0:T(8,128)(2,1)S(1)} %copy-done, bf16[1024,512]{1,0:T(8,128)(2,1)S(1)} %copy-done.1, bf16[1024,512]{1,0:T(8,128)(2,1)S(1)} %copy-done.5, ...), custom_call_target="tpu_custom_call" | custom-call | flops 1006632960 | bytes 3145728 | tf_op jit(solution)/shard_map/pallas_call | solution.py:405
  53.5 0.6 collective-permute-start.8
  54.1 2.1 %collective-permute-start.9 = (bf16[2,256,512]{2,1,0:T(8,128)(2,1)S(1)}, bf16[2,256,512]{2,1,0:T(8,128)(2,1)S(1)}, u32[]{:S(2)}, u32[]{:S(2)}) collective-permute-start(bf16[2,256,512]{2,1,0:T(8,128)(2,1)S(1)} %get-tuple-element.66), channel_id=1, source_target_pairs={{2,4},{6,8},{10,12},{14,16},{18,20},{22,24},{26,28},{4,2},{8,6},{1... | collective-permute-start | bytes 1572872 | tf_op jit(solution)/shard_map/ppermute | solution.py:532
  56.2 1.0 %collective-permute-start.10 = (bf16[2,48,512]{2,1,0:T(8,128)(2,1)S(1)}, bf16[2,48,512]{2,1,0:T(8,128)(2,1)S(1)}, u32[]{:S(2)}, u32[]{:S(2)}) collective-permute-start(bf16[2,48,512]{2,1,0:T(8,128)(2,1)S(1)} %get-tuple-element.70), channel_id=1, source_target_pairs={{0,8},{2,10},{4,12},{6,14},{8,0},{10,2},{12,4},{14,6},{16,24},{18,... | collective-permute-start | bytes 294920 | tf_op jit(solution)/shard_map/ppermute | solution.py:528
  57.2 4.2 %shard_map.95 = (bf16[1024,512]{1,0:T(8,128)(2,1)}, f32[1024,128]{1,0:T(8,128)S(1)}, f32[1024,128]{1,0:T(8,128)S(1)}) custom-call(bf16[1024,512]{1,0:T(8,128)(2,1)S(1)} %copy-done.3, bf16[1024,512]{1,0:T(8,128)(2,1)S(1)} %copy-done, bf16[1024,512]{1,0:T(8,128)(2,1)S(1)} %copy-done.1, ...), custom_call_target="tpu_custom_call", output_to_operand_aliasing={{0}: (6, {})} | custom-call | flops 1006632960 | bytes 3145728 | tf_op jit(solution)/shard_map/pallas_call | solution.py:405
  61.5 4.2 %shard_map.96 = (bf16[1024,512]{1,0:T(8,128)(2,1)}, f32[1024,128]{1,0:T(8,128)S(1)}, f32[1024,128]{1,0:T(8,128)S(1)}) custom-call(bf16[1024,512]{1,0:T(8,128)(2,1)S(1)} %copy-done.3, bf16[1024,512]{1,0:T(8,128)(2,1)S(1)} %copy-done, bf16[1024,512]{1,0:T(8,128)(2,1)S(1)} %copy-done.1, ...), custom_call_target="tpu_custom_call", output_to_operand_aliasing={{0}: (6, {})} | custom-call | flops 1006632960 | bytes 3145728 | tf_op jit(solution)/shard_map/pallas_call | solution.py:405
  65.7 1.9 %collective-permute-start.12 = (bf16[2,4,512]{2,1,0:T(4,128)(2,1)S(1)}, bf16[2,4,512]{2,1,0:T(4,128)(2,1)S(1)}, u32[]{:S(2)}, u32[]{:S(2)}) collective-permute-start(bf16[2,4,512]{2,1,0:T(4,128)(2,1)S(1)} %get-tuple-element.73), channel_id=1, source_target_pairs={{0,16},{2,18},{4,20},{6,22},{8,24},{10,26},{12,28},{14,30},{16,0},... | collective-permute-start | bytes 24584 | tf_op jit(solution)/shard_map/ppermute | solution.py:528
  67.6 2.8 %collective-permute-start.13 = (bf16[2,4,512]{2,1,0:T(4,128)(2,1)S(1)}, bf16[2,4,512]{2,1,0:T(4,128)(2,1)S(1)}, u32[]{:S(2)}, u32[]{:S(2)}) collective-permute-start(bf16[2,4,512]{2,1,0:T(4,128)(2,1)S(1)} %get-tuple-element.74), channel_id=1, source_target_pairs={{0,20},{2,22},{4,16},{6,18},{8,28},{10,30},{12,24},{14,26},{16,4},... | collective-permute-start | bytes 24584 | tf_op jit(solution)/shard_map/ppermute | solution.py:528
  70.4 4.2 %shard_map.97 = (bf16[1024,512]{1,0:T(8,128)(2,1)}, f32[1024,128]{1,0:T(8,128)S(1)}, f32[1024,128]{1,0:T(8,128)S(1)}) custom-call(bf16[1024,512]{1,0:T(8,128)(2,1)S(1)} %copy-done.3, bf16[1024,512]{1,0:T(8,128)(2,1)S(1)} %copy-done, bf16[1024,512]{1,0:T(8,128)(2,1)S(1)} %copy-done.1, ...), custom_call_target="tpu_custom_call", output_to_operand_aliasing={{0}: (6, {})} | custom-call | flops 1006632960 | bytes 3145728 | tf_op jit(solution)/shard_map/pallas_call | solution.py:405
  74.7 3.5 %shard_map.100 = (bf16[1024,512]{1,0:T(8,128)(2,1)}, bf16[1024,512]{1,0:T(8,128)(2,1)}) custom-call(s32[3]{0:T(128)S(1)} %copy-done.12, f32[1024,128]{1,0:T(8,128)S(1)} %get-tuple-element.53.rest_3_.refs_0_, f32[1024,128]{1,0:T(8,128)S(1)} %get-tuple-element.54.refs_1_, f32[1024,128]{1,0:T(8,128)S(1)} %get-tuple-element.55.rest_1_.refs_2_, ...), custom_call_target="tpu_custom_call" | custom-call | bytes 6291456 | tf_op jit(solution)/shard_map/pallas_call | solution.py:500
  (39 shorter events, 0.2 us)
Async XLA Ops:
  0.6 11.7 %copy-start.1 = (bf16[1024,512]{1,0:T(8,128)(2,1)S(1)}, bf16[1024,512]{1,0:T(8,128)(2,1)}, u32[]{:S(2)}) copy-start(bf16[1024,512]{1,0:T(8,128)(2,1)} %v.17) | copy-start | bytes 3145732
  0.6 11.7 %copy-start = (bf16[1024,512]{1,0:T(8,128)(2,1)S(1)}, bf16[1024,512]{1,0:T(8,128)(2,1)}, u32[]{:S(2)}) copy-start(bf16[1024,512]{1,0:T(8,128)(2,1)} %k.17) | copy-start | bytes 3145732
  6.5 0.8 copy-start.10
  7.3 9.3 %copy-start.11 = (bf16[2,16,512]{2,1,0:T(8,128)(2,1)S(1)}, bf16[2,16,512]{2,1,0:T(8,128)(2,1)}, u32[]{:S(2)}) copy-start(bf16[2,16,512]{2,1,0:T(8,128)(2,1)} %get-tuple-element.40.refs_0_) | copy-start | bytes 98308
  8.0 8.6 %collective-permute-start.1 = (bf16[2,20,512]{2,1,0:T(8,128)(2,1)S(1)}, bf16[2,20,512]{2,1,0:T(8,128)(2,1)S(1)}, u32[]{:S(2)}, u32[]{:S(2)}) collective-permute-start(bf16[2,20,512]{2,1,0:T(8,128)(2,1)S(1)} %bitcast.4), channel_id=1, source_target_pairs={{0,4},{2,6},{4,0},{6,2},{8,12},{10,14},{12,8},{14,10},{16,20},{18,... | collective-permute-start | bytes 122888 | tf_op jit(solution)/shard_map/ppermute | solution.py:528
  10.0 6.5 %collective-permute-start.2 = (bf16[2,4,512]{2,1,0:T(4,128)(2,1)}, bf16[2,4,512]{2,1,0:T(4,128)(2,1)S(1)}, u32[]{:S(2)}, u32[]{:S(2)}) collective-permute-start(bf16[2,4,512]{2,1,0:T(4,128)(2,1)} %get-tuple-element.41.refs_1_), channel_id=1, source_target_pairs={{0,20},{2,22},{4,16},{6,18},{8,28},{10,30},{12,24},{14,26},{16,4},... | collective-permute-start | bytes 24584 | tf_op jit(solution)/shard_map/ppermute | solution.py:528
  12.3 4.3 %collective-permute-start = (bf16[2,4,512]{2,1,0:T(4,128)(2,1)}, bf16[2,4,512]{2,1,0:T(4,128)(2,1)S(1)}, u32[]{:S(2)}, u32[]{:S(2)}) collective-permute-start(bf16[2,4,512]{2,1,0:T(4,128)(2,1)} %get-tuple-element.41.refs_1_), channel_id=1, source_target_pairs={{0,16},{2,18},{4,20},{6,22},{8,24},{10,26},{12,28},{14,30},{16,0},... | collective-permute-start | bytes 24584 | tf_op jit(solution)/shard_map/ppermute | solution.py:528
  12.3 1.2 %copy-start.2 = (bf16[1024,512]{1,0:T(8,128)(2,1)S(1)}, bf16[1024,512]{1,0:T(8,128)(2,1)}, u32[]{:S(2)}) copy-start(bf16[1024,512]{1,0:T(8,128)(2,1)} %q.17) | copy-start | bytes 3145732
  13.6 1.2 %copy-start.4 = (bf16[1024,512]{1,0:T(8,128)(2,1)S(1)}, bf16[1024,512]{1,0:T(8,128)(2,1)}, u32[]{:S(2)}) copy-start(bf16[1024,512]{1,0:T(8,128)(2,1)} %g.17) | copy-start | bytes 3145732
  14.8 1.8 %copy-start.7 = (bf16[2,256,512]{2,1,0:T(8,128)(2,1)S(1)}, bf16[2,256,512]{2,1,0:T(8,128)(2,1)}, u32[]{:S(2)}) copy-start(bf16[2,256,512]{2,1,0:T(8,128)(2,1)} %get-tuple-element.43.refs_6_) | copy-start | bytes 1572868
  14.8 1.8 %copy-start.8 = (bf16[2,256,512]{2,1,0:T(8,128)(2,1)S(1)}, bf16[2,256,512]{2,1,0:T(8,128)(2,1)}, u32[]{:S(2)}) copy-start(bf16[2,256,512]{2,1,0:T(8,128)(2,1)} %get-tuple-element.42.refs_5_) | copy-start | bytes 1572868
  14.8 8.9 %copy-start.3 = (bf16[1024,512]{1,0:T(8,128)(2,1)S(1)}, bf16[1024,512]{1,0:T(8,128)(2,1)}, u32[]{:S(2)}) copy-start(bf16[1024,512]{1,0:T(8,128)(2,1)} %q.17) | copy-start | bytes 3145732
  14.8 8.9 %copy-start.5 = (bf16[1024,512]{1,0:T(8,128)(2,1)S(1)}, bf16[1024,512]{1,0:T(8,128)(2,1)}, u32[]{:S(2)}) copy-start(bf16[1024,512]{1,0:T(8,128)(2,1)} %g.17) | copy-start | bytes 3145732
  17.3 19.5 %collective-permute-start.3 = (bf16[2,256,512]{2,1,0:T(8,128)(2,1)S(1)}, bf16[2,256,512]{2,1,0:T(8,128)(2,1)S(1)}, u32[]{:S(2)}, u32[]{:S(2)}) collective-permute-start(bf16[2,256,512]{2,1,0:T(8,128)(2,1)S(1)} %get-tuple-element.44), channel_id=1, source_target_pairs={{0,2},{2,0},{4,6},{6,4},{8,10},{10,8},{12,14},{14,12},{16,18},{18,... | collective-permute-start | bytes 1572872 | tf_op jit(solution)/shard_map/ppermute | solution.py:528
  19.1 17.8 %collective-permute-start.4 = (bf16[2,256,512]{2,1,0:T(8,128)(2,1)S(1)}, bf16[2,256,512]{2,1,0:T(8,128)(2,1)S(1)}, u32[]{:S(2)}, u32[]{:S(2)}) collective-permute-start(bf16[2,256,512]{2,1,0:T(8,128)(2,1)S(1)} %get-tuple-element.45), channel_id=1, source_target_pairs={{2,4},{6,8},{10,12},{14,16},{18,20},{22,24},{26,28},{4,2},{8,6},{1... | collective-permute-start | bytes 1572872 | tf_op jit(solution)/shard_map/ppermute | solution.py:532
  22.3 4.5 %collective-permute-start.5 = (bf16[2,2,24,512]{3,2,1,0:T(8,128)(2,1)S(1)}, bf16[2,2,24,512]{3,2,1,0:T(8,128)(2,1)S(1)}, u32[]{:S(2)}, u32[]{:S(2)}) collective-permute-start(bf16[2,2,24,512]{3,2,1,0:T(8,128)(2,1)S(1)} %get-tuple-element.46.refs_0_), channel_id=1, source_target_pairs={{0,8},{2,10},{4,12},{6,14},{8,0},{10,2},{12,4},{14,6},{16,24},{18,... | collective-permute-start | bytes 294920 | tf_op jit(solution)/shard_map/ppermute | solution.py:528
  26.8 10.1 %collective-permute-start.6 = (bf16[4,2,24,512]{3,2,1,0:T(8,128)(2,1)S(1)}, bf16[4,2,24,512]{3,2,1,0:T(8,128)(2,1)S(1)}, u32[]{:S(2)}, u32[]{:S(2)}) collective-permute-start(bf16[4,2,24,512]{3,2,1,0:T(8,128)(2,1)S(1)} %shard_map.90.mine), channel_id=1, source_target_pairs={{0,2},{2,0},{4,6},{6,4},{8,10},{10,8},{12,14},{14,12},{16,18},{18,... | collective-permute-start | bytes 589832 | tf_op jit(solution)/shard_map/ppermute | solution.py:528
  35.1 1.8 %copy-start.12 = (s32[3]{0:T(128)S(1)}, s32[3]{0:T(128)}, u32[]{:S(2)}) copy-start(s32[3]{0:T(128)} %add_convert_fusion.ends) | copy-start | bytes 40
  49.1 4.3 %collective-permute-start.7 = (bf16[2,96,512]{2,1,0:T(8,128)(2,1)S(1)}, bf16[2,96,512]{2,1,0:T(8,128)(2,1)S(1)}, u32[]{:S(2)}, u32[]{:S(2)}) collective-permute-start(bf16[2,96,512]{2,1,0:T(8,128)(2,1)S(1)} %get-tuple-element.62), channel_id=1, source_target_pairs={{0,2},{2,0},{4,6},{6,4},{8,10},{10,8},{12,14},{14,12},{16,18},{18,... | collective-permute-start | bytes 589832 | tf_op jit(solution)/shard_map/ppermute | solution.py:528
  53.5 21.2 %collective-permute-start.8 = (bf16[2,256,512]{2,1,0:T(8,128)(2,1)S(1)}, bf16[2,256,512]{2,1,0:T(8,128)(2,1)S(1)}, u32[]{:S(2)}, u32[]{:S(2)}) collective-permute-start(bf16[2,256,512]{2,1,0:T(8,128)(2,1)S(1)} %get-tuple-element.65), channel_id=1, source_target_pairs={{0,2},{2,0},{4,6},{6,4},{8,10},{10,8},{12,14},{14,12},{16,18},{18,... | collective-permute-start | bytes 1572872 | tf_op jit(solution)/shard_map/ppermute | solution.py:528
  54.1 20.6 %collective-permute-start.9 = (bf16[2,256,512]{2,1,0:T(8,128)(2,1)S(1)}, bf16[2,256,512]{2,1,0:T(8,128)(2,1)S(1)}, u32[]{:S(2)}, u32[]{:S(2)}) collective-permute-start(bf16[2,256,512]{2,1,0:T(8,128)(2,1)S(1)} %get-tuple-element.66), channel_id=1, source_target_pairs={{2,4},{6,8},{10,12},{14,16},{18,20},{22,24},{26,28},{4,2},{8,6},{1... | collective-permute-start | bytes 1572872 | tf_op jit(solution)/shard_map/ppermute | solution.py:532
  56.2 9.5 %collective-permute-start.10 = (bf16[2,48,512]{2,1,0:T(8,128)(2,1)S(1)}, bf16[2,48,512]{2,1,0:T(8,128)(2,1)S(1)}, u32[]{:S(2)}, u32[]{:S(2)}) collective-permute-start(bf16[2,48,512]{2,1,0:T(8,128)(2,1)S(1)} %get-tuple-element.70), channel_id=1, source_target_pairs={{0,8},{2,10},{4,12},{6,14},{8,0},{10,2},{12,4},{14,6},{16,24},{18,... | collective-permute-start | bytes 294920 | tf_op jit(solution)/shard_map/ppermute | solution.py:528
  65.7 8.9 %collective-permute-start.12 = (bf16[2,4,512]{2,1,0:T(4,128)(2,1)S(1)}, bf16[2,4,512]{2,1,0:T(4,128)(2,1)S(1)}, u32[]{:S(2)}, u32[]{:S(2)}) collective-permute-start(bf16[2,4,512]{2,1,0:T(4,128)(2,1)S(1)} %get-tuple-element.73), channel_id=1, source_target_pairs={{0,16},{2,18},{4,20},{6,22},{8,24},{10,26},{12,28},{14,30},{16,0},... | collective-permute-start | bytes 24584 | tf_op jit(solution)/shard_map/ppermute | solution.py:528
  67.6 7.0 %collective-permute-start.13 = (bf16[2,4,512]{2,1,0:T(4,128)(2,1)S(1)}, bf16[2,4,512]{2,1,0:T(4,128)(2,1)S(1)}, u32[]{:S(2)}, u32[]{:S(2)}) collective-permute-start(bf16[2,4,512]{2,1,0:T(4,128)(2,1)S(1)} %get-tuple-element.74), channel_id=1, source_target_pairs={{0,20},{2,22},{4,16},{6,18},{8,28},{10,30},{12,24},{14,26},{16,4},... | collective-permute-start | bytes 24584 | tf_op jit(solution)/shard_map/ppermute | solution.py:528
  70.4 4.2 %collective-permute-start.11 = (bf16[2,20,512]{2,1,0:T(8,128)(2,1)S(1)}, bf16[2,20,512]{2,1,0:T(8,128)(2,1)S(1)}, u32[]{:S(2)}, u32[]{:S(2)}) collective-permute-start(bf16[2,20,512]{2,1,0:T(8,128)(2,1)S(1)} %get-tuple-element.72), channel_id=1, source_target_pairs={{0,4},{2,6},{4,0},{6,2},{8,12},{10,14},{12,8},{14,10},{16,20},{18,... | collective-permute-start | bytes 122888 | tf_op jit(solution)/shard_map/ppermute | solution.py:528
  70.4 4.3 %copy-start.6 = (f32[256,512]{1,0:T(8,128)S(1)}, f32[256,512]{1,0:T(8,128)}, u32[]{:S(2)}) copy-start(f32[256,512]{1,0:T(8,128)} %get-tuple-element.68.refs_11_) | copy-start | bytes 1572868
  70.4 4.3 %copy-start.9 = (f32[64,512]{1,0:T(8,128)S(1)}, f32[64,512]{1,0:T(8,128)}, u32[]{:S(2)}) copy-start(f32[64,512]{1,0:T(8,128)} %get-tuple-element.67.refs_10_) | copy-start | bytes 393220

commit v3 on v2

--- a/solution.py
+++ b/solution.py
@@ -19,7 +19,6 @@
 NT = (((1,), (1,)), ((), ()))
 NN = (((1,), (0,)), ((), ()))
 VMEM_LIMIT = 32 * 2**20
-VMEM_ALL = 60 * 2**20
 ANY = pl.BlockSpec(memory_space=pl.ANY)
 
 
@@ -53,64 +52,85 @@
     return range(max(block - 1, 0), min(block + 2, blocks))
 
 
-def pool_body(
-    depth, ends, k, v, group_pool, whole_pool, groups, wholes, inner, outer, wide_group, wide_whole
-):
-    rows, width = k.shape
-    heads = group_pool.shape[0]
-    start = pl.program_id(0) * width
-    head = lax.broadcasted_iota(jnp.int32, (heads, width), 0)
-    col = lax.broadcasted_iota(jnp.int32, (heads, width), 1) + start
-    pick = ((col >= head * depth) & (col < (head + 1) * depth)).astype(F32)
-    for src, dst in ((group_pool, wide_group), (whole_pool, wide_whole)):
-        dst[...] = lax.dot_general(
-            src[...],
-            pick,
-            (((0,), (0,)), ((), ())),
-            precision=lax.Precision.HIGHEST,
-            preferred_element_type=F32,
-        )
-    odd = ends[2]
+def is_odd():
+    return lax.rem(lax.axis_index("seq"), 2)
+
+
+def pool_body(depth, k, v, group_pool, whole_pool, groups, wholes, inner, outer, *rest):
+    *bufs, group_w, whole_w, sems = rest
+    rows, cols = bufs[0].shape
+    heads = group_w.shape[0]
+    chunks = rows // SEG2
+    copies = [
+        pltpu.make_async_copy(group_pool, group_w, sems.at[2 * chunks]),
+        pltpu.make_async_copy(whole_pool, whole_w, sems.at[2 * chunks + 1]),
+    ]
+    for c in range(chunks):
+        r = pl.ds(c * SEG2, SEG2)
+        for n, src in enumerate((k, v)):
+            copies.append(pltpu.make_async_copy(src.at[r], bufs[n].at[r], sems.at[2 * c + n]))
+    for copy in copies:
+        copy.start()
+    copies[0].wait()
+    copies[1].wait()
+    per = SEG2 // SEG1
+    lane = lax.broadcasted_iota(jnp.int32, (heads, SEG2), 1)
+    tiled = jnp.concatenate([group_w[...]] * per, axis=1)
+    weights = [
+        jnp.where((lane >= s * SEG1) & (lane < (s + 1) * SEG1), tiled, 0.0) for s in range(per)
+    ]
+    rest = jnp.concatenate(weights + [whole_w[...]], axis=0)
+    terms = []
+    for _ in range(3):
+        term = rest.astype(BF16)
+        terms.append(term)
+        rest = rest - term.astype(F32)
+    left = jnp.concatenate(terms, axis=0)
+    size = (per + 1) * heads
+    head = lax.broadcasted_iota(jnp.int32, (heads, cols), 0)
+    col = lax.broadcasted_iota(jnp.int32, (heads, cols), 1)
+    pick = (col >= head * depth) & (col < (head + 1) * depth)
+    sums = [([], []), ([], [])]
+    for c in range(chunks):
+        for n in range(2):
+            copies[2 + 2 * c + n].wait()
+            full = dot(left, bufs[n][c * SEG2 : (c + 1) * SEG2], NN)
+            full = full[:size] + full[size : 2 * size] + full[2 * size :]
+            for s in range(per + 1):
+                mine = jnp.where(pick, full[s * heads : (s + 1) * heads], 0.0)
+                sums[n][s == per].append(jnp.sum(mine, axis=0, keepdims=True))
+    odd = is_odd()
     low = pl.multiple_of(odd * (rows - BLOCK), BLOCK)
     high = pl.multiple_of((1 - odd) * (rows - BLOCK), BLOCK)
-    for n, src in enumerate((k, v)):
-        inner[n] = src[pl.ds(high, BLOCK)]
-        outer[n] = src[pl.ds(low, BLOCK)]
-        for segment, wide, dst in ((SEG1, wide_group, groups), (SEG2, wide_whole, wholes)):
-            sums = []
-            for s in range(rows // segment):
-                part = src[s * segment : (s + 1) * segment].astype(F32) * wide[...]
-                sums.append(jnp.sum(part, axis=0, keepdims=True))
-            dst[n] = jnp.concatenate(sums, axis=0).astype(BF16)
-
-
-def pool(k, v, group_pool, whole_pool, ends, width):
+    for n in range(2):
+        groups[n] = jnp.concatenate(sums[n][0], axis=0).astype(BF16)
+        wholes[n] = jnp.concatenate(sums[n][1], axis=0).astype(BF16)
+        inner[n] = bufs[n][pl.ds(high, BLOCK)]
+        outer[n] = bufs[n][pl.ds(low, BLOCK)]
+
+
+def pool(k, v, group_pool, whole_pool):
     rows, cols = k.shape
     heads = group_pool.shape[0]
     count1, count2 = rows // SEG1, rows // SEG2
-    column = lambda n: pl.BlockSpec((n, width), lambda i, *_: (0, i))
-    both = lambda n: pl.BlockSpec((2, n, width), lambda i, *_: (0, 0, i))
-    full = lambda x: pl.BlockSpec(x.shape, lambda i, *_: (0, 0))
+    shapes = [(2, count1, cols), (2, count2, cols), (2, BLOCK, cols), (2, BLOCK, cols)]
+    shapes += [k.shape, v.shape]
+    inputs = [
+        pltpu.with_memory_space_constraint(x, pltpu.HBM) for x in (k, v, group_pool, whole_pool)
+    ]
     return call(
         functools.partial(pool_body, cols // heads),
         moved=k.size * 6,
-        vmem=VMEM_ALL,
-        grid_spec=pltpu.PrefetchScalarGridSpec(
-            num_scalar_prefetch=1,
-            grid=(cols // width,),
-            in_specs=[column(rows), column(rows), full(group_pool), full(whole_pool)],
-            out_specs=[both(count1), both(count2), both(BLOCK), both(BLOCK)]
-            + [column(SEG1), column(SEG2)],
-        ),
-        out_shape=[
-            struct((2, count1, cols), BF16),
-            struct((2, count2, cols), BF16),
-            struct((2, BLOCK, cols), BF16),
-            struct((2, BLOCK, cols), BF16),
-            struct((SEG1, cols), F32),
-            struct((SEG2, cols), F32),
+        vmem=16 * 2**20,
+        in_specs=[pl.BlockSpec(memory_space=pltpu.HBM)] * 4,
+        out_specs=[pl.BlockSpec(memory_space=pltpu.VMEM)] * len(shapes),
+        out_shape=[struct(shape, BF16) for shape in shapes],
+        scratch_shapes=[
+            pltpu.VMEM(group_pool.shape, F32),
+            pltpu.VMEM(whole_pool.shape, F32),
+            pltpu.SemaphoreType.DMA((2 * count2 + 2,)),
         ],
-    )(ends, k, v, group_pool, whole_pool)
+    )(*inputs)
 
 
 def join(slots, tokens=(), passed=()):
@@ -205,21 +225,70 @@
     )(q, k, v, g)
 
 
-def remote_body(depth, scale, pairs, ends, q, g, inner, outer, mine, theirs, *rest):
+def far_body(depth, scale, pairs, q, g, mine, theirs, *rest):
     partial = rest[:pairs]
-    kept, sent, inner_d, outer_d, dq_t, final = rest[pairs : pairs + 6]
-    far_k, far_v, far_kt, near_t, far_dk, far_dv, near_d, qs, gs, s_all, d_all = rest[pairs + 6 :]
+    far_k, far_v, out = rest[pairs:]
     rows, width = q.shape
-    blocks = rows // BLOCK
     slots, _, per, _ = mine.shape
     half = slots * per
     pair = pl.program_id(0)
-    masks = head_masks(width, depth)
     for n, far in enumerate((far_k, far_v)):
         for m, src in enumerate((mine, theirs)):
             for s in range(slots):
                 at = m * half + s * per
                 far[at : at + per] = src[s, n]
+    for h, mask in enumerate(head_masks(width, depth)):
+        for b in range(rows // BLOCK):
+            r = slice(b * BLOCK, (b + 1) * BLOCK)
+            qs = keep_head(q[r], mask, scale)
+            gs = keep_head(g[r], mask)
+            old = [partial[0][m, h : h + 1, r] for m in range(3)]
+            for n in range(1, pairs):
+                old = [
+                    jnp.where(pair == n, partial[n][m, h : h + 1, r], old[m]) for m in range(3)
+                ]
+            state = merge(None, dot(far_k[...], qs, NT), dot(far_v[...], gs, NT))
+            for m, value in enumerate(settle(old, state)):
+                out[m, h : h + 1, r] = value
+
+
+def settle(old, state):
+    top8, total8, inner8 = state
+    top = jnp.maximum(old[0], jnp.max(top8, axis=0, keepdims=True))
+    fade = jnp.exp(old[0] - top)
+    fade8 = jnp.exp(top8 - top)
+    total = old[1] * fade + jnp.sum(total8 * fade8, axis=0, keepdims=True)
+    dots = old[2] * fade + jnp.sum(inner8 * fade8, axis=0, keepdims=True)
+    return top, total, dots
+
+
+def far_stats(q, g, mine, theirs, partial, width, depth, scale):
+    rows, cols = q.shape
+    pairs = cols // width
+    hp = width // depth
+    slots, _, per, _ = mine.shape
+    far = 2 * slots * per
+    wide = lambda n: pl.BlockSpec((n, width), lambda i: (0, i))
+    slot = pl.BlockSpec((slots, 2, per, width), lambda i: (0, 0, 0, i))
+    fixed = pl.BlockSpec((3, hp, rows), lambda i: (0, 0, 0))
+    return call(
+        functools.partial(far_body, depth, scale, pairs),
+        flops=4 * far * rows * cols,
+        moved=rows * cols * 4,
+        grid=(pairs,),
+        in_specs=[wide(rows)] * 2 + [slot] * 2 + [fixed] * pairs,
+        out_specs=[wide(far)] * 2 + [pl.BlockSpec((None, 3, hp, rows), lambda i: (i, 0, 0, 0))],
+        out_shape=[struct((far, cols), BF16)] * 2 + [struct((pairs, 3, hp, rows), F32)],
+    )(q, g, mine, theirs, *partial)
+
+
+def remote_body(depth, scale, q, g, inner, outer, far_k, far_v, known, *rest):
+    kept, sent, inner_d, outer_d, dq_t, final = rest[:6]
+    far_kt, near_t, near_d, qs, gs = rest[6:]
+    rows, width = q.shape
+    blocks = rows // BLOCK
+    half = far_k.shape[0] // 2
+    masks = head_masks(width, depth)
     far_kt[...] = (far_k[...].astype(F32) * scale).astype(BF16).T
     near_t[0] = (inner[0].astype(F32) * scale).astype(BF16).T
     near_t[1] = (outer[0].astype(F32) * scale).astype(BF16).T
@@ -227,134 +296,85 @@
     for h, mask in enumerate(masks):
         qs[h] = jnp.where(mask, scaled, 0).astype(BF16)
         gs[h] = jnp.where(mask, g[...], 0).astype(BF16)
-    odd = ends[2]
-    missing = jnp.where((ends[0] == 1) | (ends[1] == 1), NEG, 0.0)
-    first = (1 - odd) * (blocks - 1)
-    last = odd * (blocks - 1)
-    middle = list(range(1, blocks - 1))
-    order = [first, last] + middle if blocks > 1 else [0]
-
-    def place(n):
-        return pl.ds(pl.multiple_of(order[n] * BLOCK, BLOCK), BLOCK)
-
-    def sets(n):
-        out = [(0, far_k, far_v, None, far_kt, far_dk, far_dv)]
-        if n == 0:
-            out.append(
-                (2 * half, inner.at[0], inner.at[1], None, near_t.at[0], near_d.at[0], near_d.at[1])
-            )
-        if n == (1 if blocks > 1 else 0):
-            out.append(
-                (
-                    2 * half + BLOCK,
-                    outer.at[0],
-                    outer.at[1],
-                    missing,
-                    near_t.at[1],
-                    near_d.at[2],
-                    near_d.at[3],
-                )
-            )
-        return out
-
+    odd = is_odd()
+    position = lax.axis_index("seq")
+    ends = (position == 0) | (position == lax.axis_size("seq") - 1)
+    missing = jnp.where(ends, NEG, 0.0)
+    places = [
+        pl.ds(pl.multiple_of(n * ((blocks - 1) * BLOCK), BLOCK), BLOCK) for n in (1 - odd, odd)
+    ]
+    halos = ((inner, None), (outer, missing))
+    final[0] = known[0] + jnp.log(known[1])
+    final[1] = known[2] / known[1]
     for h in range(len(masks)):
-        for b in range(blocks):
-            r = place(b)
-            old = [partial[0][m, h : h + 1, r] for m in range(3)]
-            for n in range(1, pairs):
-                old = [
-                    jnp.where(pair == n, partial[n][m, h : h + 1, r], old[m]) for m in range(3)
-                ]
-            state = None
-            for at, keys, vals, bias, *_ in sets(b):
-                size = keys.shape[0]
-                s = dot(keys[...], qs[h, r], NT)
-                d = dot(vals[...], gs[h, r], NT)
-                if bias is not None:
-                    s = s + bias
-                s_all[h * blocks + b, at : at + size] = s
-                d_all[h * blocks + b, at : at + size] = d
-                state = merge(state, s, d)
-            top8, total8, inner8 = state
-            top = jnp.maximum(old[0], jnp.max(top8, axis=0, keepdims=True))
-            fade = jnp.exp(old[0] - top)
-            fade8 = jnp.exp(top8 - top)
-            total = old[1] * fade + jnp.sum(total8 * fade8, axis=0, keepdims=True)
-            dots = old[2] * fade + jnp.sum(inner8 * fade8, axis=0, keepdims=True)
-            final[0, h : h + 1, r] = top + jnp.log(total)
-            final[1, h : h + 1, r] = dots / total
+        old = None
+        for (halo, bias), r in zip(halos, places):
+            if old is None or blocks > 1:
+                old = [known[m, h : h + 1, r] for m in range(3)]
+            s = dot(halo[0], qs[h, r], NT)
+            if bias is not None:
+                s = s + bias
+            old = settle(old, merge(None, s, dot(halo[1], gs[h, r], NT)))
+            final[0, h : h + 1, r] = old[0] + jnp.log(old[1])
+            final[1, h : h + 1, r] = old[2] / old[1]
+    totals = [None, None]
     for h in range(len(masks)):
         hr = slice(h * depth, (h + 1) * depth)
-        for b in range(blocks):
-            r = place(b)
-            lse = final[0, h : h + 1, r]
-            delta = final[1, h : h + 1, r]
-            dq = None
-            for n, (at, keys, _, _, turned, dk, dv) in enumerate(sets(b)):
-                size = keys.shape[0]
-                p = jnp.exp(s_all[h * blocks + b, at : at + size] - lse)
-                ds = (p * (d_all[h * blocks + b, at : at + size] - delta)).astype(BF16)
-                v_part = dot(p.astype(BF16), gs[h, r], NN)
-                k_part = dot(ds, qs[h, r], NN)
-                if h == 0 and (n or b == 0):
-                    dv[...] = v_part
-                    dk[...] = k_part
+        p = jnp.exp(dot(far_k[...], qs[h], NT) - final[0, h : h + 1, :])
+        ds = (p * (dot(far_v[...], gs[h], NT) - final[1, h : h + 1, :])).astype(BF16)
+        parts = (dot(ds, qs[h], NN), dot(p.astype(BF16), gs[h], NN))
+        totals = [new if old is None else old + new for old, new in zip(totals, parts)]
+        dq_t[hr] = dot(far_kt[hr], ds, NN)
+        for n, ((halo, bias), r) in enumerate(zip(halos, places)):
+            s = dot(halo[0], qs[h, r], NT)
+            if bias is not None:
+                s = s + bias
+            p = jnp.exp(s - final[0, h : h + 1, r])
+            ds = (p * (dot(halo[1], gs[h, r], NT) - final[1, h : h + 1, r])).astype(BF16)
+            parts = (dot(ds, qs[h, r], NN), dot(p.astype(BF16), gs[h, r], NN))
+            for m, part in enumerate(parts):
+                if h == 0:
+                    near_d[2 * n + m] = part
                 else:
-                    dv[...] += v_part
-                    dk[...] += k_part
-                part = dot(turned[hr], ds, NN)
-                dq = part if dq is None else dq + part
-            dq_t[hr, r] = dq
-    for n, far in enumerate((far_dk, far_dv)):
-        kept[n] = far[:half]
-        sent[n] = far[half:].astype(BF16)
+                    near_d[2 * n + m] += part
+            dq_t[hr, r] += dot(near_t[n, hr], ds, NN)
+    for n in range(2):
+        kept[n] = totals[n][:half]
+        sent[n] = totals[n][half:].astype(BF16)
         inner_d[n] = near_d[n].astype(BF16)
         outer_d[n] = near_d[2 + n].astype(BF16)
 
 
-def remote(q, g, inner, outer, mine, theirs, partial, ends, width, depth, scale):
+def remote(q, g, inner, outer, far_k, far_v, known, width, depth, scale):
     rows, cols = q.shape
     pairs = cols // width
     hp = width // depth
-    slots, _, per, _ = mine.shape
-    half = slots * per
-    far = 2 * half
-    wide = lambda n: pl.BlockSpec((n, width), lambda i, *_: (0, i))
-    both = lambda n: pl.BlockSpec((2, n, width), lambda i, *_: (0, 0, i))
-    slot = pl.BlockSpec((slots, 2, per, width), lambda i, *_: (0, 0, 0, i))
-    fixed = pl.BlockSpec((3, hp, rows), lambda i, *_: (0, 0, 0))
-    held = pltpu.VMEM((hp * rows // BLOCK, far + 2 * BLOCK, BLOCK), F32)
-    grid_spec = pltpu.PrefetchScalarGridSpec(
-        num_scalar_prefetch=1,
+    far = far_k.shape[0]
+    half = far // 2
+    wide = lambda n: pl.BlockSpec((n, width), lambda i: (0, i))
+    both = lambda n: pl.BlockSpec((2, n, width), lambda i: (0, 0, i))
+    row = lambda n: pl.BlockSpec((None, n, hp, rows), lambda i: (i, 0, 0, 0))
+    return call(
+        functools.partial(remote_body, depth, scale),
+        flops=10 * (far * rows + 2 * BLOCK * BLOCK) * cols,
+        moved=rows * cols * 8,
         grid=(pairs,),
-        in_specs=[wide(rows)] * 2 + [both(BLOCK)] * 2 + [slot] * 2 + [fixed] * pairs,
+        in_specs=[wide(rows)] * 2 + [both(BLOCK)] * 2 + [wide(far)] * 2 + [row(3)],
         out_specs=[
             both(half),
             both(half),
             both(BLOCK),
             both(BLOCK),
-            pl.BlockSpec((width, rows), lambda i, *_: (i, 0)),
-            pl.BlockSpec((None, 2, hp, rows), lambda i, *_: (i, 0, 0, 0)),
+            pl.BlockSpec((width, rows), lambda i: (i, 0)),
+            row(2),
         ],
         scratch_shapes=[
-            pltpu.VMEM((far, width), BF16),
-            pltpu.VMEM((far, width), BF16),
             pltpu.VMEM((width, far), BF16),
             pltpu.VMEM((2, width, BLOCK), BF16),
-            pltpu.VMEM((far, width), F32),
-            pltpu.VMEM((far, width), F32),
             pltpu.VMEM((4, BLOCK, width), F32),
             pltpu.VMEM((hp, rows, width), BF16),
             pltpu.VMEM((hp, rows, width), BF16),
-            held,
-            held,
         ],
-    )
-    return call(
-        functools.partial(remote_body, depth, scale, pairs),
-        flops=10 * (far * rows + 2 * BLOCK * BLOCK) * cols,
-        moved=rows * cols * 8,
-        grid_spec=grid_spec,
         out_shape=[
             struct((2, half, cols), F32),
             struct((2, half, cols), BF16),
@@ -363,7 +383,7 @@
             struct((cols, rows), F32),
             struct((pairs, 2, hp, rows), F32),
         ],
-    )(ends, q, g, inner, outer, mine, theirs, *partial)
+    )(q, g, inner, outer, far_k, far_v, known)
 
 
 def local_body(depth, scale, chained, q, k, v, g, part, final, *rest):
@@ -460,54 +480,78 @@
     )(kept, *got, *extra)
 
 
-def finish_body(pairs, ends, *refs):
+def finish_body(pairs, depth, *refs):
     dk, dv = refs[:pairs], refs[pairs : 2 * pairs]
-    from_inner, from_outer, wide_group, wide_whole, kept = refs[2 * pairs : 2 * pairs + 5]
-    got, (out_k, out_v) = refs[2 * pairs + 5 : -2], refs[-2:]
+    from_inner, from_outer, group_pool, whole_pool, kept = refs[2 * pairs : 2 * pairs + 5]
+    got = refs[2 * pairs + 5 : -4]
+    out_k, out_v, wide_group, wide_whole = refs[-4:]
     block = pl.program_id(0)
-    blocks = pl.num_programs(0)
+    rows, cols = kept.shape[1:]
+    heads = group_pool.shape[0]
     width = dk[0].shape[1]
     per = BLOCK // SEG1
-    rows = kept.shape[1]
     count1 = rows * SEG2 // (SEG1 + SEG2)
-    odd = ends[2]
-    from_in = jnp.where(block == (1 - odd) * (blocks - 1), 1.0, 0.0)
-    from_out = jnp.where(block == odd * (blocks - 1), 1.0, 0.0)
-    index = lax.broadcasted_iota(jnp.int32, (rows, 1), 0)
-    for n, (src, dst) in enumerate(((dk, out_k), (dv, out_v))):
-        sums = gathered(kept, got, n)
-        whole = jnp.sum(jnp.where(index == count1 + block, sums, 0.0), axis=0, keepdims=True)
-        for s in range(per):
-            mine = jnp.where(index == block * per + s, sums, 0.0)
-            group = jnp.sum(mine, axis=0, keepdims=True)
-            c = slice(s * SEG1, (s + 1) * SEG1)
-            piece = group * wide_group[...] + whole * wide_whole[c]
-            piece = piece + from_in * from_inner[n, c].astype(F32)
-            piece = piece + from_out * from_outer[n, c].astype(F32)
-            for p in range(pairs):
-                lanes = slice(p * width, (p + 1) * width)
-                dst[c, lanes] = (piece[:, lanes] + src[p][c]).astype(BF16)
-
-
-def finish(dk, dv, from_inner, from_outer, kept, got, wide_group, wide_whole, ends):
+    blocks = count1 // per
+
+    @pl.when(block == 0)
+    def _():
+        head = lax.broadcasted_iota(jnp.int32, (heads, cols), 0)
+        col = lax.broadcasted_iota(jnp.int32, (heads, cols), 1)
+        pick = ((col >= head * depth) & (col < (head + 1) * depth)).astype(F32)
+        for src, dst in ((group_pool, wide_group), (whole_pool, wide_whole)):
+            dst[...] = lax.dot_general(
+                src[...],
+                pick,
+                (((0,), (0,)), ((), ())),
+                precision=lax.Precision.HIGHEST,
+                preferred_element_type=F32,
+            )
+
+    def emit(halos):
+        index = lax.broadcasted_iota(jnp.int32, (rows, 1), 0)
+        for n, (src, dst) in enumerate(((dk, out_k), (dv, out_v))):
+            sums = gathered(kept, got, n)
+            whole = jnp.sum(jnp.where(index == count1 + block, sums, 0.0), axis=0, keepdims=True)
+            for s in range(per):
+                mine = jnp.where(index == block * per + s, sums, 0.0)
+                group = jnp.sum(mine, axis=0, keepdims=True)
+                c = slice(s * SEG1, (s + 1) * SEG1)
+                piece = group * wide_group[...] + whole * wide_whole[c]
+                for halo in halos:
+                    piece = piece + halo[n, c].astype(F32)
+                for p in range(pairs):
+                    lanes = slice(p * width, (p + 1) * width)
+                    dst[c, lanes] = (piece[:, lanes] + src[p][c]).astype(BF16)
+
+    if blocks == 1:
+        emit((from_inner, from_outer))
+        return
+    odd = is_odd()
+    at_inner = block == (1 - odd) * (blocks - 1)
+    at_outer = block == odd * (blocks - 1)
+    pl.when(at_inner)(lambda: emit((from_inner,)))
+    pl.when(at_outer)(lambda: emit((from_outer,)))
+    pl.when(jnp.logical_not(at_inner | at_outer))(lambda: emit(()))
+
+
+def finish(dk, dv, from_inner, from_outer, kept, got, group_pool, whole_pool):
     rows, width = dk[0].shape
     pairs = len(dk)
     cols = width * pairs
-    tile = pl.BlockSpec((BLOCK, cols), lambda i, *_: (i, 0))
-    narrow = pl.BlockSpec((BLOCK, width), lambda i, *_: (i, 0))
-    full = lambda x: pl.BlockSpec(x.shape, lambda i, *_: (0,) * x.ndim)
-    fixed = [from_inner, from_outer, wide_group, wide_whole, kept] + list(got)
-    return call(
-        functools.partial(finish_body, pairs),
+    depth = cols // group_pool.shape[0]
+    tile = pl.BlockSpec((BLOCK, cols), lambda i: (i, 0))
+    narrow = pl.BlockSpec((BLOCK, width), lambda i: (i, 0))
+    full = lambda x: pl.BlockSpec(x.shape, lambda i: (0,) * x.ndim)
+    fixed = [from_inner, from_outer, group_pool, whole_pool, kept] + list(got)
+    return call(
+        functools.partial(finish_body, pairs, depth),
         moved=rows * cols * 12,
-        grid_spec=pltpu.PrefetchScalarGridSpec(
-            num_scalar_prefetch=1,
-            grid=(rows // BLOCK,),
-            in_specs=[narrow] * (2 * pairs) + [full(x) for x in fixed],
-            out_specs=[tile, tile],
-        ),
+        grid=(rows // BLOCK,),
+        in_specs=[narrow] * (2 * pairs) + [full(x) for x in fixed],
+        out_specs=[tile, tile],
         out_shape=[struct((rows, cols), BF16)] * 2,
-    )(ends, *dk, *dv, *fixed)
+        scratch_shapes=[pltpu.VMEM((SEG1, cols), F32), pltpu.VMEM((SEG2, cols), F32)],
+    )(*dk, *dv, *fixed)
 
 
 def shards(query, key, value, out_grad, pool_group, pool_global):
@@ -518,7 +562,6 @@
     width = 128 if cols % 128 == 0 and 128 % depth == 0 else cols
     pairs = cols // width
     devices = lax.axis_size("seq")
-    position = lax.axis_index("seq")
     count1 = rows // SEG1
     group_bits = list(range(1, GROUP.bit_length() - 1))
     other_bits = list(range(GROUP.bit_length() - 1, devices.bit_length() - 1))
@@ -531,11 +574,7 @@
         route = [(i, i + 1) for i in range(1, devices - 1, 2)]
         return lax.ppermute(array, "seq", route + [(b, a) for a, b in route])
 
-    ends = jnp.stack([position == 0, position == devices - 1, position % 2 == 1])
-    ends = ends.astype(jnp.int32)
-    groups, wholes, inner, outer, wide_group, wide_whole = pool(
-        key, value, pool_group, pool_global, ends, width
-    )
+    groups, wholes, inner, outer, key, value = pool(key, value, pool_group, pool_global)
     partial = [
         stats(query, key, value, out_grad, width, depth, scale, p) for p in range(pairs)
     ]
@@ -562,8 +601,11 @@
     outer = cross(outer)
     inner = swap(inner, 0)
 
+    far_k, far_v, known = far_stats(
+        query, out_grad, comb, theirs, partial, width, depth, scale
+    )
     kept, sent, inner_d, outer_d, dq_t, final = remote(
-        query, out_grad, inner, outer, comb, theirs, partial, ends, width, depth, scale
+        query, out_grad, inner, outer, far_k, far_v, known, width, depth, scale
     )
     got = [swap(sent, 0)]
 
@@ -612,7 +654,7 @@
     while len(dk) < pairs:
         step()
     key_grad, value_grad = finish(
-        dk, dv, from_inner, from_outer, kept, got, wide_group, wide_whole, ends
+        dk, dv, from_inner, from_outer, kept, got, pool_group, pool_global
     )
     return (query_grad, key_grad, value_grad)
 

time: 78.8 us -> 76 us (0.964)
  local copies, waits for them, and re-layouts: 3.25 us -> 0.02 us
  waiting for transfers between devices: 1.38 us -> 3.11 us
    pallas_call x2 -> x3, Pallas kernels: 15.7 us -> 19.1 us  [the longest x1 11.8 us: remote(): call(functools.partial(remote_body, depth, scale), flops=10 * (far * rows...]
    unnamed x26 -> x8, local copies, waits for them, and re-layouts: 3.25 us -> 0.02 us
    pallas_call x1, Pallas kernels: 5.25 us -> 2.92 us  [pool(): call(functools.partial(pool_body, cols // heads), moved=k.size * 6, vmem=...]
    ppermute x12, waiting for transfers between devices: 1.38 us -> 3.11 us  [swap(): return lax.ppermute(array, 'seq', [(i, i ^ mask) for i in range(devices)])]
    pallas_call x3, Pallas kernels: 1.44 us -> 0.04 us  [join(): call(body, moved=4 * count * 2 * rows * cols, in_specs=[vmem] * len(flat)...]
  transfers between devices with their start and end apart: 14 -> 14, of which waited for: 1 -> 3; matrix products, arithmetic and copies ran while one was open for 0% -> 0% of each run, Pallas kernels for 31% -> 37%
where the time goes in v3:
time: 76 us; the launch traced here: 75.2 us
  Pallas kernels  46 us (61%)
  starting transfers between devices  25.3 us (33%)
  waiting for transfers between devices  3.11 us (4%)
  between operations  0.79 us (1%)
    ppermute x12, starting transfers between devices, swap(): return lax.ppermute(array, 'seq', [(i, i ^ mask) for i in range(devices)])  20.1 us
    pallas_call x4, Pallas kernels, local(): call(functools.partial(local_body, depth, scale, len(extra)), flops=10 *...  16.8 us
    pallas_call x1, Pallas kernels, remote(): call(functools.partial(remote_body, depth, scale), flops=10 * (far * rows...  11.8 us
    pallas_call x4, Pallas kernels, stats(): call(functools.partial(stats_body, depth, scale), flops=2 * 2 * 3 * BLOCK...  6.96 us
    ppermute x2, starting transfers between devices, cross(): return lax.ppermute(array, 'seq', route + [(b, a) for a, b in route])  5.18 us
    pallas_call x1, Pallas kernels, far_stats(): call(functools.partial(far_body, depth, scale, pairs), flops=4 * far * ro...  3.83 us
    pallas_call x1, Pallas kernels, finish(): call(functools.partial(finish_body, pairs, depth), moved=rows * cols * 12...  3.48 us
    ppermute x12, waiting for transfers between devices, swap(): return lax.ppermute(array, 'seq', [(i, i ^ mask) for i in range(devices)])  3.11 us
  transfers between devices with their start and end apart: 14, of which 3 were waited for; matrix products, arithmetic and copies ran while one was open for 0% of the time, Pallas kernels for 37%

profile of v3, /device:TPU:1, one launch (start us, length us, event | category | flops | bytes accessed | tf_op | source)
XLA Modules:
  0.0 75.2 jit_solution(4472816019192622659)
XLA Ops:
  0.7 2.9 %shard_map.85 = (bf16[2,16,512]{2,1,0:T(8,128)(2,1)S(1)}, bf16[2,4,512]{2,1,0:T(4,128)(2,1)S(1)}, bf16[2,256,512]{2,1,0:T(8,128)(2,1)S(1)}, bf16[2,256,512]{2,1,...) custom-call(bf16[1024,512]{1,0:T(8,128)(2,1)} %k.1, bf16[1024,512]{1,0:T(8,128)(2,1)} %v.1, ...), custom_call_target="tpu_custom_call" | custom-call | bytes 3145728 | tf_op jit(solution)/shard_map/pallas_call | solution.py:121
  3.6 2.1 %collective-permute-start.1 = (bf16[2,20,512]{2,1,0:T(8,128)(2,1)S(1)}, bf16[2,20,512]{2,1,0:T(8,128)(2,1)S(1)}, u32[]{:S(2)}, u32[]{:S(2)}) collective-permute-start(bf16[2,20,512]{2,1,0:T(8,128)(2,1)S(1)} %bitcast.1), channel_id=1, source_target_pairs={{0,4},{2,6},{4,0},{6,2},{8,12},{10,14},{12,8},{14,10},{16,20},{18,... | collective-permute-start | bytes 122888 | tf_op jit(solution)/shard_map/ppermute | solution.py:571
  5.7 2.2 %collective-permute-start.2 = (bf16[2,4,512]{2,1,0:T(4,128)(2,1)S(1)}, bf16[2,4,512]{2,1,0:T(4,128)(2,1)S(1)}, u32[]{:S(2)}, u32[]{:S(2)}) collective-permute-start(bf16[2,4,512]{2,1,0:T(4,128)(2,1)S(1)} %get-tuple-element.46.refs_1_), channel_id=1, source_target_pairs={{0,20},{2,22},{4,16},{6,18},{8,28},{10,30},{12,24},{14,26},{16,4},... | collective-permute-start | bytes 24584 | tf_op jit(solution)/shard_map/ppermute | solution.py:571
  8.0 0.1 collective-permute-start
  8.0 1.7 %shard_map.87.refs_7_.rest_0_ = f32[3,2,1024]{2,1,0:T(2,128)S(1)} custom-call(bf16[1024,512]{1,0:T(8,128)(2,1)S(1)} %copy-done, bf16[1024,512]{1,0:T(8,128)(2,1)S(1)} %get-tuple-element.43.k, bf16[1024,512]{1,0:T(8,128)(2,1)S(1)} %get-tuple-element.44.v, bf16[1024,512]{1,0:T(8,128)(2,1)S(1)} %copy-done.1), custom_call_target="tpu_custom_call" | custom-call | flops 402653184 | bytes 1048576 | tf_op jit(solution)/shard_map/pallas_call | solution.py:217
  9.8 0.2 collective-permute-done.2.refs_4_
  10.0 1.6 %collective-permute-done.refs_2_ = bf16[2,4,512]{2,1,0:T(4,128)(2,1)S(1)} collective-permute-done((bf16[2,4,512]{2,1,0:T(4,128)(2,1)S(1)}, bf16[2,4,512]{2,1,0:T(4,128)(2,1)S(1)}, u32[]{:S(2)}, u32[]{:S(2)}) %collective-permute-start) | collective-permute-done | bytes 8224 | tf_op jit(solution)/shard_map/ppermute | solution.py:571
  11.7 2.2 %collective-permute-start.3 = (bf16[2,256,512]{2,1,0:T(8,128)(2,1)S(1)}, bf16[2,256,512]{2,1,0:T(8,128)(2,1)S(1)}, u32[]{:S(2)}, u32[]{:S(2)}) collective-permute-start(bf16[2,256,512]{2,1,0:T(8,128)(2,1)S(1)} %get-tuple-element.49), channel_id=1, source_target_pairs={{0,2},{2,0},{4,6},{6,4},{8,10},{10,8},{12,14},{14,12},{16,18},{18,... | collective-permute-start | bytes 1572872 | tf_op jit(solution)/shard_map/ppermute | solution.py:571
  13.8 3.1 %collective-permute-start.4 = (bf16[2,256,512]{2,1,0:T(8,128)(2,1)S(1)}, bf16[2,256,512]{2,1,0:T(8,128)(2,1)S(1)}, u32[]{:S(2)}, u32[]{:S(2)}) collective-permute-start(bf16[2,256,512]{2,1,0:T(8,128)(2,1)S(1)} %get-tuple-element.50), channel_id=1, source_target_pairs={{2,4},{6,8},{10,12},{14,16},{18,20},{22,24},{26,28},{4,2},{8,6},{1... | collective-permute-start | bytes 1572872 | tf_op jit(solution)/shard_map/ppermute | solution.py:575
  16.9 1.4 %collective-permute-start.5 = (bf16[2,2,24,512]{3,2,1,0:T(8,128)(2,1)S(1)}, bf16[2,2,24,512]{3,2,1,0:T(8,128)(2,1)S(1)}, u32[]{:S(2)}, u32[]{:S(2)}) collective-permute-start(bf16[2,2,24,512]{3,2,1,0:T(8,128)(2,1)S(1)} %get-tuple-element.51.refs_0_), channel_id=1, source_target_pairs={{0,8},{2,10},{4,12},{6,14},{8,0},{10,2},{12,4},{14,6},{16,24},{18,... | collective-permute-start | bytes 294920 | tf_op jit(solution)/shard_map/ppermute | solution.py:571
  18.3 1.7 %shard_map.89.refs_2_.rest_1_ = f32[3,2,1024]{2,1,0:T(2,128)S(1)} custom-call(bf16[1024,512]{1,0:T(8,128)(2,1)S(1)} %copy-done, bf16[1024,512]{1,0:T(8,128)(2,1)S(1)} %get-tuple-element.43.k, bf16[1024,512]{1,0:T(8,128)(2,1)S(1)} %get-tuple-element.44.v, bf16[1024,512]{1,0:T(8,128)(2,1)S(1)} %copy-done.1), custom_call_target="tpu_custom_call" | custom-call | flops 402653184 | bytes 1048576 | tf_op jit(solution)/shard_map/pallas_call | solution.py:217
  20.0 1.2 %collective-permute-done.5.refs_1_ = bf16[2,2,24,512]{3,2,1,0:T(8,128)(2,1)S(1)} collective-permute-done((bf16[2,2,24,512]{3,2,1,0:T(8,128)(2,1)S(1)}, bf16[2,2,24,512]{3,2,1,0:T(8,128)(2,1)S(1)}, u32[]{:S(2)}, u32[]{:S(2)}) %collective-permute-start.5) | collective-permute-done | bytes 98336 | tf_op jit(solution)/shard_map/ppermute | solution.py:571
  21.2 6.7 %collective-permute-start.6 = (bf16[4,2,24,512]{3,2,1,0:T(8,128)(2,1)S(1)}, bf16[4,2,24,512]{3,2,1,0:T(8,128)(2,1)S(1)}, u32[]{:S(2)}, u32[]{:S(2)}) collective-permute-start(bf16[4,2,24,512]{3,2,1,0:T(8,128)(2,1)S(1)} %shard_map.90.mine), channel_id=1, source_target_pairs={{0,2},{2,0},{4,6},{6,4},{8,10},{10,8},{12,14},{14,12},{16,18},{18,... | collective-permute-start | bytes 589832 | tf_op jit(solution)/shard_map/ppermute | solution.py:571
  27.9 1.7 %shard_map.92.rest_3_ = f32[3,2,1024]{2,1,0:T(2,128)S(1)} custom-call(bf16[1024,512]{1,0:T(8,128)(2,1)S(1)} %copy-done, bf16[1024,512]{1,0:T(8,128)(2,1)S(1)} %get-tuple-element.43.k, bf16[1024,512]{1,0:T(8,128)(2,1)S(1)} %get-tuple-element.44.v, bf16[1024,512]{1,0:T(8,128)(2,1)S(1)} %copy-done.1), custom_call_target="tpu_custom_call" | custom-call | flops 402653184 | bytes 1048576 | tf_op jit(solution)/shard_map/pallas_call | solution.py:217
  29.7 1.7 %shard_map.91.rest_2_ = f32[3,2,1024]{2,1,0:T(2,128)S(1)} custom-call(bf16[1024,512]{1,0:T(8,128)(2,1)S(1)} %copy-done, bf16[1024,512]{1,0:T(8,128)(2,1)S(1)} %get-tuple-element.43.k, bf16[1024,512]{1,0:T(8,128)(2,1)S(1)} %get-tuple-element.44.v, bf16[1024,512]{1,0:T(8,128)(2,1)S(1)} %copy-done.1), custom_call_target="tpu_custom_call" | custom-call | flops 402653184 | bytes 1048576 | tf_op jit(solution)/shard_map/pallas_call | solution.py:217
  31.4 3.8 %shard_map.93 = (bf16[192,512]{1,0:T(8,128)(2,1)S(1)}, bf16[192,512]{1,0:T(8,128)(2,1)S(1)}, f32[4,3,2,1024]{3,2,1,0:T(2,128)S(1)}) custom-call(bf16[1024,512]{1,0:T(8,128)(2,1)S(1)} %copy-done, bf16[1024,512]{1,0:T(8,128)(2,1)S(1)} %copy-done.1, bf16[4,2,24,512]{3,2,1,0:T(8,128)(2,1)S(1)} %shard_map.90.mine, ...), custom_call_target="tpu_custom_call" | custom-call | flops 402653184 | bytes 2097152 | tf_op jit(solution)/shard_map/pallas_call | solution.py:274
  35.3 0.0 collective-permute-done.4.outer
  35.3 11.8 %shard_map.94 = (f32[2,96,512]{2,1,0:T(8,128)S(1)}, bf16[2,96,512]{2,1,0:T(8,128)(2,1)S(1)}, bf16[2,256,512]{2,1,0:T(8,128)(2,1)S(1)}, bf16[2,256,512]{2,1,0:T(8...) custom-call(bf16[1024,512]{1,0:T(8,128)(2,1)S(1)} %copy-done, bf16[1024,512]{1,0:T(8,128)(2,1)S(1)} %copy-done.1, ...), custom_call_target="tpu_custom_call" | custom-call | flops 1677721600 | bytes 4194304 | tf_op jit(solution)/shard_map/pallas_call | solution.py:357
  47.1 0.1 collective-permute-start.7
  47.2 4.2 %shard_map.95 = (bf16[1024,512]{1,0:T(8,128)(2,1)}, f32[1024,128]{1,0:T(8,128)S(1)}, f32[1024,128]{1,0:T(8,128)S(1)}) custom-call(bf16[1024,512]{1,0:T(8,128)(2,1)S(1)} %copy-done, bf16[1024,512]{1,0:T(8,128)(2,1)S(1)} %get-tuple-element.43.k, bf16[1024,512]{1,0:T(8,128)(2,1)S(1)} %get-tuple-element.44.v, bf16[1024,512]{1,0:T(8,128)(2,1)S(1)} %copy-done.1, ...), custom_call_target="tpu_custom_call" | custom-call | flops 1006632960 | bytes 3145728 | tf_op jit(solution)/shard_map/pallas_call | solution.py:425
  51.4 0.0 collective-permute-done.7.rest_0_
  51.5 0.6 collective-permute-start.8
  52.0 2.1 %collective-permute-start.9 = (bf16[2,256,512]{2,1,0:T(8,128)(2,1)S(1)}, bf16[2,256,512]{2,1,0:T(8,128)(2,1)S(1)}, u32[]{:S(2)}, u32[]{:S(2)}) collective-permute-start(bf16[2,256,512]{2,1,0:T(8,128)(2,1)S(1)} %get-tuple-element.74), channel_id=1, source_target_pairs={{2,4},{6,8},{10,12},{14,16},{18,20},{22,24},{26,28},{4,2},{8,6},{1... | collective-permute-start | bytes 1572872 | tf_op jit(solution)/shard_map/ppermute | solution.py:575
  54.2 1.2 %collective-permute-start.10 = (bf16[2,48,512]{2,1,0:T(8,128)(2,1)S(1)}, bf16[2,48,512]{2,1,0:T(8,128)(2,1)S(1)}, u32[]{:S(2)}, u32[]{:S(2)}) collective-permute-start(bf16[2,48,512]{2,1,0:T(8,128)(2,1)S(1)} %get-tuple-element.76), channel_id=1, source_target_pairs={{0,8},{2,10},{4,12},{6,14},{8,0},{10,2},{12,4},{14,6},{16,24},{18,... | collective-permute-start | bytes 294920 | tf_op jit(solution)/shard_map/ppermute | solution.py:571
  55.4 4.2 %shard_map.96 = (bf16[1024,512]{1,0:T(8,128)(2,1)}, f32[1024,128]{1,0:T(8,128)S(1)}, f32[1024,128]{1,0:T(8,128)S(1)}) custom-call(bf16[1024,512]{1,0:T(8,128)(2,1)S(1)} %copy-done, bf16[1024,512]{1,0:T(8,128)(2,1)S(1)} %get-tuple-element.43.k, bf16[1024,512]{1,0:T(8,128)(2,1)S(1)} %get-tuple-element.44.v, ...), custom_call_target="tpu_custom_call", output_to_operand_aliasing={{0}: (6, {})} | custom-call | flops 1006632960 | bytes 3145728 | tf_op jit(solution)/shard_map/pallas_call | solution.py:425
  59.6 4.2 %shard_map.97 = (bf16[1024,512]{1,0:T(8,128)(2,1)}, f32[1024,128]{1,0:T(8,128)S(1)}, f32[1024,128]{1,0:T(8,128)S(1)}) custom-call(bf16[1024,512]{1,0:T(8,128)(2,1)S(1)} %copy-done, bf16[1024,512]{1,0:T(8,128)(2,1)S(1)} %get-tuple-element.43.k, bf16[1024,512]{1,0:T(8,128)(2,1)S(1)} %get-tuple-element.44.v, ...), custom_call_target="tpu_custom_call", output_to_operand_aliasing={{0}: (6, {})} | custom-call | flops 1006632960 | bytes 3145728 | tf_op jit(solution)/shard_map/pallas_call | solution.py:425
  63.8 0.4 collective-permute-start.12
  64.3 1.9 %collective-permute-start.13 = (bf16[2,4,512]{2,1,0:T(4,128)(2,1)S(1)}, bf16[2,4,512]{2,1,0:T(4,128)(2,1)S(1)}, u32[]{:S(2)}, u32[]{:S(2)}) collective-permute-start(bf16[2,4,512]{2,1,0:T(4,128)(2,1)S(1)} %get-tuple-element.80), channel_id=1, source_target_pairs={{0,20},{2,22},{4,16},{6,18},{8,28},{10,30},{12,24},{14,26},{16,4},... | collective-permute-start | bytes 24584 | tf_op jit(solution)/shard_map/ppermute | solution.py:571
  66.2 1.2 %collective-permute-start.11 = (bf16[2,20,512]{2,1,0:T(8,128)(2,1)S(1)}, bf16[2,20,512]{2,1,0:T(8,128)(2,1)S(1)}, u32[]{:S(2)}, u32[]{:S(2)}) collective-permute-start(bf16[2,20,512]{2,1,0:T(8,128)(2,1)S(1)} %get-tuple-element.78), channel_id=1, source_target_pairs={{0,4},{2,6},{4,0},{6,2},{8,12},{10,14},{12,8},{14,10},{16,20},{18,... | collective-permute-start | bytes 122888 | tf_op jit(solution)/shard_map/ppermute | solution.py:571
  67.5 4.2 %shard_map.98 = (bf16[1024,512]{1,0:T(8,128)(2,1)}, f32[1024,128]{1,0:T(8,128)S(1)}, f32[1024,128]{1,0:T(8,128)S(1)}) custom-call(bf16[1024,512]{1,0:T(8,128)(2,1)S(1)} %copy-done, bf16[1024,512]{1,0:T(8,128)(2,1)S(1)} %get-tuple-element.43.k, bf16[1024,512]{1,0:T(8,128)(2,1)S(1)} %get-tuple-element.44.v, ...), custom_call_target="tpu_custom_call", output_to_operand_aliasing={{0}: (6, {})} | custom-call | flops 1006632960 | bytes 3145728 | tf_op jit(solution)/shard_map/pallas_call | solution.py:425
  71.7 0.0 collective-permute-done.8.refs_8_
  71.7 3.5 %shard_map.101 = (bf16[1024,512]{1,0:T(8,128)(2,1)}, bf16[1024,512]{1,0:T(8,128)(2,1)}) custom-call(f32[1024,128]{1,0:T(8,128)S(1)} %get-tuple-element.61.rest_3_.refs_0_, f32[1024,128]{1,0:T(8,128)S(1)} %get-tuple-element.62.refs_1_, f32[1024,128]{1,0:T(8,128)S(1)} %get-tuple-element.63.rest_1_.refs_2_, f32[1024,128]{1,0:T(8,128)S(1)} %get-tuple-element.64.refs_3_, ...), custom_call_target="tpu_custom_call" | custom-call | bytes 6291456 | tf_op jit(solution)/shard_map/pallas_call | solution.py:546
  (21 shorter events, 0.1 us)
Async XLA Ops:
  0.6 7.4 %copy-start.1 = (bf16[1024,512]{1,0:T(8,128)(2,1)S(1)}, bf16[1024,512]{1,0:T(8,128)(2,1)}, u32[]{:S(2)}) copy-start(bf16[1024,512]{1,0:T(8,128)(2,1)} %g.19) | copy-start | bytes 3145732
  0.6 7.4 %copy-start = (bf16[1024,512]{1,0:T(8,128)(2,1)S(1)}, bf16[1024,512]{1,0:T(8,128)(2,1)}, u32[]{:S(2)}) copy-start(bf16[1024,512]{1,0:T(8,128)(2,1)} %q.19) | copy-start | bytes 3145732
  3.6 8.1 %collective-permute-start.1 = (bf16[2,20,512]{2,1,0:T(8,128)(2,1)S(1)}, bf16[2,20,512]{2,1,0:T(8,128)(2,1)S(1)}, u32[]{:S(2)}, u32[]{:S(2)}) collective-permute-start(bf16[2,20,512]{2,1,0:T(8,128)(2,1)S(1)} %bitcast.1), channel_id=1, source_target_pairs={{0,4},{2,6},{4,0},{6,2},{8,12},{10,14},{12,8},{14,10},{16,20},{18,... | collective-permute-start | bytes 122888 | tf_op jit(solution)/shard_map/ppermute | solution.py:571
  5.7 4.3 %collective-permute-start.2 = (bf16[2,4,512]{2,1,0:T(4,128)(2,1)S(1)}, bf16[2,4,512]{2,1,0:T(4,128)(2,1)S(1)}, u32[]{:S(2)}, u32[]{:S(2)}) collective-permute-start(bf16[2,4,512]{2,1,0:T(4,128)(2,1)S(1)} %get-tuple-element.46.refs_1_), channel_id=1, source_target_pairs={{0,20},{2,22},{4,16},{6,18},{8,28},{10,30},{12,24},{14,26},{16,4},... | collective-permute-start | bytes 24584 | tf_op jit(solution)/shard_map/ppermute | solution.py:571
  8.0 3.7 %collective-permute-start = (bf16[2,4,512]{2,1,0:T(4,128)(2,1)S(1)}, bf16[2,4,512]{2,1,0:T(4,128)(2,1)S(1)}, u32[]{:S(2)}, u32[]{:S(2)}) collective-permute-start(bf16[2,4,512]{2,1,0:T(4,128)(2,1)S(1)} %get-tuple-element.46.refs_1_), channel_id=1, source_target_pairs={{0,16},{2,18},{4,20},{6,22},{8,24},{10,26},{12,28},{14,30},{16,0},... | collective-permute-start | bytes 24584 | tf_op jit(solution)/shard_map/ppermute | solution.py:571
  11.7 23.6 %collective-permute-start.3 = (bf16[2,256,512]{2,1,0:T(8,128)(2,1)S(1)}, bf16[2,256,512]{2,1,0:T(8,128)(2,1)S(1)}, u32[]{:S(2)}, u32[]{:S(2)}) collective-permute-start(bf16[2,256,512]{2,1,0:T(8,128)(2,1)S(1)} %get-tuple-element.49), channel_id=1, source_target_pairs={{0,2},{2,0},{4,6},{6,4},{8,10},{10,8},{12,14},{14,12},{16,18},{18,... | collective-permute-start | bytes 1572872 | tf_op jit(solution)/shard_map/ppermute | solution.py:571
  13.8 21.4 %collective-permute-start.4 = (bf16[2,256,512]{2,1,0:T(8,128)(2,1)S(1)}, bf16[2,256,512]{2,1,0:T(8,128)(2,1)S(1)}, u32[]{:S(2)}, u32[]{:S(2)}) collective-permute-start(bf16[2,256,512]{2,1,0:T(8,128)(2,1)S(1)} %get-tuple-element.50), channel_id=1, source_target_pairs={{2,4},{6,8},{10,12},{14,16},{18,20},{22,24},{26,28},{4,2},{8,6},{1... | collective-permute-start | bytes 1572872 | tf_op jit(solution)/shard_map/ppermute | solution.py:575
  16.9 4.3 %collective-permute-start.5 = (bf16[2,2,24,512]{3,2,1,0:T(8,128)(2,1)S(1)}, bf16[2,2,24,512]{3,2,1,0:T(8,128)(2,1)S(1)}, u32[]{:S(2)}, u32[]{:S(2)}) collective-permute-start(bf16[2,2,24,512]{3,2,1,0:T(8,128)(2,1)S(1)} %get-tuple-element.51.refs_0_), channel_id=1, source_target_pairs={{0,8},{2,10},{4,12},{6,14},{8,0},{10,2},{12,4},{14,6},{16,24},{18,... | collective-permute-start | bytes 294920 | tf_op jit(solution)/shard_map/ppermute | solution.py:571
  21.2 10.2 %collective-permute-start.6 = (bf16[4,2,24,512]{3,2,1,0:T(8,128)(2,1)S(1)}, bf16[4,2,24,512]{3,2,1,0:T(8,128)(2,1)S(1)}, u32[]{:S(2)}, u32[]{:S(2)}) collective-permute-start(bf16[4,2,24,512]{3,2,1,0:T(8,128)(2,1)S(1)} %shard_map.90.mine), channel_id=1, source_target_pairs={{0,2},{2,0},{4,6},{6,4},{8,10},{10,8},{12,14},{14,12},{16,18},{18,... | collective-permute-start | bytes 589832 | tf_op jit(solution)/shard_map/ppermute | solution.py:571
  47.1 4.3 %collective-permute-start.7 = (bf16[2,96,512]{2,1,0:T(8,128)(2,1)S(1)}, bf16[2,96,512]{2,1,0:T(8,128)(2,1)S(1)}, u32[]{:S(2)}, u32[]{:S(2)}) collective-permute-start(bf16[2,96,512]{2,1,0:T(8,128)(2,1)S(1)} %get-tuple-element.70), channel_id=1, source_target_pairs={{0,2},{2,0},{4,6},{6,4},{8,10},{10,8},{12,14},{14,12},{16,18},{18,... | collective-permute-start | bytes 589832 | tf_op jit(solution)/shard_map/ppermute | solution.py:571
  51.5 20.2 %collective-permute-start.8 = (bf16[2,256,512]{2,1,0:T(8,128)(2,1)S(1)}, bf16[2,256,512]{2,1,0:T(8,128)(2,1)S(1)}, u32[]{:S(2)}, u32[]{:S(2)}) collective-permute-start(bf16[2,256,512]{2,1,0:T(8,128)(2,1)S(1)} %get-tuple-element.73), channel_id=1, source_target_pairs={{0,2},{2,0},{4,6},{6,4},{8,10},{10,8},{12,14},{14,12},{16,18},{18,... | collective-permute-start | bytes 1572872 | tf_op jit(solution)/shard_map/ppermute | solution.py:571
  52.0 19.7 %collective-permute-start.9 = (bf16[2,256,512]{2,1,0:T(8,128)(2,1)S(1)}, bf16[2,256,512]{2,1,0:T(8,128)(2,1)S(1)}, u32[]{:S(2)}, u32[]{:S(2)}) collective-permute-start(bf16[2,256,512]{2,1,0:T(8,128)(2,1)S(1)} %get-tuple-element.74), channel_id=1, source_target_pairs={{2,4},{6,8},{10,12},{14,16},{18,20},{22,24},{26,28},{4,2},{8,6},{1... | collective-permute-start | bytes 1572872 | tf_op jit(solution)/shard_map/ppermute | solution.py:575
  54.2 9.7 %collective-permute-start.10 = (bf16[2,48,512]{2,1,0:T(8,128)(2,1)S(1)}, bf16[2,48,512]{2,1,0:T(8,128)(2,1)S(1)}, u32[]{:S(2)}, u32[]{:S(2)}) collective-permute-start(bf16[2,48,512]{2,1,0:T(8,128)(2,1)S(1)} %get-tuple-element.76), channel_id=1, source_target_pairs={{0,8},{2,10},{4,12},{6,14},{8,0},{10,2},{12,4},{14,6},{16,24},{18,... | collective-permute-start | bytes 294920 | tf_op jit(solution)/shard_map/ppermute | solution.py:571
  63.8 7.8 %collective-permute-start.12 = (bf16[2,4,512]{2,1,0:T(4,128)(2,1)S(1)}, bf16[2,4,512]{2,1,0:T(4,128)(2,1)S(1)}, u32[]{:S(2)}, u32[]{:S(2)}) collective-permute-start(bf16[2,4,512]{2,1,0:T(4,128)(2,1)S(1)} %get-tuple-element.79), channel_id=1, source_target_pairs={{0,16},{2,18},{4,20},{6,22},{8,24},{10,26},{12,28},{14,30},{16,0},... | collective-permute-start | bytes 24584 | tf_op jit(solution)/shard_map/ppermute | solution.py:571
  64.3 7.4 %collective-permute-start.13 = (bf16[2,4,512]{2,1,0:T(4,128)(2,1)S(1)}, bf16[2,4,512]{2,1,0:T(4,128)(2,1)S(1)}, u32[]{:S(2)}, u32[]{:S(2)}) collective-permute-start(bf16[2,4,512]{2,1,0:T(4,128)(2,1)S(1)} %get-tuple-element.80), channel_id=1, source_target_pairs={{0,20},{2,22},{4,16},{6,18},{8,28},{10,30},{12,24},{14,26},{16,4},... | collective-permute-start | bytes 24584 | tf_op jit(solution)/shard_map/ppermute | solution.py:571
  66.2 5.4 %collective-permute-start.11 = (bf16[2,20,512]{2,1,0:T(8,128)(2,1)S(1)}, bf16[2,20,512]{2,1,0:T(8,128)(2,1)S(1)}, u32[]{:S(2)}, u32[]{:S(2)}) collective-permute-start(bf16[2,20,512]{2,1,0:T(8,128)(2,1)S(1)} %get-tuple-element.78), channel_id=1, source_target_pairs={{0,4},{2,6},{4,0},{6,2},{8,12},{10,14},{12,8},{14,10},{16,20},{18,... | collective-permute-start | bytes 122888 | tf_op jit(solution)/shard_map/ppermute | solution.py:571
  67.5 4.2 %copy-start.2 = (f32[8,256]{1,0:T(8,128)S(1)}, f32[8,256]{1,0:T(8,128)}, u32[]{:S(2)}) copy-start(f32[8,256]{1,0:T(8,128)} %refs_11_.1) | copy-start | bytes 24580
  67.5 4.3 %copy-start.3 = (f32[8,64]{1,0:T(8,128)S(1)}, f32[8,64]{1,0:T(8,128)}, u32[]{:S(2)}) copy-start(f32[8,64]{1,0:T(8,128)} %refs_10_.1) | copy-start | bytes 6148

commit v4 on v3

--- a/solution.py
+++ b/solution.py
@@ -20,6 +20,7 @@
 NN = (((1,), (0,)), ((), ()))
 VMEM_LIMIT = 32 * 2**20
 ANY = pl.BlockSpec(memory_space=pl.ANY)
+WHOLE = pl.BlockSpec(memory_space=pltpu.VMEM)
 
 
 def dot(a, b, dims):
@@ -54,6 +55,32 @@
 
 def is_odd():
     return lax.rem(lax.axis_index("seq"), 2)
+
+
+def split(x):
+    terms = []
+    for _ in range(3):
+        term = x.astype(BF16)
+        terms.append(term)
+        x = x - term.astype(F32)
+    return terms
+
+
+def pooling(group_w, whole_w):
+    heads = group_w.shape[0]
+    per = SEG2 // SEG1
+    lane = lax.broadcasted_iota(jnp.int32, (heads, SEG2), 1)
+    tiled = jnp.concatenate([group_w] * per, axis=1)
+    rows = [
+        jnp.where((lane >= s * SEG1) & (lane < (s + 1) * SEG1), tiled, 0.0) for s in range(per)
+    ]
+    return jnp.concatenate(rows + [whole_w], axis=0)
+
+
+def head_columns(heads, cols, depth):
+    head = lax.broadcasted_iota(jnp.int32, (heads, cols), 0)
+    col = lax.broadcasted_iota(jnp.int32, (heads, cols), 1)
+    return (col >= head * depth) & (col < (head + 1) * depth)
 
 
 def pool_body(depth, k, v, group_pool, whole_pool, groups, wholes, inner, outer, *rest):
@@ -74,22 +101,9 @@
     copies[0].wait()
     copies[1].wait()
     per = SEG2 // SEG1
-    lane = lax.broadcasted_iota(jnp.int32, (heads, SEG2), 1)
-    tiled = jnp.concatenate([group_w[...]] * per, axis=1)
-    weights = [
-        jnp.where((lane >= s * SEG1) & (lane < (s + 1) * SEG1), tiled, 0.0) for s in range(per)
-    ]
-    rest = jnp.concatenate(weights + [whole_w[...]], axis=0)
-    terms = []
-    for _ in range(3):
-        term = rest.astype(BF16)
-        terms.append(term)
-        rest = rest - term.astype(F32)
-    left = jnp.concatenate(terms, axis=0)
+    left = jnp.concatenate(split(pooling(group_w[...], whole_w[...])), axis=0)
     size = (per + 1) * heads
-    head = lax.broadcasted_iota(jnp.int32, (heads, cols), 0)
-    col = lax.broadcasted_iota(jnp.int32, (heads, cols), 1)
-    pick = (col >= head * depth) & (col < (head + 1) * depth)
+    pick = head_columns(heads, cols, depth)
     sums = [([], []), ([], [])]
     for c in range(chunks):
         for n in range(2):
@@ -193,8 +207,11 @@
     return state
 
 
-def stats_body(depth, scale, q, k, v, g, out):
-    rows, width = q.shape
+def stats_body(depth, scale, width, pair, *refs):
+    lanes = slice(pair * width, (pair + 1) * width)
+    q, k, v, g = (ref.at[:, lanes] for ref in refs[:4])
+    out = refs[4]
+    rows = q.shape[0]
     blocks = rows // BLOCK
     for h, mask in enumerate(head_masks(width, depth)):
         for b in range(blocks):
@@ -213,25 +230,27 @@
 def stats(q, k, v, g, width, depth, scale, pair):
     rows = q.shape[0]
     hp = width // depth
-    cols = pl.BlockSpec((rows, width), lambda i: (0, pair))
-    return call(
-        functools.partial(stats_body, depth, scale),
+    return call(
+        functools.partial(stats_body, depth, scale, width, pair),
         flops=2 * 2 * 3 * BLOCK * rows * width,
         moved=rows * width * 8,
-        grid=(1,),
-        in_specs=[cols] * 4,
-        out_specs=pl.BlockSpec((3, hp, rows), lambda i: (0, 0, 0)),
+        in_specs=[WHOLE] * 4,
+        out_specs=WHOLE,
         out_shape=struct((3, hp, rows), F32),
     )(q, k, v, g)
 
 
-def far_body(depth, scale, pairs, q, g, mine, theirs, *rest):
+def far_body(depth, scale, width, pairs, q, g, mine, theirs, *rest):
     partial = rest[:pairs]
-    far_k, far_v, out = rest[pairs:]
-    rows, width = q.shape
+    far_k, far_v, known = rest[pairs:]
+    rows = q.shape[0]
     slots, _, per, _ = mine.shape
     half = slots * per
     pair = pl.program_id(0)
+    lanes = pl.ds(pl.multiple_of(pair * width, width), width)
+    q, g, far_k, far_v = (ref.at[:, lanes] for ref in (q, g, far_k, far_v))
+    mine, theirs = (ref.at[:, :, :, lanes] for ref in (mine, theirs))
+    out = known.at[pair]
     for n, far in enumerate((far_k, far_v)):
         for m, src in enumerate((mine, theirs)):
             for s in range(slots):
@@ -268,27 +287,31 @@
     hp = width // depth
     slots, _, per, _ = mine.shape
     far = 2 * slots * per
-    wide = lambda n: pl.BlockSpec((n, width), lambda i: (0, i))
-    slot = pl.BlockSpec((slots, 2, per, width), lambda i: (0, 0, 0, i))
-    fixed = pl.BlockSpec((3, hp, rows), lambda i: (0, 0, 0))
-    return call(
-        functools.partial(far_body, depth, scale, pairs),
+    return call(
+        functools.partial(far_body, depth, scale, width, pairs),
         flops=4 * far * rows * cols,
         moved=rows * cols * 4,
         grid=(pairs,),
-        in_specs=[wide(rows)] * 2 + [slot] * 2 + [fixed] * pairs,
-        out_specs=[wide(far)] * 2 + [pl.BlockSpec((None, 3, hp, rows), lambda i: (i, 0, 0, 0))],
+        in_specs=[WHOLE] * (4 + pairs),
+        out_specs=[WHOLE] * 3,
         out_shape=[struct((far, cols), BF16)] * 2 + [struct((pairs, 3, hp, rows), F32)],
     )(q, g, mine, theirs, *partial)
 
 
-def remote_body(depth, scale, q, g, inner, outer, far_k, far_v, known, *rest):
-    kept, sent, inner_d, outer_d, dq_t, final = rest[:6]
-    far_kt, near_t, near_d, qs, gs = rest[6:]
-    rows, width = q.shape
+def remote_body(depth, scale, width, q, g, inner, outer, far_k, far_v, known, *rest):
+    far_kt, near_t, near_d, qs, gs, s_held, d_held = rest[6:]
+    rows = q.shape[0]
     blocks = rows // BLOCK
     half = far_k.shape[0] // 2
     masks = head_masks(width, depth)
+    pair = pl.program_id(0)
+    lanes = pl.ds(pl.multiple_of(pair * width, width), width)
+    q, g, far_k, far_v = (ref.at[:, lanes] for ref in (q, g, far_k, far_v))
+    inner, outer = (ref.at[:, :, lanes] for ref in (inner, outer))
+    kept, sent, inner_d, outer_d = (ref.at[:, :, lanes] for ref in rest[:4])
+    dq_t = rest[4].at[lanes]
+    final = rest[5].at[pair]
+    known = known.at[pair]
     far_kt[...] = (far_k[...].astype(F32) * scale).astype(BF16).T
     near_t[0] = (inner[0].astype(F32) * scale).astype(BF16).T
     near_t[1] = (outer[0].astype(F32) * scale).astype(BF16).T
@@ -308,13 +331,16 @@
     final[1] = known[2] / known[1]
     for h in range(len(masks)):
         old = None
-        for (halo, bias), r in zip(halos, places):
+        for n, ((halo, bias), r) in enumerate(zip(halos, places)):
             if old is None or blocks > 1:
                 old = [known[m, h : h + 1, r] for m in range(3)]
             s = dot(halo[0], qs[h, r], NT)
             if bias is not None:
                 s = s + bias
-            old = settle(old, merge(None, s, dot(halo[1], gs[h, r], NT)))
+            d = dot(halo[1], gs[h, r], NT)
+            s_held[2 * h + n] = s
+            d_held[2 * h + n] = d
+            old = settle(old, merge(None, s, d))
             final[0, h : h + 1, r] = old[0] + jnp.log(old[1])
             final[1, h : h + 1, r] = old[2] / old[1]
     totals = [None, None]
@@ -325,12 +351,9 @@
         parts = (dot(ds, qs[h], NN), dot(p.astype(BF16), gs[h], NN))
         totals = [new if old is None else old + new for old, new in zip(totals, parts)]
         dq_t[hr] = dot(far_kt[hr], ds, NN)
-        for n, ((halo, bias), r) in enumerate(zip(halos, places)):
-            s = dot(halo[0], qs[h, r], NT)
-            if bias is not None:
-                s = s + bias
-            p = jnp.exp(s - final[0, h : h + 1, r])
-            ds = (p * (dot(halo[1], gs[h, r], NT) - final[1, h : h + 1, r])).astype(BF16)
+        for n, r in enumerate(places):
+            p = jnp.exp(s_held[2 * h + n] - final[0, h : h + 1, r])
+            ds = (p * (d_held[2 * h + n] - final[1, h : h + 1, r])).astype(BF16)
             parts = (dot(ds, qs[h, r], NN), dot(p.astype(BF16), gs[h, r], NN))
             for m, part in enumerate(parts):
                 if h == 0:
@@ -351,29 +374,21 @@
     hp = width // depth
     far = far_k.shape[0]
     half = far // 2
-    wide = lambda n: pl.BlockSpec((n, width), lambda i: (0, i))
-    both = lambda n: pl.BlockSpec((2, n, width), lambda i: (0, 0, i))
-    row = lambda n: pl.BlockSpec((None, n, hp, rows), lambda i: (i, 0, 0, 0))
-    return call(
-        functools.partial(remote_body, depth, scale),
+    return call(
+        functools.partial(remote_body, depth, scale, width),
         flops=10 * (far * rows + 2 * BLOCK * BLOCK) * cols,
         moved=rows * cols * 8,
         grid=(pairs,),
-        in_specs=[wide(rows)] * 2 + [both(BLOCK)] * 2 + [wide(far)] * 2 + [row(3)],
-        out_specs=[
-            both(half),
-            both(half),
-            both(BLOCK),
-            both(BLOCK),
-            pl.BlockSpec((width, rows), lambda i: (i, 0)),
-            row(2),
-        ],
+        in_specs=[WHOLE] * 7,
+        out_specs=[WHOLE] * 6,
         scratch_shapes=[
             pltpu.VMEM((width, far), BF16),
             pltpu.VMEM((2, width, BLOCK), BF16),
             pltpu.VMEM((4, BLOCK, width), F32),
             pltpu.VMEM((hp, rows, width), BF16),
             pltpu.VMEM((hp, rows, width), BF16),
+            pltpu.VMEM((2 * hp, BLOCK, BLOCK), F32),
+            pltpu.VMEM((2 * hp, BLOCK, BLOCK), F32),
         ],
         out_shape=[
             struct((2, half, cols), F32),
@@ -386,9 +401,13 @@
     )(q, g, inner, outer, far_k, far_v, known)
 
 
-def local_body(depth, scale, chained, q, k, v, g, part, final, *rest):
-    dq, dk, dv, k_t, dq_t = rest[chained:]
-    rows, width = q.shape
+def local_body(depth, scale, width, pair, chained, *refs):
+    lanes = slice(pair * width, (pair + 1) * width)
+    q, k, v, g = (ref.at[:, lanes] for ref in refs[:4])
+    part = refs[4].at[lanes]
+    final = refs[5].at[pair]
+    dq, dk, dv, k_t, dq_t = refs[6 + chained :]
+    rows = q.shape[0]
     blocks = rows // BLOCK
     k_t[...] = (k[...].astype(F32) * scale).astype(BF16).T
     for h, mask in enumerate(head_masks(width, depth)):
@@ -418,22 +437,14 @@
 
 def local(q, k, v, g, part, final, before, width, depth, scale, pair):
     rows, cols = q.shape
-    hp = width // depth
-    column = pl.BlockSpec((rows, width), lambda i: (0, pair))
-    alone = pl.BlockSpec((rows, width), lambda i: (0, 0))
     extra = [] if before is None else [before]
     return call(
-        functools.partial(local_body, depth, scale, len(extra)),
+        functools.partial(local_body, depth, scale, width, pair, len(extra)),
         flops=10 * 3 * BLOCK * rows * width,
         moved=rows * width * 24,
         grid=(1,),
-        in_specs=[column] * 4
-        + [
-            pl.BlockSpec((width, rows), lambda i: (pair, 0)),
-            pl.BlockSpec((None, 2, hp, rows), lambda i: (pair, 0, 0, 0)),
-        ]
-        + [ANY] * len(extra),
-        out_specs=[column, alone, alone],
+        in_specs=[WHOLE] * 6 + [ANY] * len(extra),
+        out_specs=[pl.BlockSpec((rows, width), lambda i: (0, pair)), WHOLE, WHOLE],
         out_shape=[struct((rows, cols), BF16)] + [struct((rows, width), F32)] * 2,
         scratch_shapes=[pltpu.VMEM((width, rows), BF16), pltpu.VMEM((width, rows), F32)],
         input_output_aliases={6: 0} if extra else {},
@@ -484,7 +495,7 @@
     dk, dv = refs[:pairs], refs[pairs : 2 * pairs]
     from_inner, from_outer, group_pool, whole_pool, kept = refs[2 * pairs : 2 * pairs + 5]
     got = refs[2 * pairs + 5 : -4]
-    out_k, out_v, wide_group, wide_whole = refs[-4:]
+    out_k, out_v, left, total = refs[-4:]
     block = pl.program_id(0)
     rows, cols = kept.shape[1:]
     heads = group_pool.shape[0]
@@ -495,33 +506,23 @@
 
     @pl.when(block == 0)
     def _():
-        head = lax.broadcasted_iota(jnp.int32, (heads, cols), 0)
-        col = lax.broadcasted_iota(jnp.int32, (heads, cols), 1)
-        pick = ((col >= head * depth) & (col < (head + 1) * depth)).astype(F32)
-        for src, dst in ((group_pool, wide_group), (whole_pool, wide_whole)):
-            dst[...] = lax.dot_general(
-                src[...],
-                pick,
-                (((0,), (0,)), ((), ())),
-                precision=lax.Precision.HIGHEST,
-                preferred_element_type=F32,
-            )
+        a, b, c = (t.astype(F32) for t in split(pooling(group_pool[...], whole_pool[...])))
+        left[...] = jnp.concatenate([a, a, a, b, b, c], axis=0).T.astype(BF16)
+        for n in range(2):
+            total[n] = gathered(kept, got, n)
 
     def emit(halos):
-        index = lax.broadcasted_iota(jnp.int32, (rows, 1), 0)
+        pick = head_columns(heads, cols, depth)
         for n, (src, dst) in enumerate(((dk, out_k), (dv, out_v))):
-            sums = gathered(kept, got, n)
-            whole = jnp.sum(jnp.where(index == count1 + block, sums, 0.0), axis=0, keepdims=True)
-            for s in range(per):
-                mine = jnp.where(index == block * per + s, sums, 0.0)
-                group = jnp.sum(mine, axis=0, keepdims=True)
-                c = slice(s * SEG1, (s + 1) * SEG1)
-                piece = group * wide_group[...] + whole * wide_whole[c]
-                for halo in halos:
-                    piece = piece + halo[n, c].astype(F32)
-                for p in range(pairs):
-                    lanes = slice(p * width, (p + 1) * width)
-                    dst[c, lanes] = (piece[:, lanes] + src[p][c]).astype(BF16)
+            places = [block * per + s for s in range(per)] + [count1 + block]
+            found = [jnp.where(pick, total[n, pl.ds(at, 1)], 0.0) for at in places]
+            a, b, c = split(jnp.concatenate(found, axis=0))
+            spread = dot(left[...], jnp.concatenate([a, b, c, a, b, a], axis=0), NN)
+            for halo in halos:
+                spread = spread + halo[n].astype(F32)
+            for p in range(pairs):
+                lanes = slice(p * width, (p + 1) * width)
+                dst[:, lanes] = (spread[:, lanes] + src[p][...]).astype(BF16)
 
     if blocks == 1:
         emit((from_inner, from_outer))
@@ -550,7 +551,10 @@
         in_specs=[narrow] * (2 * pairs) + [full(x) for x in fixed],
         out_specs=[tile, tile],
         out_shape=[struct((rows, cols), BF16)] * 2,
-        scratch_shapes=[pltpu.VMEM((SEG1, cols), F32), pltpu.VMEM((SEG2, cols), F32)],
+        scratch_shapes=[
+            pltpu.VMEM((SEG2, 6 * (BLOCK // SEG1 + 1) * group_pool.shape[0]), BF16),
+            pltpu.VMEM(kept.shape, F32),
+        ],
     )(*dk, *dv, *fixed)
 
 
@@ -593,10 +597,10 @@
     for bit in far_bit:
         here.append(swap(wholes, bit))
         there.append(swap(wholes, base, bit))
-    comb, outer, inner = join([here, there], token(), [outer, inner])
+    comb, inner = join([here, there], token(), [inner])
     for bit in group_bits[1:]:
         got = swap(comb, bit)
-        (comb,) = join([comb, got], token())
+        (comb,) = join([comb, got], token() + token())
     theirs = swap(comb, 0)
     outer = cross(outer)
     inner = swap(inner, 0)

time: 76 us -> 66.5 us (0.88)
  Pallas kernels: 46 us -> 42.2 us
  waiting for transfers between devices: 3.11 us -> 0.04 us
  starting transfers between devices: 25.3 us -> 22.4 us
    ppermute x12, starting transfers between devices: 20.1 us -> 15.5 us  [swap(): return lax.ppermute(array, 'seq', [(i, i ^ mask) for i in range(devices)])]
    pallas_call x10, Pallas kernels: 39.5 us -> 36.3 us  [the longest x4 16.6 us: local(): call(functools.partial(local_body, depth, scale, width, pair, len(extra))...]
    ppermute x12, waiting for transfers between devices: 3.11 us -> 0.03 us  [swap(): return lax.ppermute(array, 'seq', [(i, i ^ mask) for i in range(devices)])]
    ppermute x2, starting transfers between devices: 5.18 us -> 6.84 us  [cross(): return lax.ppermute(array, 'seq', route + [(b, a) for a, b in route])]
  transfers between devices with their start and end apart: 14 -> 14, of which waited for: 3 -> 0; matrix products, arithmetic and copies ran while one was open for 0% -> 0% of each run, Pallas kernels for 37% -> 41%
where the time goes in v4:
time: 66.5 us; the launch traced here: 65.5 us
  Pallas kernels  42.2 us (63%)
  starting transfers between devices  22.4 us (34%)
  between operations  0.85 us (1%)
    pallas_call x4, Pallas kernels, local(): call(functools.partial(local_body, depth, scale, width, pair, len(extra))...  16.6 us
    ppermute x12, starting transfers between devices, swap(): return lax.ppermute(array, 'seq', [(i, i ^ mask) for i in range(devices)])  15.5 us
    pallas_call x1, Pallas kernels, remote(): call(functools.partial(remote_body, depth, scale, width), flops=10 * (far...  9.51 us
    pallas_call x4, Pallas kernels, stats(): call(functools.partial(stats_body, depth, scale, width, pair), flops=2 *...  6.85 us
    ppermute x2, starting transfers between devices, cross(): return lax.ppermute(array, 'seq', route + [(b, a) for a, b in route])  6.84 us
    pallas_call x1, Pallas kernels, far_stats(): call(functools.partial(far_body, depth, scale, width, pairs), flops=4 * f...  3.36 us
    pallas_call x1, Pallas kernels, pool(): call(functools.partial(pool_body, cols // heads), moved=k.size * 6, vmem=...  2.92 us
    pallas_call x1, Pallas kernels, finish(): call(functools.partial(finish_body, pairs, depth), moved=rows * cols * 12...  2.85 us
  transfers between devices with their start and end apart: 14, of which 0 were waited for; matrix products, arithmetic and copies ran while one was open for 0% of the time, Pallas kernels for 41%

profile of v4, /device:TPU:1, one launch (start us, length us, event | category | flops | bytes accessed | tf_op | source)
XLA Modules:
  0.0 65.5 jit_solution(286069281397714541)
XLA Ops:
  0.7 2.9 %shard_map.85 = (bf16[2,16,512]{2,1,0:T(8,128)(2,1)S(1)}, bf16[2,4,512]{2,1,0:T(4,128)(2,1)S(1)}, bf16[2,256,512]{2,1,0:T(8,128)(2,1)S(1)}, bf16[2,256,512]{2,1,...) custom-call(bf16[1024,512]{1,0:T(8,128)(2,1)} %k.1, bf16[1024,512]{1,0:T(8,128)(2,1)} %v.1, ...), custom_call_target="tpu_custom_call" | custom-call | bytes 3145728 | tf_op jit(solution)/shard_map/pallas_call | solution.py:135
  3.6 2.1 %collective-permute-start.1 = (bf16[2,20,512]{2,1,0:T(8,128)(2,1)S(1)}, bf16[2,20,512]{2,1,0:T(8,128)(2,1)S(1)}, u32[]{:S(2)}, u32[]{:S(2)}) collective-permute-start(bf16[2,20,512]{2,1,0:T(8,128)(2,1)S(1)} %bitcast.1), channel_id=1, source_target_pairs={{0,4},{2,6},{4,0},{6,2},{8,12},{10,14},{12,8},{14,10},{16,20},{18,... | collective-permute-start | bytes 122888 | tf_op jit(solution)/shard_map/ppermute | solution.py:575
  5.7 2.2 %collective-permute-start.2 = (bf16[2,4,512]{2,1,0:T(4,128)(2,1)S(1)}, bf16[2,4,512]{2,1,0:T(4,128)(2,1)S(1)}, u32[]{:S(2)}, u32[]{:S(2)}) collective-permute-start(bf16[2,4,512]{2,1,0:T(4,128)(2,1)S(1)} %get-tuple-element.45.refs_1_), channel_id=1, source_target_pairs={{0,20},{2,22},{4,16},{6,18},{8,28},{10,30},{12,24},{14,26},{16,4},... | collective-permute-start | bytes 24584 | tf_op jit(solution)/shard_map/ppermute | solution.py:575
  8.0 0.1 collective-permute-start
  8.0 4.5 %collective-permute-start.4 = (bf16[2,256,512]{2,1,0:T(8,128)(2,1)S(1)}, bf16[2,256,512]{2,1,0:T(8,128)(2,1)S(1)}, u32[]{:S(2)}, u32[]{:S(2)}) collective-permute-start(bf16[2,256,512]{2,1,0:T(8,128)(2,1)S(1)} %get-tuple-element.48), channel_id=1, source_target_pairs={{2,4},{6,8},{10,12},{14,16},{18,20},{22,24},{26,28},{4,2},{8,6},{1... | collective-permute-start | bytes 1572872 | tf_op jit(solution)/shard_map/ppermute | solution.py:579
  12.6 1.7 %shard_map.87.refs_6_.rest_0_ = f32[3,2,1024]{2,1,0:T(2,128)S(1)} custom-call(bf16[1024,512]{1,0:T(8,128)(2,1)S(1)} %copy-done, bf16[1024,512]{1,0:T(8,128)(2,1)S(1)} %get-tuple-element.42.refs_1_, bf16[1024,512]{1,0:T(8,128)(2,1)S(1)} %get-tuple-element.43.refs_2_, bf16[1024,512]{1,0:T(8,128)(2,1)S(1)} %copy-done.1), custom_call_target="tpu_custom_call" | custom-call | flops 402653184 | bytes 1048576 | tf_op jit(solution)/shard_map/pallas_call | solution.py:233
  14.3 0.0 collective-permute-done.refs_2_
  14.4 0.1 collective-permute-start.3
  14.5 1.4 %collective-permute-start.5 = (bf16[2,2,24,512]{3,2,1,0:T(8,128)(2,1)S(1)}, bf16[2,2,24,512]{3,2,1,0:T(8,128)(2,1)S(1)}, u32[]{:S(2)}, u32[]{:S(2)}) collective-permute-start(bf16[2,2,24,512]{3,2,1,0:T(8,128)(2,1)S(1)} %get-tuple-element.49.refs_0_), channel_id=1, source_target_pairs={{0,8},{2,10},{4,12},{6,14},{8,0},{10,2},{12,4},{14,6},{16,24},{18,... | collective-permute-start | bytes 294920 | tf_op jit(solution)/shard_map/ppermute | solution.py:575
  15.8 1.7 %shard_map.90.refs_3_.rest_2_ = f32[3,2,1024]{2,1,0:T(2,128)S(1)} custom-call(bf16[1024,512]{1,0:T(8,128)(2,1)S(1)} %copy-done, bf16[1024,512]{1,0:T(8,128)(2,1)S(1)} %get-tuple-element.42.refs_1_, bf16[1024,512]{1,0:T(8,128)(2,1)S(1)} %get-tuple-element.43.refs_2_, bf16[1024,512]{1,0:T(8,128)(2,1)S(1)} %copy-done.1), custom_call_target="tpu_custom_call" | custom-call | flops 402653184 | bytes 1048576 | tf_op jit(solution)/shard_map/pallas_call | solution.py:233
  17.5 1.7 %shard_map.89.refs_2_.rest_1_ = f32[3,2,1024]{2,1,0:T(2,128)S(1)} custom-call(bf16[1024,512]{1,0:T(8,128)(2,1)S(1)} %copy-done, bf16[1024,512]{1,0:T(8,128)(2,1)S(1)} %get-tuple-element.42.refs_1_, bf16[1024,512]{1,0:T(8,128)(2,1)S(1)} %get-tuple-element.43.refs_2_, bf16[1024,512]{1,0:T(8,128)(2,1)S(1)} %copy-done.1), custom_call_target="tpu_custom_call" | custom-call | flops 402653184 | bytes 1048576 | tf_op jit(solution)/shard_map/pallas_call | solution.py:233
  19.3 3.1 %collective-permute-start.6 = (bf16[4,2,24,512]{3,2,1,0:T(8,128)(2,1)S(1)}, bf16[4,2,24,512]{3,2,1,0:T(8,128)(2,1)S(1)}, u32[]{:S(2)}, u32[]{:S(2)}) collective-permute-start(bf16[4,2,24,512]{3,2,1,0:T(8,128)(2,1)S(1)} %shard_map.91.mine), channel_id=1, source_target_pairs={{0,2},{2,0},{4,6},{6,4},{8,10},{10,8},{12,14},{14,12},{16,18},{18,... | collective-permute-start | bytes 589832 | tf_op jit(solution)/shard_map/ppermute | solution.py:575
  22.4 1.7 %shard_map.92.rest_3_ = f32[3,2,1024]{2,1,0:T(2,128)S(1)} custom-call(bf16[1024,512]{1,0:T(8,128)(2,1)S(1)} %copy-done, bf16[1024,512]{1,0:T(8,128)(2,1)S(1)} %get-tuple-element.42.refs_1_, bf16[1024,512]{1,0:T(8,128)(2,1)S(1)} %get-tuple-element.43.refs_2_, bf16[1024,512]{1,0:T(8,128)(2,1)S(1)} %copy-done.1), custom_call_target="tpu_custom_call" | custom-call | flops 402653184 | bytes 1048576 | tf_op jit(solution)/shard_map/pallas_call | solution.py:233
  24.1 0.0 collective-permute-done.6.theirs
  24.1 3.4 %shard_map.93 = (bf16[192,512]{1,0:T(8,128)(2,1)S(1)}, bf16[192,512]{1,0:T(8,128)(2,1)S(1)}, f32[4,3,2,1024]{3,2,1,0:T(2,128)S(1)}) custom-call(bf16[1024,512]{1,0:T(8,128)(2,1)S(1)} %copy-done, bf16[1024,512]{1,0:T(8,128)(2,1)S(1)} %copy-done.1, bf16[4,2,24,512]{3,2,1,0:T(8,128)(2,1)S(1)} %shard_map.91.mine, ...), custom_call_target="tpu_custom_call" | custom-call | flops 402653184 | bytes 2097152 | tf_op jit(solution)/shard_map/pallas_call | solution.py:290
  27.5 0.0 collective-permute-done.3.inner
  27.5 9.5 %shard_map.94 = (f32[2,96,512]{2,1,0:T(8,128)S(1)}, bf16[2,96,512]{2,1,0:T(8,128)(2,1)S(1)}, bf16[2,256,512]{2,1,0:T(8,128)(2,1)S(1)}, bf16[2,256,512]{2,1,0:T(8...) custom-call(bf16[1024,512]{1,0:T(8,128)(2,1)S(1)} %copy-done, bf16[1024,512]{1,0:T(8,128)(2,1)S(1)} %copy-done.1, ...), custom_call_target="tpu_custom_call" | custom-call | flops 1677721600 | bytes 4194304 | tf_op jit(solution)/shard_map/pallas_call | solution.py:377
  37.0 0.1 collective-permute-start.7
  37.2 4.2 %shard_map.95 = (bf16[1024,512]{1,0:T(8,128)(2,1)}, f32[1024,128]{1,0:T(8,128)S(1)}, f32[1024,128]{1,0:T(8,128)S(1)}) custom-call(bf16[1024,512]{1,0:T(8,128)(2,1)S(1)} %copy-done, bf16[1024,512]{1,0:T(8,128)(2,1)S(1)} %get-tuple-element.42.refs_1_, bf16[1024,512]{1,0:T(8,128)(2,1)S(1)} %get-tuple-element.43.refs_2_, bf16[1024,512]{1,0:T(8,128)(2,1)S(1)} %copy-done.1, ...), custom_call_target="tpu_custom_call" | custom-call | flops 1006632960 | bytes 3145728 | tf_op jit(solution)/shard_map/pallas_call | solution.py:441
  41.3 0.0 collective-permute-done.7.rest_0_
  41.4 0.5 collective-permute-start.8
  41.9 2.3 %collective-permute-start.9 = (bf16[2,256,512]{2,1,0:T(8,128)(2,1)S(1)}, bf16[2,256,512]{2,1,0:T(8,128)(2,1)S(1)}, u32[]{:S(2)}, u32[]{:S(2)}) collective-permute-start(bf16[2,256,512]{2,1,0:T(8,128)(2,1)S(1)} %get-tuple-element.72), channel_id=1, source_target_pairs={{2,4},{6,8},{10,12},{14,16},{18,20},{22,24},{26,28},{4,2},{8,6},{1... | collective-permute-start | bytes 1572872 | tf_op jit(solution)/shard_map/ppermute | solution.py:579
  44.2 2.3 %collective-permute-start.10 = (bf16[2,48,512]{2,1,0:T(8,128)(2,1)S(1)}, bf16[2,48,512]{2,1,0:T(8,128)(2,1)S(1)}, u32[]{:S(2)}, u32[]{:S(2)}) collective-permute-start(bf16[2,48,512]{2,1,0:T(8,128)(2,1)S(1)} %get-tuple-element.74), channel_id=1, source_target_pairs={{0,8},{2,10},{4,12},{6,14},{8,0},{10,2},{12,4},{14,6},{16,24},{18,... | collective-permute-start | bytes 294920 | tf_op jit(solution)/shard_map/ppermute | solution.py:575
  46.5 4.1 %shard_map.96 = (bf16[1024,512]{1,0:T(8,128)(2,1)}, f32[1024,128]{1,0:T(8,128)S(1)}, f32[1024,128]{1,0:T(8,128)S(1)}) custom-call(bf16[1024,512]{1,0:T(8,128)(2,1)S(1)} %copy-done, bf16[1024,512]{1,0:T(8,128)(2,1)S(1)} %get-tuple-element.42.refs_1_, bf16[1024,512]{1,0:T(8,128)(2,1)S(1)} %get-tuple-element.43.refs_2_, ...), custom_call_target="tpu_custom_call", output_to_operand_aliasing={{0}: (6, {})} | custom-call | flops 1006632960 | bytes 3145728 | tf_op jit(solution)/shard_map/pallas_call | solution.py:441
  50.6 4.1 %shard_map.97 = (bf16[1024,512]{1,0:T(8,128)(2,1)}, f32[1024,128]{1,0:T(8,128)S(1)}, f32[1024,128]{1,0:T(8,128)S(1)}) custom-call(bf16[1024,512]{1,0:T(8,128)(2,1)S(1)} %copy-done, bf16[1024,512]{1,0:T(8,128)(2,1)S(1)} %get-tuple-element.42.refs_1_, bf16[1024,512]{1,0:T(8,128)(2,1)S(1)} %get-tuple-element.43.refs_2_, ...), custom_call_target="tpu_custom_call", output_to_operand_aliasing={{0}: (6, {})} | custom-call | flops 1006632960 | bytes 3145728 | tf_op jit(solution)/shard_map/pallas_call | solution.py:441
  54.8 2.1 %collective-permute-start.12 = (bf16[2,4,512]{2,1,0:T(4,128)(2,1)S(1)}, bf16[2,4,512]{2,1,0:T(4,128)(2,1)S(1)}, u32[]{:S(2)}, u32[]{:S(2)}) collective-permute-start(bf16[2,4,512]{2,1,0:T(4,128)(2,1)S(1)} %get-tuple-element.77), channel_id=1, source_target_pairs={{0,16},{2,18},{4,20},{6,22},{8,24},{10,26},{12,28},{14,30},{16,0},... | collective-permute-start | bytes 24584 | tf_op jit(solution)/shard_map/ppermute | solution.py:575
  56.9 1.4 %collective-permute-start.13 = (bf16[2,4,512]{2,1,0:T(4,128)(2,1)S(1)}, bf16[2,4,512]{2,1,0:T(4,128)(2,1)S(1)}, u32[]{:S(2)}, u32[]{:S(2)}) collective-permute-start(bf16[2,4,512]{2,1,0:T(4,128)(2,1)S(1)} %get-tuple-element.78), channel_id=1, source_target_pairs={{0,20},{2,22},{4,16},{6,18},{8,28},{10,30},{12,24},{14,26},{16,4},... | collective-permute-start | bytes 24584 | tf_op jit(solution)/shard_map/ppermute | solution.py:575
  58.3 0.1 collective-permute-start.11
  58.4 4.2 %shard_map.98 = (bf16[1024,512]{1,0:T(8,128)(2,1)}, f32[1024,128]{1,0:T(8,128)S(1)}, f32[1024,128]{1,0:T(8,128)S(1)}) custom-call(bf16[1024,512]{1,0:T(8,128)(2,1)S(1)} %copy-done, bf16[1024,512]{1,0:T(8,128)(2,1)S(1)} %get-tuple-element.42.refs_1_, bf16[1024,512]{1,0:T(8,128)(2,1)S(1)} %get-tuple-element.43.refs_2_, ...), custom_call_target="tpu_custom_call", output_to_operand_aliasing={{0}: (6, {})} | custom-call | flops 1006632960 | bytes 3145728 | tf_op jit(solution)/shard_map/pallas_call | solution.py:441
  62.6 0.0 collective-permute-done.8.refs_8_
  62.6 0.0 collective-permute-done.9.refs_9_
  62.6 2.8 %shard_map.101 = (bf16[1024,512]{1,0:T(8,128)(2,1)}, bf16[1024,512]{1,0:T(8,128)(2,1)}) custom-call(f32[1024,128]{1,0:T(8,128)S(1)} %get-tuple-element.59.rest_3_.refs_0_, f32[1024,128]{1,0:T(8,128)S(1)} %get-tuple-element.60.refs_1_, f32[1024,128]{1,0:T(8,128)S(1)} %get-tuple-element.61.rest_1_.refs_2_, f32[1024,128]{1,0:T(8,128)S(1)} %get-tuple-element.62.refs_3_, ...), custom_call_target="tpu_custom_call" | custom-call | bytes 6291456 | tf_op jit(solution)/shard_map/pallas_call | solution.py:547
  (21 shorter events, 0.1 us)
Async XLA Ops:
  0.6 12.0 %copy-start.1 = (bf16[1024,512]{1,0:T(8,128)(2,1)S(1)}, bf16[1024,512]{1,0:T(8,128)(2,1)}, u32[]{:S(2)}) copy-start(bf16[1024,512]{1,0:T(8,128)(2,1)} %refs_3_.15) | copy-start | bytes 3145732
  0.6 12.0 %copy-start = (bf16[1024,512]{1,0:T(8,128)(2,1)S(1)}, bf16[1024,512]{1,0:T(8,128)(2,1)}, u32[]{:S(2)}) copy-start(bf16[1024,512]{1,0:T(8,128)(2,1)} %refs_0_.15) | copy-start | bytes 3145732
  3.6 10.7 %collective-permute-start.1 = (bf16[2,20,512]{2,1,0:T(8,128)(2,1)S(1)}, bf16[2,20,512]{2,1,0:T(8,128)(2,1)S(1)}, u32[]{:S(2)}, u32[]{:S(2)}) collective-permute-start(bf16[2,20,512]{2,1,0:T(8,128)(2,1)S(1)} %bitcast.1), channel_id=1, source_target_pairs={{0,4},{2,6},{4,0},{6,2},{8,12},{10,14},{12,8},{14,10},{16,20},{18,... | collective-permute-start | bytes 122888 | tf_op jit(solution)/shard_map/ppermute | solution.py:575
  5.7 8.6 %collective-permute-start.2 = (bf16[2,4,512]{2,1,0:T(4,128)(2,1)S(1)}, bf16[2,4,512]{2,1,0:T(4,128)(2,1)S(1)}, u32[]{:S(2)}, u32[]{:S(2)}) collective-permute-start(bf16[2,4,512]{2,1,0:T(4,128)(2,1)S(1)} %get-tuple-element.45.refs_1_), channel_id=1, source_target_pairs={{0,20},{2,22},{4,16},{6,18},{8,28},{10,30},{12,24},{14,26},{16,4},... | collective-permute-start | bytes 24584 | tf_op jit(solution)/shard_map/ppermute | solution.py:575
  8.0 6.4 %collective-permute-start = (bf16[2,4,512]{2,1,0:T(4,128)(2,1)S(1)}, bf16[2,4,512]{2,1,0:T(4,128)(2,1)S(1)}, u32[]{:S(2)}, u32[]{:S(2)}) collective-permute-start(bf16[2,4,512]{2,1,0:T(4,128)(2,1)S(1)} %get-tuple-element.45.refs_1_), channel_id=1, source_target_pairs={{0,16},{2,18},{4,20},{6,22},{8,24},{10,26},{12,28},{14,30},{16,0},... | collective-permute-start | bytes 24584 | tf_op jit(solution)/shard_map/ppermute | solution.py:575
  8.0 19.5 %collective-permute-start.4 = (bf16[2,256,512]{2,1,0:T(8,128)(2,1)S(1)}, bf16[2,256,512]{2,1,0:T(8,128)(2,1)S(1)}, u32[]{:S(2)}, u32[]{:S(2)}) collective-permute-start(bf16[2,256,512]{2,1,0:T(8,128)(2,1)S(1)} %get-tuple-element.48), channel_id=1, source_target_pairs={{2,4},{6,8},{10,12},{14,16},{18,20},{22,24},{26,28},{4,2},{8,6},{1... | collective-permute-start | bytes 1572872 | tf_op jit(solution)/shard_map/ppermute | solution.py:579
  14.4 13.1 %collective-permute-start.3 = (bf16[2,256,512]{2,1,0:T(8,128)(2,1)S(1)}, bf16[2,256,512]{2,1,0:T(8,128)(2,1)S(1)}, u32[]{:S(2)}, u32[]{:S(2)}) collective-permute-start(bf16[2,256,512]{2,1,0:T(8,128)(2,1)S(1)} %get-tuple-element.47), channel_id=1, source_target_pairs={{0,2},{2,0},{4,6},{6,4},{8,10},{10,8},{12,14},{14,12},{16,18},{18,... | collective-permute-start | bytes 1572872 | tf_op jit(solution)/shard_map/ppermute | solution.py:575
  14.5 4.8 %collective-permute-start.5 = (bf16[2,2,24,512]{3,2,1,0:T(8,128)(2,1)S(1)}, bf16[2,2,24,512]{3,2,1,0:T(8,128)(2,1)S(1)}, u32[]{:S(2)}, u32[]{:S(2)}) collective-permute-start(bf16[2,2,24,512]{3,2,1,0:T(8,128)(2,1)S(1)} %get-tuple-element.49.refs_0_), channel_id=1, source_target_pairs={{0,8},{2,10},{4,12},{6,14},{8,0},{10,2},{12,4},{14,6},{16,24},{18,... | collective-permute-start | bytes 294920 | tf_op jit(solution)/shard_map/ppermute | solution.py:575
  19.3 4.9 %collective-permute-start.6 = (bf16[4,2,24,512]{3,2,1,0:T(8,128)(2,1)S(1)}, bf16[4,2,24,512]{3,2,1,0:T(8,128)(2,1)S(1)}, u32[]{:S(2)}, u32[]{:S(2)}) collective-permute-start(bf16[4,2,24,512]{3,2,1,0:T(8,128)(2,1)S(1)} %shard_map.91.mine), channel_id=1, source_target_pairs={{0,2},{2,0},{4,6},{6,4},{8,10},{10,8},{12,14},{14,12},{16,18},{18,... | collective-permute-start | bytes 589832 | tf_op jit(solution)/shard_map/ppermute | solution.py:575
  37.0 4.3 %collective-permute-start.7 = (bf16[2,96,512]{2,1,0:T(8,128)(2,1)S(1)}, bf16[2,96,512]{2,1,0:T(8,128)(2,1)S(1)}, u32[]{:S(2)}, u32[]{:S(2)}) collective-permute-start(bf16[2,96,512]{2,1,0:T(8,128)(2,1)S(1)} %get-tuple-element.68), channel_id=1, source_target_pairs={{0,2},{2,0},{4,6},{6,4},{8,10},{10,8},{12,14},{14,12},{16,18},{18,... | collective-permute-start | bytes 589832 | tf_op jit(solution)/shard_map/ppermute | solution.py:575
  41.4 21.2 %collective-permute-start.8 = (bf16[2,256,512]{2,1,0:T(8,128)(2,1)S(1)}, bf16[2,256,512]{2,1,0:T(8,128)(2,1)S(1)}, u32[]{:S(2)}, u32[]{:S(2)}) collective-permute-start(bf16[2,256,512]{2,1,0:T(8,128)(2,1)S(1)} %get-tuple-element.71), channel_id=1, source_target_pairs={{0,2},{2,0},{4,6},{6,4},{8,10},{10,8},{12,14},{14,12},{16,18},{18,... | collective-permute-start | bytes 1572872 | tf_op jit(solution)/shard_map/ppermute | solution.py:575
  41.9 20.7 %collective-permute-start.9 = (bf16[2,256,512]{2,1,0:T(8,128)(2,1)S(1)}, bf16[2,256,512]{2,1,0:T(8,128)(2,1)S(1)}, u32[]{:S(2)}, u32[]{:S(2)}) collective-permute-start(bf16[2,256,512]{2,1,0:T(8,128)(2,1)S(1)} %get-tuple-element.72), channel_id=1, source_target_pairs={{2,4},{6,8},{10,12},{14,16},{18,20},{22,24},{26,28},{4,2},{8,6},{1... | collective-permute-start | bytes 1572872 | tf_op jit(solution)/shard_map/ppermute | solution.py:579
  44.2 10.6 %collective-permute-start.10 = (bf16[2,48,512]{2,1,0:T(8,128)(2,1)S(1)}, bf16[2,48,512]{2,1,0:T(8,128)(2,1)S(1)}, u32[]{:S(2)}, u32[]{:S(2)}) collective-permute-start(bf16[2,48,512]{2,1,0:T(8,128)(2,1)S(1)} %get-tuple-element.74), channel_id=1, source_target_pairs={{0,8},{2,10},{4,12},{6,14},{8,0},{10,2},{12,4},{14,6},{16,24},{18,... | collective-permute-start | bytes 294920 | tf_op jit(solution)/shard_map/ppermute | solution.py:575
  54.8 7.8 %collective-permute-start.12 = (bf16[2,4,512]{2,1,0:T(4,128)(2,1)S(1)}, bf16[2,4,512]{2,1,0:T(4,128)(2,1)S(1)}, u32[]{:S(2)}, u32[]{:S(2)}) collective-permute-start(bf16[2,4,512]{2,1,0:T(4,128)(2,1)S(1)} %get-tuple-element.77), channel_id=1, source_target_pairs={{0,16},{2,18},{4,20},{6,22},{8,24},{10,26},{12,28},{14,30},{16,0},... | collective-permute-start | bytes 24584 | tf_op jit(solution)/shard_map/ppermute | solution.py:575
  56.9 5.7 %collective-permute-start.13 = (bf16[2,4,512]{2,1,0:T(4,128)(2,1)S(1)}, bf16[2,4,512]{2,1,0:T(4,128)(2,1)S(1)}, u32[]{:S(2)}, u32[]{:S(2)}) collective-permute-start(bf16[2,4,512]{2,1,0:T(4,128)(2,1)S(1)} %get-tuple-element.78), channel_id=1, source_target_pairs={{0,20},{2,22},{4,16},{6,18},{8,28},{10,30},{12,24},{14,26},{16,4},... | collective-permute-start | bytes 24584 | tf_op jit(solution)/shard_map/ppermute | solution.py:575
  58.3 4.3 %collective-permute-start.11 = (bf16[2,20,512]{2,1,0:T(8,128)(2,1)S(1)}, bf16[2,20,512]{2,1,0:T(8,128)(2,1)S(1)}, u32[]{:S(2)}, u32[]{:S(2)}) collective-permute-start(bf16[2,20,512]{2,1,0:T(8,128)(2,1)S(1)} %get-tuple-element.76), channel_id=1, source_target_pairs={{0,4},{2,6},{4,0},{6,2},{8,12},{10,14},{12,8},{14,10},{16,20},{18,... | collective-permute-start | bytes 122888 | tf_op jit(solution)/shard_map/ppermute | solution.py:575
  58.4 4.2 %copy-start.2 = (f32[8,256]{1,0:T(8,128)S(1)}, f32[8,256]{1,0:T(8,128)}, u32[]{:S(2)}) copy-start(f32[8,256]{1,0:T(8,128)} %refs_11_.1) | copy-start | bytes 24580
  58.4 4.2 %copy-start.3 = (f32[8,64]{1,0:T(8,128)S(1)}, f32[8,64]{1,0:T(8,128)}, u32[]{:S(2)}) copy-start(f32[8,64]{1,0:T(8,128)} %refs_10_.1) | copy-start | bytes 6148

commit v5 on v4

--- a/solution.py
+++ b/solution.py
@@ -20,6 +20,7 @@
 NN = (((1,), (0,)), ((), ()))
 VMEM_LIMIT = 32 * 2**20
 ANY = pl.BlockSpec(memory_space=pl.ANY)
+HBM = pl.BlockSpec(memory_space=pltpu.HBM)
 WHOLE = pl.BlockSpec(memory_space=pltpu.VMEM)
 
 
@@ -406,7 +407,12 @@
     q, k, v, g = (ref.at[:, lanes] for ref in refs[:4])
     part = refs[4].at[lanes]
     final = refs[5].at[pair]
-    dq, dk, dv, k_t, dq_t = refs[6 + chained :]
+    dq, dk, dv, *rest = refs[6 + chained :]
+    k_t, dq_t = rest[chained > 0 :][:2]
+    if chained:
+        earlier = slice((pair - 1) * width, pair * width)
+        copy = pltpu.make_async_copy(refs[6], rest[0].at[:, earlier], rest[3])
+        copy.start()
     rows = q.shape[0]
     blocks = rows // BLOCK
     k_t[...] = (k[...].astype(F32) * scale).astype(BF16).T
@@ -433,22 +439,25 @@
                     dk[rj] += k_part[here]
             dq_t[hr, r] = part[hr, r] + dot(k_t[hr, c], ds, NN)
     dq[...] = dq_t[...].T.astype(BF16)
-
-
-def local(q, k, v, g, part, final, before, width, depth, scale, pair):
+    if chained:
+        copy.wait()
+
+
+def local(q, k, v, g, part, final, earlier, width, depth, scale, pair):
     rows, cols = q.shape
-    extra = [] if before is None else [before]
-    return call(
-        functools.partial(local_body, depth, scale, width, pair, len(extra)),
+    chained = len(earlier)
+    tile, wide = struct((rows, width), BF16), struct((rows, width), F32)
+    return call(
+        functools.partial(local_body, depth, scale, width, pair, chained),
         flops=10 * 3 * BLOCK * rows * width,
         moved=rows * width * 24,
-        grid=(1,),
-        in_specs=[WHOLE] * 6 + [ANY] * len(extra),
-        out_specs=[pl.BlockSpec((rows, width), lambda i: (0, pair)), WHOLE, WHOLE],
-        out_shape=[struct((rows, cols), BF16)] + [struct((rows, width), F32)] * 2,
-        scratch_shapes=[pltpu.VMEM((width, rows), BF16), pltpu.VMEM((width, rows), F32)],
-        input_output_aliases={6: 0} if extra else {},
-    )(q, k, v, g, part, final, *extra)
+        in_specs=[WHOLE] * 6 + [WHOLE, ANY][:chained],
+        out_specs=[WHOLE] * 3 + [HBM] * (chained > 0),
+        out_shape=[tile, wide, wide] + [struct((rows, cols), BF16)] * (chained > 0),
+        scratch_shapes=[pltpu.VMEM((width, rows), BF16), pltpu.VMEM((width, rows), F32)]
+        + [pltpu.SemaphoreType.DMA] * (chained > 0),
+        input_output_aliases={7: 3} if chained == 2 else {},
+    )(q, k, v, g, part, final, *earlier)
 
 
 def gathered(kept, got, n):
@@ -491,12 +500,16 @@
     )(kept, *got, *extra)
 
 
-def finish_body(pairs, depth, *refs):
+def finish_body(pairs, depth, count, *refs):
     dk, dv = refs[:pairs], refs[pairs : 2 * pairs]
     from_inner, from_outer, group_pool, whole_pool, kept = refs[2 * pairs : 2 * pairs + 5]
-    got = refs[2 * pairs + 5 : -4]
-    out_k, out_v, left, total = refs[-4:]
+    got = refs[2 * pairs + 5 : 2 * pairs + 5 + count]
+    tile = refs[2 * pairs + 5 + count]
+    out_k, out_v, out_q, left, total, sem = refs[-6:]
     block = pl.program_id(0)
+    last = slice((pairs - 1) * tile.shape[1], pairs * tile.shape[1])
+    copy = pltpu.make_async_copy(tile, out_q.at[:, last], sem)
+    pl.when(block == 0)(copy.start)
     rows, cols = kept.shape[1:]
     heads = group_pool.shape[0]
     width = dk[0].shape[1]
@@ -526,6 +539,7 @@
 
     if blocks == 1:
         emit((from_inner, from_outer))
+        copy.wait()
         return
     odd = is_odd()
     at_inner = block == (1 - odd) * (blocks - 1)
@@ -533,29 +547,34 @@
     pl.when(at_inner)(lambda: emit((from_inner,)))
     pl.when(at_outer)(lambda: emit((from_outer,)))
     pl.when(jnp.logical_not(at_inner | at_outer))(lambda: emit(()))
-
-
-def finish(dk, dv, from_inner, from_outer, kept, got, group_pool, whole_pool):
+    pl.when(block == blocks - 1)(copy.wait)
+
+
+def finish(dk, dv, from_inner, from_outer, kept, got, group_pool, whole_pool, earlier):
     rows, width = dk[0].shape
     pairs = len(dk)
     cols = width * pairs
     depth = cols // group_pool.shape[0]
-    tile = pl.BlockSpec((BLOCK, cols), lambda i: (i, 0))
+    out = pl.BlockSpec((BLOCK, cols), lambda i: (i, 0))
     narrow = pl.BlockSpec((BLOCK, width), lambda i: (i, 0))
-    full = lambda x: pl.BlockSpec(x.shape, lambda i: (0,) * x.ndim)
     fixed = [from_inner, from_outer, group_pool, whole_pool, kept] + list(got)
-    return call(
-        functools.partial(finish_body, pairs, depth),
+    place = 2 * pairs + len(fixed) + 1
+    return call(
+        functools.partial(finish_body, pairs, depth, len(got)),
         moved=rows * cols * 12,
         grid=(rows // BLOCK,),
-        in_specs=[narrow] * (2 * pairs) + [full(x) for x in fixed],
-        out_specs=[tile, tile],
-        out_shape=[struct((rows, cols), BF16)] * 2,
+        in_specs=[narrow] * (2 * pairs)
+        + [WHOLE] * (len(fixed) + 1)
+        + [ANY] * (len(earlier) - 1),
+        out_specs=[out, out, HBM],
+        out_shape=[struct((rows, cols), BF16)] * 3,
         scratch_shapes=[
             pltpu.VMEM((SEG2, 6 * (BLOCK // SEG1 + 1) * group_pool.shape[0]), BF16),
             pltpu.VMEM(kept.shape, F32),
+            pltpu.SemaphoreType.DMA,
         ],
-    )(*dk, *dv, *fixed)
+        input_output_aliases={place: 2} if len(earlier) == 2 else {},
+    )(*dk, *dv, *fixed, *earlier)
 
 
 def shards(query, key, value, out_grad, pool_group, pool_global):
@@ -613,15 +632,16 @@
     )
     got = [swap(sent, 0)]
 
-    query_grad, dk, dv = None, [], []
+    earlier, dk, dv = [], [], []
 
     def step():
-        nonlocal query_grad
+        nonlocal earlier
         if len(dk) == pairs:
             return []
-        query_grad, a, b = local(
-            query, key, value, out_grad, dq_t, final, query_grad, width, depth, scale, len(dk)
+        tile, a, b, *rest = local(
+            query, key, value, out_grad, dq_t, final, earlier, width, depth, scale, len(dk)
         )
+        earlier = [tile] + rest
         dk.append(a)
         dv.append(b)
         return [a]
@@ -657,8 +677,8 @@
         got = [swap(sent, bit)]
     while len(dk) < pairs:
         step()
-    key_grad, value_grad = finish(
-        dk, dv, from_inner, from_outer, kept, got, pool_group, pool_global
+    key_grad, value_grad, query_grad = finish(
+        dk, dv, from_inner, from_outer, kept, got, pool_group, pool_global, earlier
     )
     return (query_grad, key_grad, value_grad)
 

time: 66.5 us -> 65.6 us (0.986)
  the two profiles are of different devices: /device:TPU:1 before, /device:TPU:0 now
where the time goes in v5:
time: 65.6 us; the launch traced here: 65.5 us
  Pallas kernels  40.2 us (61%)
  starting transfers between devices  18 us (27%)
  waiting for transfers between devices  6.17 us (9%)
  between operations  1.04 us (2%)
    ppermute x12, starting transfers between devices, swap(): return lax.ppermute(array, 'seq', [(i, i ^ mask) for i in range(devices)])  16.5 us
    pallas_call x4, Pallas kernels, local(): call(functools.partial(local_body, depth, scale, width, pair, chained), f...  14.5 us
    pallas_call x1, Pallas kernels, remote(): call(functools.partial(remote_body, depth, scale, width), flops=10 * (far...  9.55 us
    pallas_call x4, Pallas kernels, stats(): call(functools.partial(stats_body, depth, scale, width, pair), flops=2 *...  6.85 us
    ppermute x12, waiting for transfers between devices, swap(): return lax.ppermute(array, 'seq', [(i, i ^ mask) for i in range(devices)])  6.17 us
    pallas_call x1, Pallas kernels, far_stats(): call(functools.partial(far_body, depth, scale, width, pairs), flops=4 * f...  3.36 us
    pallas_call x1, Pallas kernels, pool(): call(functools.partial(pool_body, cols // heads), moved=k.size * 6, vmem=...  2.93 us
    pallas_call x1, Pallas kernels, finish(): call(functools.partial(finish_body, pairs, depth, len(got)), moved=rows *...  2.87 us
  transfers between devices with their start and end apart: 14, of which 4 were waited for; matrix products, arithmetic and copies ran while one was open for 0% of the time, Pallas kernels for 38%

profile of v5, /device:TPU:0, one launch (start us, length us, event | category | flops | bytes accessed | tf_op | source)
XLA Modules:
  0.0 65.5 jit_solution(10992363683281653401)
XLA Ops:
  0.7 2.9 %shard_map.85 = (bf16[2,16,512]{2,1,0:T(8,128)(2,1)S(1)}, bf16[2,4,512]{2,1,0:T(4,128)(2,1)S(1)}, bf16[2,256,512]{2,1,0:T(8,128)(2,1)S(1)}, bf16[2,256,512]{2,1,...) custom-call(bf16[1024,512]{1,0:T(8,128)(2,1)} %k.1, bf16[1024,512]{1,0:T(8,128)(2,1)} %v.1, ...), custom_call_target="tpu_custom_call" | custom-call | bytes 3145728 | tf_op jit(solution)/shard_map/pallas_call | solution.py:136
  3.6 3.1 %collective-permute-start.1 = (bf16[2,20,512]{2,1,0:T(8,128)(2,1)S(1)}, bf16[2,20,512]{2,1,0:T(8,128)(2,1)S(1)}, u32[]{:S(2)}, u32[]{:S(2)}) collective-permute-start(bf16[2,20,512]{2,1,0:T(8,128)(2,1)S(1)} %bitcast.1), channel_id=1, source_target_pairs={{0,4},{2,6},{4,0},{6,2},{8,12},{10,14},{12,8},{14,10},{16,20},{18,... | collective-permute-start | bytes 122888 | tf_op jit(solution)/shard_map/ppermute | solution.py:594
  6.7 2.5 %collective-permute-start.2 = (bf16[2,4,512]{2,1,0:T(4,128)(2,1)S(1)}, bf16[2,4,512]{2,1,0:T(4,128)(2,1)S(1)}, u32[]{:S(2)}, u32[]{:S(2)}) collective-permute-start(bf16[2,4,512]{2,1,0:T(4,128)(2,1)S(1)} %get-tuple-element.49.refs_1_), channel_id=1, source_target_pairs={{0,20},{2,22},{4,16},{6,18},{8,28},{10,30},{12,24},{14,26},{16,4},... | collective-permute-start | bytes 24584 | tf_op jit(solution)/shard_map/ppermute | solution.py:594
  9.2 0.1 collective-permute-start
  9.3 0.7 %collective-permute-start.4 = (bf16[2,256,512]{2,1,0:T(8,128)(2,1)S(1)}, bf16[2,256,512]{2,1,0:T(8,128)(2,1)S(1)}, u32[]{:S(2)}, u32[]{:S(2)}) collective-permute-start(bf16[2,256,512]{2,1,0:T(8,128)(2,1)S(1)} %get-tuple-element.52), channel_id=1, source_target_pairs={{2,4},{6,8},{10,12},{14,16},{18,20},{22,24},{26,28},{4,2},{8,6},{1... | collective-permute-start | bytes 1572872 | tf_op jit(solution)/shard_map/ppermute | solution.py:598
  10.0 1.7 %shard_map.87.refs_6_.rest_0_ = f32[3,2,1024]{2,1,0:T(2,128)S(1)} custom-call(bf16[1024,512]{1,0:T(8,128)(2,1)S(1)} %copy-done, bf16[1024,512]{1,0:T(8,128)(2,1)S(1)} %get-tuple-element.46.refs_1_, bf16[1024,512]{1,0:T(8,128)(2,1)S(1)} %get-tuple-element.47.refs_2_, bf16[1024,512]{1,0:T(8,128)(2,1)S(1)} %copy-done.1), custom_call_target="tpu_custom_call" | custom-call | flops 402653184 | bytes 1048576 | tf_op jit(solution)/shard_map/pallas_call | solution.py:234
  11.7 0.4 collective-permute-done.2.refs_4_
  12.1 1.6 %collective-permute-done.refs_2_ = bf16[2,4,512]{2,1,0:T(4,128)(2,1)S(1)} collective-permute-done((bf16[2,4,512]{2,1,0:T(4,128)(2,1)S(1)}, bf16[2,4,512]{2,1,0:T(4,128)(2,1)S(1)}, u32[]{:S(2)}, u32[]{:S(2)}) %collective-permute-start) | collective-permute-done | bytes 8224 | tf_op jit(solution)/shard_map/ppermute | solution.py:594
  13.8 1.2 %collective-permute-start.3 = (bf16[2,256,512]{2,1,0:T(8,128)(2,1)S(1)}, bf16[2,256,512]{2,1,0:T(8,128)(2,1)S(1)}, u32[]{:S(2)}, u32[]{:S(2)}) collective-permute-start(bf16[2,256,512]{2,1,0:T(8,128)(2,1)S(1)} %get-tuple-element.51), channel_id=1, source_target_pairs={{0,2},{2,0},{4,6},{6,4},{8,10},{10,8},{12,14},{14,12},{16,18},{18,... | collective-permute-start | bytes 1572872 | tf_op jit(solution)/shard_map/ppermute | solution.py:594
  14.9 1.6 %collective-permute-start.5 = (bf16[2,2,24,512]{3,2,1,0:T(8,128)(2,1)S(1)}, bf16[2,2,24,512]{3,2,1,0:T(8,128)(2,1)S(1)}, u32[]{:S(2)}, u32[]{:S(2)}) collective-permute-start(bf16[2,2,24,512]{3,2,1,0:T(8,128)(2,1)S(1)} %get-tuple-element.53.refs_0_), channel_id=1, source_target_pairs={{0,8},{2,10},{4,12},{6,14},{8,0},{10,2},{12,4},{14,6},{16,24},{18,... | collective-permute-start | bytes 294920 | tf_op jit(solution)/shard_map/ppermute | solution.py:594
  16.5 1.7 %shard_map.90.refs_3_.rest_2_ = f32[3,2,1024]{2,1,0:T(2,128)S(1)} custom-call(bf16[1024,512]{1,0:T(8,128)(2,1)S(1)} %copy-done, bf16[1024,512]{1,0:T(8,128)(2,1)S(1)} %get-tuple-element.46.refs_1_, bf16[1024,512]{1,0:T(8,128)(2,1)S(1)} %get-tuple-element.47.refs_2_, bf16[1024,512]{1,0:T(8,128)(2,1)S(1)} %copy-done.1), custom_call_target="tpu_custom_call" | custom-call | flops 402653184 | bytes 1048576 | tf_op jit(solution)/shard_map/pallas_call | solution.py:234
  18.2 1.7 %shard_map.89.refs_2_.rest_1_ = f32[3,2,1024]{2,1,0:T(2,128)S(1)} custom-call(bf16[1024,512]{1,0:T(8,128)(2,1)S(1)} %copy-done, bf16[1024,512]{1,0:T(8,128)(2,1)S(1)} %get-tuple-element.46.refs_1_, bf16[1024,512]{1,0:T(8,128)(2,1)S(1)} %get-tuple-element.47.refs_2_, bf16[1024,512]{1,0:T(8,128)(2,1)S(1)} %copy-done.1), custom_call_target="tpu_custom_call" | custom-call | flops 402653184 | bytes 1048576 | tf_op jit(solution)/shard_map/pallas_call | solution.py:234
  19.9 2.4 %collective-permute-done.5.refs_1_ = bf16[2,2,24,512]{3,2,1,0:T(8,128)(2,1)S(1)} collective-permute-done((bf16[2,2,24,512]{3,2,1,0:T(8,128)(2,1)S(1)}, bf16[2,2,24,512]{3,2,1,0:T(8,128)(2,1)S(1)}, u32[]{:S(2)}, u32[]{:S(2)}) %collective-permute-start.5) | collective-permute-done | bytes 98336 | tf_op jit(solution)/shard_map/ppermute | solution.py:594
  22.3 0.1 collective-permute-start.6
  22.4 1.7 %shard_map.92.rest_3_ = f32[3,2,1024]{2,1,0:T(2,128)S(1)} custom-call(bf16[1024,512]{1,0:T(8,128)(2,1)S(1)} %copy-done, bf16[1024,512]{1,0:T(8,128)(2,1)S(1)} %get-tuple-element.46.refs_1_, bf16[1024,512]{1,0:T(8,128)(2,1)S(1)} %get-tuple-element.47.refs_2_, bf16[1024,512]{1,0:T(8,128)(2,1)S(1)} %copy-done.1), custom_call_target="tpu_custom_call" | custom-call | flops 402653184 | bytes 1048576 | tf_op jit(solution)/shard_map/pallas_call | solution.py:234
  24.1 0.0 collective-permute-done.6.theirs
  24.1 3.4 %shard_map.93 = (bf16[192,512]{1,0:T(8,128)(2,1)S(1)}, bf16[192,512]{1,0:T(8,128)(2,1)S(1)}, f32[4,3,2,1024]{3,2,1,0:T(2,128)S(1)}) custom-call(bf16[1024,512]{1,0:T(8,128)(2,1)S(1)} %copy-done, bf16[1024,512]{1,0:T(8,128)(2,1)S(1)} %copy-done.1, bf16[4,2,24,512]{3,2,1,0:T(8,128)(2,1)S(1)} %shard_map.91.mine, ...), custom_call_target="tpu_custom_call" | custom-call | flops 402653184 | bytes 2097152 | tf_op jit(solution)/shard_map/pallas_call | solution.py:291
  27.5 0.0 collective-permute-done.4.outer
  27.5 0.0 collective-permute-done.3.inner
  27.5 9.5 %shard_map.94 = (f32[2,96,512]{2,1,0:T(8,128)S(1)}, bf16[2,96,512]{2,1,0:T(8,128)(2,1)S(1)}, bf16[2,256,512]{2,1,0:T(8,128)(2,1)S(1)}, bf16[2,256,512]{2,1,0:T(8...) custom-call(bf16[1024,512]{1,0:T(8,128)(2,1)S(1)} %copy-done, bf16[1024,512]{1,0:T(8,128)(2,1)S(1)} %copy-done.1, ...), custom_call_target="tpu_custom_call" | custom-call | flops 1677721600 | bytes 4194304 | tf_op jit(solution)/shard_map/pallas_call | solution.py:378
  37.1 0.5 collective-permute-start.7
  37.6 3.5 %shard_map.95 = (bf16[1024,128]{1,0:T(8,128)(2,1)S(1)}, f32[1024,128]{1,0:T(8,128)S(1)}, f32[1024,128]{1,0:T(8,128)S(1)}) custom-call(bf16[1024,512]{1,0:T(8,128)(2,1)S(1)} %copy-done, bf16[1024,512]{1,0:T(8,128)(2,1)S(1)} %get-tuple-element.46.refs_1_, bf16[1024,512]{1,0:T(8,128)(2,1)S(1)} %get-tuple-element.47.refs_2_, bf16[1024,512]{1,0:T(8,128)(2,1)S(1)} %copy-done.1, ...), custom_call_target="tpu_custom_call" | custom-call | flops 1006632960 | bytes 3145728 | tf_op jit(solution)/shard_map/pallas_call | solution.py:450
  41.1 0.1 collective-permute-start.8
  41.2 0.9 %collective-permute-start.9 = (bf16[2,256,512]{2,1,0:T(8,128)(2,1)S(1)}, bf16[2,256,512]{2,1,0:T(8,128)(2,1)S(1)}, u32[]{:S(2)}, u32[]{:S(2)}) collective-permute-start(bf16[2,256,512]{2,1,0:T(8,128)(2,1)S(1)} %get-tuple-element.77), channel_id=1, source_target_pairs={{2,4},{6,8},{10,12},{14,16},{18,20},{22,24},{26,28},{4,2},{8,6},{1... | collective-permute-start | bytes 1572872 | tf_op jit(solution)/shard_map/ppermute | solution.py:598
  42.2 2.9 %collective-permute-start.10 = (bf16[2,48,512]{2,1,0:T(8,128)(2,1)S(1)}, bf16[2,48,512]{2,1,0:T(8,128)(2,1)S(1)}, u32[]{:S(2)}, u32[]{:S(2)}) collective-permute-start(bf16[2,48,512]{2,1,0:T(8,128)(2,1)S(1)} %get-tuple-element.79), channel_id=1, source_target_pairs={{0,8},{2,10},{4,12},{6,14},{8,0},{10,2},{12,4},{14,6},{16,24},{18,... | collective-permute-start | bytes 294920 | tf_op jit(solution)/shard_map/ppermute | solution.py:594
  45.1 3.5 %shard_map.96 = (bf16[1024,128]{1,0:T(8,128)(2,1)S(1)}, f32[1024,128]{1,0:T(8,128)S(1)}, f32[1024,128]{1,0:T(8,128)S(1)}, bf16[1024,512]{1,0:T(8,128)(2,1)}) custom-call(bf16[1024,512]{1,0:T(8,128)(2,1)S(1)} %copy-done, bf16[1024,512]{1,0:T(8,128)(2,1)S(1)} %get-tuple-element.46.refs_1_, bf16[1024,512]{1,0:T(8,128)(2,1)S(1)} %get-tuple-element.47.refs_2_, ...), custom_call_target="tpu_custom_call" | custom-call | flops 1006632960 | bytes 3145728 | tf_op jit(solution)/shard_map/pallas_call | solution.py:450
  48.5 3.8 %shard_map.97 = (bf16[1024,128]{1,0:T(8,128)(2,1)S(1)}, f32[1024,128]{1,0:T(8,128)S(1)}, f32[1024,128]{1,0:T(8,128)S(1)}, bf16[1024,512]{1,0:T(8,128)(2,1)}) custom-call(bf16[1024,512]{1,0:T(8,128)(2,1)S(1)} %copy-done, bf16[1024,512]{1,0:T(8,128)(2,1)S(1)} %get-tuple-element.46.refs_1_, ...), custom_call_target="tpu_custom_call", output_to_operand_aliasing={{3}: (7, {})} | custom-call | flops 1006632960 | bytes 3145728 | tf_op jit(solution)/shard_map/pallas_call | solution.py:450
  52.3 1.7 %collective-permute-done.10.rest_0_ = bf16[2,48,512]{2,1,0:T(8,128)(2,1)S(1)} collective-permute-done((bf16[2,48,512]{2,1,0:T(8,128)(2,1)S(1)}, bf16[2,48,512]{2,1,0:T(8,128)(2,1)S(1)}, u32[]{:S(2)}, u32[]{:S(2)}) %collective-permute-start.10) | collective-permute-done | bytes 98336 | tf_op jit(solution)/shard_map/ppermute | solution.py:594
  54.1 2.6 %collective-permute-start.12 = (bf16[2,4,512]{2,1,0:T(4,128)(2,1)S(1)}, bf16[2,4,512]{2,1,0:T(4,128)(2,1)S(1)}, u32[]{:S(2)}, u32[]{:S(2)}) collective-permute-start(bf16[2,4,512]{2,1,0:T(4,128)(2,1)S(1)} %get-tuple-element.82), channel_id=1, source_target_pairs={{0,16},{2,18},{4,20},{6,22},{8,24},{10,26},{12,28},{14,30},{16,0},... | collective-permute-start | bytes 24584 | tf_op jit(solution)/shard_map/ppermute | solution.py:594
  56.7 1.9 %collective-permute-start.11 = (bf16[2,20,512]{2,1,0:T(8,128)(2,1)S(1)}, bf16[2,20,512]{2,1,0:T(8,128)(2,1)S(1)}, u32[]{:S(2)}, u32[]{:S(2)}) collective-permute-start(bf16[2,20,512]{2,1,0:T(8,128)(2,1)S(1)} %get-tuple-element.81), channel_id=1, source_target_pairs={{0,4},{2,6},{4,0},{6,2},{8,12},{10,14},{12,8},{14,10},{16,20},{18,... | collective-permute-start | bytes 122888 | tf_op jit(solution)/shard_map/ppermute | solution.py:594
  58.5 3.8 %shard_map.98 = (bf16[1024,128]{1,0:T(8,128)(2,1)S(1)}, f32[1024,128]{1,0:T(8,128)S(1)}, f32[1024,128]{1,0:T(8,128)S(1)}, bf16[1024,512]{1,0:T(8,128)(2,1)}) custom-call(bf16[1024,512]{1,0:T(8,128)(2,1)S(1)} %copy-done, bf16[1024,512]{1,0:T(8,128)(2,1)S(1)} %get-tuple-element.46.refs_1_, ...), custom_call_target="tpu_custom_call", output_to_operand_aliasing={{3}: (7, {})} | custom-call | flops 1006632960 | bytes 3145728 | tf_op jit(solution)/shard_map/pallas_call | solution.py:450
  62.4 2.9 %shard_map.101 = (bf16[1024,512]{1,0:T(8,128)(2,1)}, bf16[1024,512]{1,0:T(8,128)(2,1)}, bf16[1024,512]{1,0:T(8,128)(2,1)}) custom-call(f32[1024,128]{1,0:T(8,128)S(1)} %get-tuple-element.59.rest_3_.refs_0_, f32[1024,128]{1,0:T(8,128)S(1)} %get-tuple-element.61.refs_1_, ...), custom_call_target="tpu_custom_call", output_to_operand_aliasing={{2}: (17, {})} | custom-call | bytes 6291456 | tf_op jit(solution)/shard_map/pallas_call | solution.py:562
  (21 shorter events, 0.1 us)
Async XLA Ops:
  0.6 9.3 %copy-start.1 = (bf16[1024,512]{1,0:T(8,128)(2,1)S(1)}, bf16[1024,512]{1,0:T(8,128)(2,1)}, u32[]{:S(2)}) copy-start(bf16[1024,512]{1,0:T(8,128)(2,1)} %refs_3_.15) | copy-start | bytes 3145732
  0.6 9.3 %copy-start = (bf16[1024,512]{1,0:T(8,128)(2,1)S(1)}, bf16[1024,512]{1,0:T(8,128)(2,1)}, u32[]{:S(2)}) copy-start(bf16[1024,512]{1,0:T(8,128)(2,1)} %refs_0_.15) | copy-start | bytes 3145732
  3.6 10.1 %collective-permute-start.1 = (bf16[2,20,512]{2,1,0:T(8,128)(2,1)S(1)}, bf16[2,20,512]{2,1,0:T(8,128)(2,1)S(1)}, u32[]{:S(2)}, u32[]{:S(2)}) collective-permute-start(bf16[2,20,512]{2,1,0:T(8,128)(2,1)S(1)} %bitcast.1), channel_id=1, source_target_pairs={{0,4},{2,6},{4,0},{6,2},{8,12},{10,14},{12,8},{14,10},{16,20},{18,... | collective-permute-start | bytes 122888 | tf_op jit(solution)/shard_map/ppermute | solution.py:594
  6.7 5.4 %collective-permute-start.2 = (bf16[2,4,512]{2,1,0:T(4,128)(2,1)S(1)}, bf16[2,4,512]{2,1,0:T(4,128)(2,1)S(1)}, u32[]{:S(2)}, u32[]{:S(2)}) collective-permute-start(bf16[2,4,512]{2,1,0:T(4,128)(2,1)S(1)} %get-tuple-element.49.refs_1_), channel_id=1, source_target_pairs={{0,20},{2,22},{4,16},{6,18},{8,28},{10,30},{12,24},{14,26},{16,4},... | collective-permute-start | bytes 24584 | tf_op jit(solution)/shard_map/ppermute | solution.py:594
  9.2 4.5 %collective-permute-start = (bf16[2,4,512]{2,1,0:T(4,128)(2,1)S(1)}, bf16[2,4,512]{2,1,0:T(4,128)(2,1)S(1)}, u32[]{:S(2)}, u32[]{:S(2)}) collective-permute-start(bf16[2,4,512]{2,1,0:T(4,128)(2,1)S(1)} %get-tuple-element.49.refs_1_), channel_id=1, source_target_pairs={{0,16},{2,18},{4,20},{6,22},{8,24},{10,26},{12,28},{14,30},{16,0},... | collective-permute-start | bytes 24584 | tf_op jit(solution)/shard_map/ppermute | solution.py:594
  9.3 18.2 %collective-permute-start.4 = (bf16[2,256,512]{2,1,0:T(8,128)(2,1)S(1)}, bf16[2,256,512]{2,1,0:T(8,128)(2,1)S(1)}, u32[]{:S(2)}, u32[]{:S(2)}) collective-permute-start(bf16[2,256,512]{2,1,0:T(8,128)(2,1)S(1)} %get-tuple-element.52), channel_id=1, source_target_pairs={{2,4},{6,8},{10,12},{14,16},{18,20},{22,24},{26,28},{4,2},{8,6},{1... | collective-permute-start | bytes 1572872 | tf_op jit(solution)/shard_map/ppermute | solution.py:598
  13.8 13.7 %collective-permute-start.3 = (bf16[2,256,512]{2,1,0:T(8,128)(2,1)S(1)}, bf16[2,256,512]{2,1,0:T(8,128)(2,1)S(1)}, u32[]{:S(2)}, u32[]{:S(2)}) collective-permute-start(bf16[2,256,512]{2,1,0:T(8,128)(2,1)S(1)} %get-tuple-element.51), channel_id=1, source_target_pairs={{0,2},{2,0},{4,6},{6,4},{8,10},{10,8},{12,14},{14,12},{16,18},{18,... | collective-permute-start | bytes 1572872 | tf_op jit(solution)/shard_map/ppermute | solution.py:594
  14.9 7.4 %collective-permute-start.5 = (bf16[2,2,24,512]{3,2,1,0:T(8,128)(2,1)S(1)}, bf16[2,2,24,512]{3,2,1,0:T(8,128)(2,1)S(1)}, u32[]{:S(2)}, u32[]{:S(2)}) collective-permute-start(bf16[2,2,24,512]{3,2,1,0:T(8,128)(2,1)S(1)} %get-tuple-element.53.refs_0_), channel_id=1, source_target_pairs={{0,8},{2,10},{4,12},{6,14},{8,0},{10,2},{12,4},{14,6},{16,24},{18,... | collective-permute-start | bytes 294920 | tf_op jit(solution)/shard_map/ppermute | solution.py:594
  22.3 1.8 %collective-permute-start.6 = (bf16[4,2,24,512]{3,2,1,0:T(8,128)(2,1)S(1)}, bf16[4,2,24,512]{3,2,1,0:T(8,128)(2,1)S(1)}, u32[]{:S(2)}, u32[]{:S(2)}) collective-permute-start(bf16[4,2,24,512]{3,2,1,0:T(8,128)(2,1)S(1)} %shard_map.91.mine), channel_id=1, source_target_pairs={{0,2},{2,0},{4,6},{6,4},{8,10},{10,8},{12,14},{14,12},{16,18},{18,... | collective-permute-start | bytes 589832 | tf_op jit(solution)/shard_map/ppermute | solution.py:594
  37.1 4.0 %collective-permute-start.7 = (bf16[2,96,512]{2,1,0:T(8,128)(2,1)S(1)}, bf16[2,96,512]{2,1,0:T(8,128)(2,1)S(1)}, u32[]{:S(2)}, u32[]{:S(2)}) collective-permute-start(bf16[2,96,512]{2,1,0:T(8,128)(2,1)S(1)} %get-tuple-element.73), channel_id=1, source_target_pairs={{0,2},{2,0},{4,6},{6,4},{8,10},{10,8},{12,14},{14,12},{16,18},{18,... | collective-permute-start | bytes 589832 | tf_op jit(solution)/shard_map/ppermute | solution.py:594
  41.1 21.2 %collective-permute-start.8 = (bf16[2,256,512]{2,1,0:T(8,128)(2,1)S(1)}, bf16[2,256,512]{2,1,0:T(8,128)(2,1)S(1)}, u32[]{:S(2)}, u32[]{:S(2)}) collective-permute-start(bf16[2,256,512]{2,1,0:T(8,128)(2,1)S(1)} %get-tuple-element.76), channel_id=1, source_target_pairs={{0,2},{2,0},{4,6},{6,4},{8,10},{10,8},{12,14},{14,12},{16,18},{18,... | collective-permute-start | bytes 1572872 | tf_op jit(solution)/shard_map/ppermute | solution.py:594
  41.2 21.1 %collective-permute-start.9 = (bf16[2,256,512]{2,1,0:T(8,128)(2,1)S(1)}, bf16[2,256,512]{2,1,0:T(8,128)(2,1)S(1)}, u32[]{:S(2)}, u32[]{:S(2)}) collective-permute-start(bf16[2,256,512]{2,1,0:T(8,128)(2,1)S(1)} %get-tuple-element.77), channel_id=1, source_target_pairs={{2,4},{6,8},{10,12},{14,16},{18,20},{22,24},{26,28},{4,2},{8,6},{1... | collective-permute-start | bytes 1572872 | tf_op jit(solution)/shard_map/ppermute | solution.py:598
  42.2 11.9 %collective-permute-start.10 = (bf16[2,48,512]{2,1,0:T(8,128)(2,1)S(1)}, bf16[2,48,512]{2,1,0:T(8,128)(2,1)S(1)}, u32[]{:S(2)}, u32[]{:S(2)}) collective-permute-start(bf16[2,48,512]{2,1,0:T(8,128)(2,1)S(1)} %get-tuple-element.79), channel_id=1, source_target_pairs={{0,8},{2,10},{4,12},{6,14},{8,0},{10,2},{12,4},{14,6},{16,24},{18,... | collective-permute-start | bytes 294920 | tf_op jit(solution)/shard_map/ppermute | solution.py:594
  54.1 8.3 %collective-permute-start.12 = (bf16[2,4,512]{2,1,0:T(4,128)(2,1)S(1)}, bf16[2,4,512]{2,1,0:T(4,128)(2,1)S(1)}, u32[]{:S(2)}, u32[]{:S(2)}) collective-permute-start(bf16[2,4,512]{2,1,0:T(4,128)(2,1)S(1)} %get-tuple-element.82), channel_id=1, source_target_pairs={{0,16},{2,18},{4,20},{6,22},{8,24},{10,26},{12,28},{14,30},{16,0},... | collective-permute-start | bytes 24584 | tf_op jit(solution)/shard_map/ppermute | solution.py:594
  56.7 5.7 %collective-permute-start.13 = (bf16[2,4,512]{2,1,0:T(4,128)(2,1)S(1)}, bf16[2,4,512]{2,1,0:T(4,128)(2,1)S(1)}, u32[]{:S(2)}, u32[]{:S(2)}) collective-permute-start(bf16[2,4,512]{2,1,0:T(4,128)(2,1)S(1)} %get-tuple-element.83), channel_id=1, source_target_pairs={{0,20},{2,22},{4,16},{6,18},{8,28},{10,30},{12,24},{14,26},{16,4},... | collective-permute-start | bytes 24584 | tf_op jit(solution)/shard_map/ppermute | solution.py:594
  56.7 5.7 %collective-permute-start.11 = (bf16[2,20,512]{2,1,0:T(8,128)(2,1)S(1)}, bf16[2,20,512]{2,1,0:T(8,128)(2,1)S(1)}, u32[]{:S(2)}, u32[]{:S(2)}) collective-permute-start(bf16[2,20,512]{2,1,0:T(8,128)(2,1)S(1)} %get-tuple-element.81), channel_id=1, source_target_pairs={{0,4},{2,6},{4,0},{6,2},{8,12},{10,14},{12,8},{14,10},{16,20},{18,... | collective-permute-start | bytes 122888 | tf_op jit(solution)/shard_map/ppermute | solution.py:594
  58.5 3.8 %copy-start.2 = (f32[8,256]{1,0:T(8,128)S(1)}, f32[8,256]{1,0:T(8,128)}, u32[]{:S(2)}) copy-start(f32[8,256]{1,0:T(8,128)} %refs_11_.1) | copy-start | bytes 24580
  58.5 3.9 %copy-start.3 = (f32[8,64]{1,0:T(8,128)S(1)}, f32[8,64]{1,0:T(8,128)}, u32[]{:S(2)}) copy-start(f32[8,64]{1,0:T(8,128)} %refs_10_.1) | copy-start | bytes 6148

commit v6 on v5

--- a/solution.py
+++ b/solution.py
@@ -241,34 +241,61 @@
     )(q, k, v, g)
 
 
-def far_body(depth, scale, width, pairs, q, g, mine, theirs, *rest):
+def place_slots(sources, far, n):
+    at = 0
+    for src in sources:
+        for s in range(src.shape[0]):
+            far[at : at + src.shape[2]] = src[s, n]
+            at += src.shape[2]
+
+
+def far_body(depth, scale, width, pairs, q, g, mine, *rest):
     partial = rest[:pairs]
-    far_k, far_v, known = rest[pairs:]
+    qs, gs, known, near_k, near_v = rest[pairs:]
     rows = q.shape[0]
-    slots, _, per, _ = mine.shape
-    half = slots * per
     pair = pl.program_id(0)
     lanes = pl.ds(pl.multiple_of(pair * width, width), width)
-    q, g, far_k, far_v = (ref.at[:, lanes] for ref in (q, g, far_k, far_v))
-    mine, theirs = (ref.at[:, :, :, lanes] for ref in (mine, theirs))
+    q, g = (ref.at[:, lanes] for ref in (q, g))
+    qs, gs = (ref.at[:, :, lanes] for ref in (qs, gs))
+    mine = mine.at[:, :, :, lanes]
     out = known.at[pair]
-    for n, far in enumerate((far_k, far_v)):
-        for m, src in enumerate((mine, theirs)):
-            for s in range(slots):
-                at = m * half + s * per
-                far[at : at + per] = src[s, n]
+    place_slots((mine,), near_k, 0)
+    place_slots((mine,), near_v, 1)
     for h, mask in enumerate(head_masks(width, depth)):
         for b in range(rows // BLOCK):
             r = slice(b * BLOCK, (b + 1) * BLOCK)
-            qs = keep_head(q[r], mask, scale)
-            gs = keep_head(g[r], mask)
+            q_rows = keep_head(q[r], mask, scale)
+            g_rows = keep_head(g[r], mask)
+            qs[h, r] = q_rows
+            gs[h, r] = g_rows
             old = [partial[0][m, h : h + 1, r] for m in range(3)]
             for n in range(1, pairs):
                 old = [
                     jnp.where(pair == n, partial[n][m, h : h + 1, r], old[m]) for m in range(3)
                 ]
-            state = merge(None, dot(far_k[...], qs, NT), dot(far_v[...], gs, NT))
+            state = merge(None, dot(near_k[...], q_rows, NT), dot(near_v[...], g_rows, NT))
             for m, value in enumerate(settle(old, state)):
+                out[m, h : h + 1, r] = value
+
+
+def more_body(width, qs, gs, mine, theirs, known, far_k, far_v, out):
+    rows = qs.shape[1]
+    pair = pl.program_id(0)
+    lanes = pl.ds(pl.multiple_of(pair * width, width), width)
+    qs, gs = (ref.at[:, :, lanes] for ref in (qs, gs))
+    mine, theirs = (ref.at[:, :, :, lanes] for ref in (mine, theirs))
+    far_k, far_v = (ref.at[:, lanes] for ref in (far_k, far_v))
+    known, out = known.at[pair], out.at[pair]
+    place_slots((mine, theirs), far_k, 0)
+    place_slots((mine, theirs), far_v, 1)
+    half = far_k.shape[0] // 2
+    for h in range(qs.shape[0]):
+        for b in range(rows // BLOCK):
+            r = slice(b * BLOCK, (b + 1) * BLOCK)
+            old = [known[m, h : h + 1, r] for m in range(3)]
+            s = dot(far_k[half:], qs[h, r], NT)
+            d = dot(far_v[half:], gs[h, r], NT)
+            for m, value in enumerate(settle(old, merge(None, s, d))):
                 out[m, h : h + 1, r] = value
 
 
@@ -282,33 +309,47 @@
     return top, total, dots
 
 
-def far_stats(q, g, mine, theirs, partial, width, depth, scale):
+def far_stats(q, g, mine, partial, width, depth, scale):
     rows, cols = q.shape
     pairs = cols // width
     hp = width // depth
-    slots, _, per, _ = mine.shape
-    far = 2 * slots * per
+    half = mine.shape[0] * mine.shape[2]
     return call(
         functools.partial(far_body, depth, scale, width, pairs),
-        flops=4 * far * rows * cols,
+        flops=4 * half * rows * cols,
         moved=rows * cols * 4,
         grid=(pairs,),
-        in_specs=[WHOLE] * (4 + pairs),
+        in_specs=[WHOLE] * (3 + pairs),
         out_specs=[WHOLE] * 3,
-        out_shape=[struct((far, cols), BF16)] * 2 + [struct((pairs, 3, hp, rows), F32)],
-    )(q, g, mine, theirs, *partial)
-
-
-def remote_body(depth, scale, width, q, g, inner, outer, far_k, far_v, known, *rest):
-    far_kt, near_t, near_d, qs, gs, s_held, d_held = rest[6:]
-    rows = q.shape[0]
+        out_shape=[struct((hp, rows, cols), BF16)] * 2 + [struct((pairs, 3, hp, rows), F32)],
+        scratch_shapes=[pltpu.VMEM((half, width), BF16)] * 2,
+    )(q, g, mine, *partial)
+
+
+def more_stats(qs, gs, mine, theirs, known, width):
+    rows, cols = qs.shape[1:]
+    far = 2 * mine.shape[0] * mine.shape[2]
+    return call(
+        functools.partial(more_body, width),
+        flops=2 * far * rows * cols,
+        moved=rows * cols * 4,
+        grid=(cols // width,),
+        in_specs=[WHOLE] * 5,
+        out_specs=[WHOLE] * 3,
+        out_shape=[struct((far, cols), BF16)] * 2 + [struct(known.shape, F32)],
+    )(qs, gs, mine, theirs, known)
+
+
+def remote_body(depth, scale, width, qs, gs, inner, outer, far_k, far_v, known, *rest):
+    far_kt, near_t, near_d, s_held, d_held = rest[6:]
+    rows = qs.shape[1]
     blocks = rows // BLOCK
     half = far_k.shape[0] // 2
-    masks = head_masks(width, depth)
+    heads = qs.shape[0]
     pair = pl.program_id(0)
     lanes = pl.ds(pl.multiple_of(pair * width, width), width)
-    q, g, far_k, far_v = (ref.at[:, lanes] for ref in (q, g, far_k, far_v))
-    inner, outer = (ref.at[:, :, lanes] for ref in (inner, outer))
+    far_k, far_v = (ref.at[:, lanes] for ref in (far_k, far_v))
+    qs, gs, inner, outer = (ref.at[:, :, lanes] for ref in (qs, gs, inner, outer))
     kept, sent, inner_d, outer_d = (ref.at[:, :, lanes] for ref in rest[:4])
     dq_t = rest[4].at[lanes]
     final = rest[5].at[pair]
@@ -316,10 +357,6 @@
     far_kt[...] = (far_k[...].astype(F32) * scale).astype(BF16).T
     near_t[0] = (inner[0].astype(F32) * scale).astype(BF16).T
     near_t[1] = (outer[0].astype(F32) * scale).astype(BF16).T
-    scaled = (q[...].astype(F32) * scale).astype(BF16)
-    for h, mask in enumerate(masks):
-        qs[h] = jnp.where(mask, scaled, 0).astype(BF16)
-        gs[h] = jnp.where(mask, g[...], 0).astype(BF16)
     odd = is_odd()
     position = lax.axis_index("seq")
     ends = (position == 0) | (position == lax.axis_size("seq") - 1)
@@ -330,7 +367,7 @@
     halos = ((inner, None), (outer, missing))
     final[0] = known[0] + jnp.log(known[1])
     final[1] = known[2] / known[1]
-    for h in range(len(masks)):
+    for h in range(heads):
         old = None
         for n, ((halo, bias), r) in enumerate(zip(halos, places)):
             if old is None or blocks > 1:
@@ -345,7 +382,7 @@
             final[0, h : h + 1, r] = old[0] + jnp.log(old[1])
             final[1, h : h + 1, r] = old[2] / old[1]
     totals = [None, None]
-    for h in range(len(masks)):
+    for h in range(heads):
         hr = slice(h * depth, (h + 1) * depth)
         p = jnp.exp(dot(far_k[...], qs[h], NT) - final[0, h : h + 1, :])
         ds = (p * (dot(far_v[...], gs[h], NT) - final[1, h : h + 1, :])).astype(BF16)
@@ -369,8 +406,8 @@
         outer_d[n] = near_d[2 + n].astype(BF16)
 
 
-def remote(q, g, inner, outer, far_k, far_v, known, width, depth, scale):
-    rows, cols = q.shape
+def remote(qs, gs, inner, outer, far_k, far_v, known, width, depth, scale):
+    rows, cols = qs.shape[1:]
     pairs = cols // width
     hp = width // depth
     far = far_k.shape[0]
@@ -386,8 +423,6 @@
             pltpu.VMEM((width, far), BF16),
             pltpu.VMEM((2, width, BLOCK), BF16),
             pltpu.VMEM((4, BLOCK, width), F32),
-            pltpu.VMEM((hp, rows, width), BF16),
-            pltpu.VMEM((hp, rows, width), BF16),
             pltpu.VMEM((2 * hp, BLOCK, BLOCK), F32),
             pltpu.VMEM((2 * hp, BLOCK, BLOCK), F32),
         ],
@@ -399,7 +434,7 @@
             struct((cols, rows), F32),
             struct((pairs, 2, hp, rows), F32),
         ],
-    )(q, g, inner, outer, far_k, far_v, known)
+    )(qs, gs, inner, outer, far_k, far_v, known)
 
 
 def local_body(depth, scale, width, pair, chained, *refs):
@@ -619,16 +654,15 @@
     comb, inner = join([here, there], token(), [inner])
     for bit in group_bits[1:]:
         got = swap(comb, bit)
-        (comb,) = join([comb, got], token() + token())
+        (comb,) = join([comb, got], token() + token() + token())
     theirs = swap(comb, 0)
     outer = cross(outer)
     inner = swap(inner, 0)
 
-    far_k, far_v, known = far_stats(
-        query, out_grad, comb, theirs, partial, width, depth, scale
-    )
+    qs, gs, known = far_stats(query, out_grad, comb, partial, width, depth, scale)
+    far_k, far_v, known = more_stats(qs, gs, comb, theirs, known, width)
     kept, sent, inner_d, outer_d, dq_t, final = remote(
-        query, out_grad, inner, outer, far_k, far_v, known, width, depth, scale
+        qs, gs, inner, outer, far_k, far_v, known, width, depth, scale
     )
     got = [swap(sent, 0)]
 

time: 65.6 us -> 65.5 us (level)
  waiting for transfers between devices: 6.17 us -> 4.4 us
  Pallas kernels: 40.2 us -> 41.2 us
  starting transfers between devices: 18 us -> 18.7 us
    ppermute x12, waiting for transfers between devices: 6.17 us -> 4.4 us  [swap(): return lax.ppermute(array, 'seq', [(i, i ^ mask) for i in range(devices)])]
    pallas_call x1 -> x2, Pallas kernels: 3.36 us -> 4.91 us  [the longest x1 2.74 us: far_stats(): call(functools.partial(far_body, depth, scale, width, pairs), flops=4 * h...]
  transfers between devices with their start and end apart: 14 -> 14, of which waited for: 4 -> 4; matrix products, arithmetic and copies ran while one was open for 0% -> 0% of each run, Pallas kernels for 38% -> 40%
where the time goes in v6:
time: 65.5 us; the launch traced here: 65.3 us
  Pallas kernels  41.2 us (63%)
  starting transfers between devices  18.7 us (29%)
  waiting for transfers between devices  4.4 us (7%)
  between operations  1.06 us (2%)
    ppermute x12, starting transfers between devices, swap(): return lax.ppermute(array, 'seq', [(i, i ^ mask) for i in range(devices)])  17.1 us
    pallas_call x4, Pallas kernels, local(): call(functools.partial(local_body, depth, scale, width, pair, chained), f...  14.5 us
    pallas_call x1, Pallas kernels, remote(): call(functools.partial(remote_body, depth, scale, width), flops=10 * (far...  9.01 us
    pallas_call x4, Pallas kernels, stats(): call(functools.partial(stats_body, depth, scale, width, pair), flops=2 *...  6.86 us
    ppermute x12, waiting for transfers between devices, swap(): return lax.ppermute(array, 'seq', [(i, i ^ mask) for i in range(devices)])  4.4 us
    pallas_call x1, Pallas kernels, pool(): call(functools.partial(pool_body, cols // heads), moved=k.size * 6, vmem=...  2.93 us
    pallas_call x1, Pallas kernels, finish(): call(functools.partial(finish_body, pairs, depth, len(got)), moved=rows *...  2.87 us
    pallas_call x1, Pallas kernels, far_stats(): call(functools.partial(far_body, depth, scale, width, pairs), flops=4 * h...  2.74 us
  transfers between devices with their start and end apart: 14, of which 4 were waited for; matrix products, arithmetic and copies ran while one was open for 0% of the time, Pallas kernels for 40%

profile of v6, /device:TPU:0, one launch (start us, length us, event | category | flops | bytes accessed | tf_op | source)
XLA Modules:
  0.0 65.3 jit_solution(16199217446165382684)
XLA Ops:
  0.7 2.9 %shard_map.85 = (bf16[2,16,512]{2,1,0:T(8,128)(2,1)S(1)}, bf16[2,4,512]{2,1,0:T(4,128)(2,1)S(1)}, bf16[2,256,512]{2,1,0:T(8,128)(2,1)S(1)}, bf16[2,256,512]{2,1,...) custom-call(bf16[1024,512]{1,0:T(8,128)(2,1)} %k.1, bf16[1024,512]{1,0:T(8,128)(2,1)} %v.1, ...), custom_call_target="tpu_custom_call" | custom-call | bytes 3145728 | tf_op jit(solution)/shard_map/pallas_call | solution.py:136
  3.6 3.1 %collective-permute-start.1 = (bf16[2,20,512]{2,1,0:T(8,128)(2,1)S(1)}, bf16[2,20,512]{2,1,0:T(8,128)(2,1)S(1)}, u32[]{:S(2)}, u32[]{:S(2)}) collective-permute-start(bf16[2,20,512]{2,1,0:T(8,128)(2,1)S(1)} %bitcast.1), channel_id=1, source_target_pairs={{0,4},{2,6},{4,0},{6,2},{8,12},{10,14},{12,8},{14,10},{16,20},{18,... | collective-permute-start | bytes 122888 | tf_op jit(solution)/shard_map/ppermute | solution.py:629
  6.7 2.5 %collective-permute-start.2 = (bf16[2,4,512]{2,1,0:T(4,128)(2,1)S(1)}, bf16[2,4,512]{2,1,0:T(4,128)(2,1)S(1)}, u32[]{:S(2)}, u32[]{:S(2)}) collective-permute-start(bf16[2,4,512]{2,1,0:T(4,128)(2,1)S(1)} %get-tuple-element.52.refs_1_), channel_id=1, source_target_pairs={{0,20},{2,22},{4,16},{6,18},{8,28},{10,30},{12,24},{14,26},{16,4},... | collective-permute-start | bytes 24584 | tf_op jit(solution)/shard_map/ppermute | solution.py:629
  9.2 0.1 collective-permute-start
  9.3 0.7 %collective-permute-start.5 = (bf16[2,256,512]{2,1,0:T(8,128)(2,1)S(1)}, bf16[2,256,512]{2,1,0:T(8,128)(2,1)S(1)}, u32[]{:S(2)}, u32[]{:S(2)}) collective-permute-start(bf16[2,256,512]{2,1,0:T(8,128)(2,1)S(1)} %get-tuple-element.58), channel_id=1, source_target_pairs={{2,4},{6,8},{10,12},{14,16},{18,20},{22,24},{26,28},{4,2},{8,6},{1... | collective-permute-start | bytes 1572872 | tf_op jit(solution)/shard_map/ppermute | solution.py:633
  10.0 1.7 %shard_map.87.refs_6_.rest_0_ = f32[3,2,1024]{2,1,0:T(2,128)S(1)} custom-call(bf16[1024,512]{1,0:T(8,128)(2,1)S(1)} %copy-done, bf16[1024,512]{1,0:T(8,128)(2,1)S(1)} %get-tuple-element.49.refs_1_, bf16[1024,512]{1,0:T(8,128)(2,1)S(1)} %get-tuple-element.50.refs_2_, bf16[1024,512]{1,0:T(8,128)(2,1)S(1)} %copy-done.1), custom_call_target="tpu_custom_call" | custom-call | flops 402653184 | bytes 1048576 | tf_op jit(solution)/shard_map/pallas_call | solution.py:234
  11.7 0.4 collective-permute-done.2.refs_4_
  12.1 1.6 %collective-permute-done.refs_2_ = bf16[2,4,512]{2,1,0:T(4,128)(2,1)S(1)} collective-permute-done((bf16[2,4,512]{2,1,0:T(4,128)(2,1)S(1)}, bf16[2,4,512]{2,1,0:T(4,128)(2,1)S(1)}, u32[]{:S(2)}, u32[]{:S(2)}) %collective-permute-start) | collective-permute-done | bytes 8224 | tf_op jit(solution)/shard_map/ppermute | solution.py:629
  13.8 1.2 %collective-permute-start.4 = (bf16[2,256,512]{2,1,0:T(8,128)(2,1)S(1)}, bf16[2,256,512]{2,1,0:T(8,128)(2,1)S(1)}, u32[]{:S(2)}, u32[]{:S(2)}) collective-permute-start(bf16[2,256,512]{2,1,0:T(8,128)(2,1)S(1)} %get-tuple-element.57), channel_id=1, source_target_pairs={{0,2},{2,0},{4,6},{6,4},{8,10},{10,8},{12,14},{14,12},{16,18},{18,... | collective-permute-start | bytes 1572872 | tf_op jit(solution)/shard_map/ppermute | solution.py:629
  14.9 1.6 %collective-permute-start.3 = (bf16[2,2,24,512]{3,2,1,0:T(8,128)(2,1)S(1)}, bf16[2,2,24,512]{3,2,1,0:T(8,128)(2,1)S(1)}, u32[]{:S(2)}, u32[]{:S(2)}) collective-permute-start(bf16[2,2,24,512]{3,2,1,0:T(8,128)(2,1)S(1)} %get-tuple-element.54.refs_0_), channel_id=1, source_target_pairs={{0,8},{2,10},{4,12},{6,14},{8,0},{10,2},{12,4},{14,6},{16,24},{18,... | collective-permute-start | bytes 294920 | tf_op jit(solution)/shard_map/ppermute | solution.py:629
  16.5 1.7 %shard_map.91.refs_4_.rest_3_ = f32[3,2,1024]{2,1,0:T(2,128)S(1)} custom-call(bf16[1024,512]{1,0:T(8,128)(2,1)S(1)} %copy-done, bf16[1024,512]{1,0:T(8,128)(2,1)S(1)} %get-tuple-element.49.refs_1_, bf16[1024,512]{1,0:T(8,128)(2,1)S(1)} %get-tuple-element.50.refs_2_, bf16[1024,512]{1,0:T(8,128)(2,1)S(1)} %copy-done.1), custom_call_target="tpu_custom_call" | custom-call | flops 402653184 | bytes 1048576 | tf_op jit(solution)/shard_map/pallas_call | solution.py:234
  18.2 1.7 %shard_map.90.refs_3_.rest_2_ = f32[3,2,1024]{2,1,0:T(2,128)S(1)} custom-call(bf16[1024,512]{1,0:T(8,128)(2,1)S(1)} %copy-done, bf16[1024,512]{1,0:T(8,128)(2,1)S(1)} %get-tuple-element.49.refs_1_, bf16[1024,512]{1,0:T(8,128)(2,1)S(1)} %get-tuple-element.50.refs_2_, bf16[1024,512]{1,0:T(8,128)(2,1)S(1)} %copy-done.1), custom_call_target="tpu_custom_call" | custom-call | flops 402653184 | bytes 1048576 | tf_op jit(solution)/shard_map/pallas_call | solution.py:234
  19.9 1.7 %shard_map.89.refs_2_.rest_1_ = f32[3,2,1024]{2,1,0:T(2,128)S(1)} custom-call(bf16[1024,512]{1,0:T(8,128)(2,1)S(1)} %copy-done, bf16[1024,512]{1,0:T(8,128)(2,1)S(1)} %get-tuple-element.49.refs_1_, bf16[1024,512]{1,0:T(8,128)(2,1)S(1)} %get-tuple-element.50.refs_2_, bf16[1024,512]{1,0:T(8,128)(2,1)S(1)} %copy-done.1), custom_call_target="tpu_custom_call" | custom-call | flops 402653184 | bytes 1048576 | tf_op jit(solution)/shard_map/pallas_call | solution.py:234
  21.7 0.6 collective-permute-done.3.refs_1_
  22.3 0.1 collective-permute-start.6
  22.4 2.7 %shard_map.93 = (bf16[2,1024,512]{2,1,0:T(8,128)(2,1)S(1)}, bf16[2,1024,512]{2,1,0:T(8,128)(2,1)S(1)}, f32[4,3,2,1024]{3,2,1,0:T(2,128)S(1)}) custom-call(bf16[1024,512]{1,0:T(8,128)(2,1)S(1)} %copy-done, bf16[1024,512]{1,0:T(8,128)(2,1)S(1)} %copy-done.1, bf16[4,2,24,512]{3,2,1,0:T(8,128)(2,1)S(1)} %shard_map.92.mine, ...), custom_call_target="tpu_custom_call" | custom-call | flops 201326592 | bytes 2097152 | tf_op jit(solution)/shard_map/pallas_call | solution.py:317
  25.2 2.2 %shard_map.94 = (bf16[192,512]{1,0:T(8,128)(2,1)S(1)}, bf16[192,512]{1,0:T(8,128)(2,1)S(1)}, f32[4,3,2,1024]{3,2,1,0:T(2,128)S(1)}) custom-call(bf16[2,1024,512]{2,1,0:T(8,128)(2,1)S(1)} %get-tuple-element.55.qs, bf16[2,1024,512]{2,1,0:T(8,128)(2,1)S(1)} %get-tuple-element.56.gs, bf16[4,2,24,512]{3,2,1,0:T(8,128)(2,1)S(1)} %shard_map.92.mine, ...), custom_call_target="tpu_custom_call" | custom-call | flops 201326592 | bytes 2097152 | tf_op jit(solution)/shard_map/pallas_call | solution.py:332
  27.3 0.0 collective-permute-done.5.outer
  27.4 9.0 %shard_map.95 = (f32[2,96,512]{2,1,0:T(8,128)S(1)}, bf16[2,96,512]{2,1,0:T(8,128)(2,1)S(1)}, bf16[2,256,512]{2,1,0:T(8,128)(2,1)S(1)}, bf16[2,256,512]{2,1,0:T(8...) custom-call(bf16[2,1024,512]{2,1,0:T(8,128)(2,1)S(1)} %get-tuple-element.55.qs, ...), custom_call_target="tpu_custom_call" | custom-call | flops 1677721600 | bytes 4194304 | tf_op jit(solution)/shard_map/pallas_call | solution.py:415
  36.4 0.4 collective-permute-start.7
  36.8 3.5 %shard_map.96 = (bf16[1024,128]{1,0:T(8,128)(2,1)S(1)}, f32[1024,128]{1,0:T(8,128)S(1)}, f32[1024,128]{1,0:T(8,128)S(1)}) custom-call(bf16[1024,512]{1,0:T(8,128)(2,1)S(1)} %copy-done, bf16[1024,512]{1,0:T(8,128)(2,1)S(1)} %get-tuple-element.49.refs_1_, bf16[1024,512]{1,0:T(8,128)(2,1)S(1)} %get-tuple-element.50.refs_2_, bf16[1024,512]{1,0:T(8,128)(2,1)S(1)} %copy-done.1, ...), custom_call_target="tpu_custom_call" | custom-call | flops 1006632960 | bytes 3145728 | tf_op jit(solution)/shard_map/pallas_call | solution.py:485
  40.2 0.0 collective-permute-done.7.rest_0_
  40.3 0.3 collective-permute-start.8
  40.5 0.9 %collective-permute-start.9 = (bf16[2,256,512]{2,1,0:T(8,128)(2,1)S(1)}, bf16[2,256,512]{2,1,0:T(8,128)(2,1)S(1)}, u32[]{:S(2)}, u32[]{:S(2)}) collective-permute-start(bf16[2,256,512]{2,1,0:T(8,128)(2,1)S(1)} %get-tuple-element.83), channel_id=1, source_target_pairs={{2,4},{6,8},{10,12},{14,16},{18,20},{22,24},{26,28},{4,2},{8,6},{1... | collective-permute-start | bytes 1572872 | tf_op jit(solution)/shard_map/ppermute | solution.py:633
  41.5 3.5 %collective-permute-start.10 = (bf16[2,48,512]{2,1,0:T(8,128)(2,1)S(1)}, bf16[2,48,512]{2,1,0:T(8,128)(2,1)S(1)}, u32[]{:S(2)}, u32[]{:S(2)}) collective-permute-start(bf16[2,48,512]{2,1,0:T(8,128)(2,1)S(1)} %get-tuple-element.85), channel_id=1, source_target_pairs={{0,8},{2,10},{4,12},{6,14},{8,0},{10,2},{12,4},{14,6},{16,24},{18,... | collective-permute-start | bytes 294920 | tf_op jit(solution)/shard_map/ppermute | solution.py:629
  45.0 3.5 %shard_map.97 = (bf16[1024,128]{1,0:T(8,128)(2,1)S(1)}, f32[1024,128]{1,0:T(8,128)S(1)}, f32[1024,128]{1,0:T(8,128)S(1)}, bf16[1024,512]{1,0:T(8,128)(2,1)}) custom-call(bf16[1024,512]{1,0:T(8,128)(2,1)S(1)} %copy-done, bf16[1024,512]{1,0:T(8,128)(2,1)S(1)} %get-tuple-element.49.refs_1_, bf16[1024,512]{1,0:T(8,128)(2,1)S(1)} %get-tuple-element.50.refs_2_, ...), custom_call_target="tpu_custom_call" | custom-call | flops 1006632960 | bytes 3145728 | tf_op jit(solution)/shard_map/pallas_call | solution.py:485
  48.5 3.8 %shard_map.98 = (bf16[1024,128]{1,0:T(8,128)(2,1)S(1)}, f32[1024,128]{1,0:T(8,128)S(1)}, f32[1024,128]{1,0:T(8,128)S(1)}, bf16[1024,512]{1,0:T(8,128)(2,1)}) custom-call(bf16[1024,512]{1,0:T(8,128)(2,1)S(1)} %copy-done, bf16[1024,512]{1,0:T(8,128)(2,1)S(1)} %get-tuple-element.49.refs_1_, ...), custom_call_target="tpu_custom_call", output_to_operand_aliasing={{3}: (7, {})} | custom-call | flops 1006632960 | bytes 3145728 | tf_op jit(solution)/shard_map/pallas_call | solution.py:485
  52.3 1.7 %collective-permute-done.10.rest_0_ = bf16[2,48,512]{2,1,0:T(8,128)(2,1)S(1)} collective-permute-done((bf16[2,48,512]{2,1,0:T(8,128)(2,1)S(1)}, bf16[2,48,512]{2,1,0:T(8,128)(2,1)S(1)}, u32[]{:S(2)}, u32[]{:S(2)}) %collective-permute-start.10) | collective-permute-done | bytes 98336 | tf_op jit(solution)/shard_map/ppermute | solution.py:629
  54.0 2.0 %collective-permute-start.12 = (bf16[2,4,512]{2,1,0:T(4,128)(2,1)S(1)}, bf16[2,4,512]{2,1,0:T(4,128)(2,1)S(1)}, u32[]{:S(2)}, u32[]{:S(2)}) collective-permute-start(bf16[2,4,512]{2,1,0:T(4,128)(2,1)S(1)} %get-tuple-element.88), channel_id=1, source_target_pairs={{0,16},{2,18},{4,20},{6,22},{8,24},{10,26},{12,28},{14,30},{16,0},... | collective-permute-start | bytes 24584 | tf_op jit(solution)/shard_map/ppermute | solution.py:629
  56.0 2.4 %collective-permute-start.11 = (bf16[2,20,512]{2,1,0:T(8,128)(2,1)S(1)}, bf16[2,20,512]{2,1,0:T(8,128)(2,1)S(1)}, u32[]{:S(2)}, u32[]{:S(2)}) collective-permute-start(bf16[2,20,512]{2,1,0:T(8,128)(2,1)S(1)} %get-tuple-element.87), channel_id=1, source_target_pairs={{0,4},{2,6},{4,0},{6,2},{8,12},{10,14},{12,8},{14,10},{16,20},{18,... | collective-permute-start | bytes 122888 | tf_op jit(solution)/shard_map/ppermute | solution.py:629
  58.4 3.8 %shard_map.99 = (bf16[1024,128]{1,0:T(8,128)(2,1)S(1)}, f32[1024,128]{1,0:T(8,128)S(1)}, f32[1024,128]{1,0:T(8,128)S(1)}, bf16[1024,512]{1,0:T(8,128)(2,1)}) custom-call(bf16[1024,512]{1,0:T(8,128)(2,1)S(1)} %copy-done, bf16[1024,512]{1,0:T(8,128)(2,1)S(1)} %get-tuple-element.49.refs_1_, ...), custom_call_target="tpu_custom_call", output_to_operand_aliasing={{3}: (7, {})} | custom-call | flops 1006632960 | bytes 3145728 | tf_op jit(solution)/shard_map/pallas_call | solution.py:485
  62.3 2.9 %shard_map.102 = (bf16[1024,512]{1,0:T(8,128)(2,1)}, bf16[1024,512]{1,0:T(8,128)(2,1)}, bf16[1024,512]{1,0:T(8,128)(2,1)}) custom-call(f32[1024,128]{1,0:T(8,128)S(1)} %get-tuple-element.65.rest_3_.refs_0_, f32[1024,128]{1,0:T(8,128)S(1)} %get-tuple-element.67.refs_1_, ...), custom_call_target="tpu_custom_call", output_to_operand_aliasing={{2}: (17, {})} | custom-call | bytes 6291456 | tf_op jit(solution)/shard_map/pallas_call | solution.py:597
  (22 shorter events, 0.1 us)
Async XLA Ops:
  0.6 9.3 %copy-start.1 = (bf16[1024,512]{1,0:T(8,128)(2,1)S(1)}, bf16[1024,512]{1,0:T(8,128)(2,1)}, u32[]{:S(2)}) copy-start(bf16[1024,512]{1,0:T(8,128)(2,1)} %refs_3_.15) | copy-start | bytes 3145732
  0.6 9.3 %copy-start = (bf16[1024,512]{1,0:T(8,128)(2,1)S(1)}, bf16[1024,512]{1,0:T(8,128)(2,1)}, u32[]{:S(2)}) copy-start(bf16[1024,512]{1,0:T(8,128)(2,1)} %refs_0_.15) | copy-start | bytes 3145732
  3.6 10.1 %collective-permute-start.1 = (bf16[2,20,512]{2,1,0:T(8,128)(2,1)S(1)}, bf16[2,20,512]{2,1,0:T(8,128)(2,1)S(1)}, u32[]{:S(2)}, u32[]{:S(2)}) collective-permute-start(bf16[2,20,512]{2,1,0:T(8,128)(2,1)S(1)} %bitcast.1), channel_id=1, source_target_pairs={{0,4},{2,6},{4,0},{6,2},{8,12},{10,14},{12,8},{14,10},{16,20},{18,... | collective-permute-start | bytes 122888 | tf_op jit(solution)/shard_map/ppermute | solution.py:629
  6.7 5.4 %collective-permute-start.2 = (bf16[2,4,512]{2,1,0:T(4,128)(2,1)S(1)}, bf16[2,4,512]{2,1,0:T(4,128)(2,1)S(1)}, u32[]{:S(2)}, u32[]{:S(2)}) collective-permute-start(bf16[2,4,512]{2,1,0:T(4,128)(2,1)S(1)} %get-tuple-element.52.refs_1_), channel_id=1, source_target_pairs={{0,20},{2,22},{4,16},{6,18},{8,28},{10,30},{12,24},{14,26},{16,4},... | collective-permute-start | bytes 24584 | tf_op jit(solution)/shard_map/ppermute | solution.py:629
  9.2 4.5 %collective-permute-start = (bf16[2,4,512]{2,1,0:T(4,128)(2,1)S(1)}, bf16[2,4,512]{2,1,0:T(4,128)(2,1)S(1)}, u32[]{:S(2)}, u32[]{:S(2)}) collective-permute-start(bf16[2,4,512]{2,1,0:T(4,128)(2,1)S(1)} %get-tuple-element.52.refs_1_), channel_id=1, source_target_pairs={{0,16},{2,18},{4,20},{6,22},{8,24},{10,26},{12,28},{14,30},{16,0},... | collective-permute-start | bytes 24584 | tf_op jit(solution)/shard_map/ppermute | solution.py:629
  9.3 18.1 %collective-permute-start.5 = (bf16[2,256,512]{2,1,0:T(8,128)(2,1)S(1)}, bf16[2,256,512]{2,1,0:T(8,128)(2,1)S(1)}, u32[]{:S(2)}, u32[]{:S(2)}) collective-permute-start(bf16[2,256,512]{2,1,0:T(8,128)(2,1)S(1)} %get-tuple-element.58), channel_id=1, source_target_pairs={{2,4},{6,8},{10,12},{14,16},{18,20},{22,24},{26,28},{4,2},{8,6},{1... | collective-permute-start | bytes 1572872 | tf_op jit(solution)/shard_map/ppermute | solution.py:633
  13.8 13.6 %collective-permute-start.4 = (bf16[2,256,512]{2,1,0:T(8,128)(2,1)S(1)}, bf16[2,256,512]{2,1,0:T(8,128)(2,1)S(1)}, u32[]{:S(2)}, u32[]{:S(2)}) collective-permute-start(bf16[2,256,512]{2,1,0:T(8,128)(2,1)S(1)} %get-tuple-element.57), channel_id=1, source_target_pairs={{0,2},{2,0},{4,6},{6,4},{8,10},{10,8},{12,14},{14,12},{16,18},{18,... | collective-permute-start | bytes 1572872 | tf_op jit(solution)/shard_map/ppermute | solution.py:629
  14.9 7.4 %collective-permute-start.3 = (bf16[2,2,24,512]{3,2,1,0:T(8,128)(2,1)S(1)}, bf16[2,2,24,512]{3,2,1,0:T(8,128)(2,1)S(1)}, u32[]{:S(2)}, u32[]{:S(2)}) collective-permute-start(bf16[2,2,24,512]{3,2,1,0:T(8,128)(2,1)S(1)} %get-tuple-element.54.refs_0_), channel_id=1, source_target_pairs={{0,8},{2,10},{4,12},{6,14},{8,0},{10,2},{12,4},{14,6},{16,24},{18,... | collective-permute-start | bytes 294920 | tf_op jit(solution)/shard_map/ppermute | solution.py:629
  22.3 2.8 %collective-permute-start.6 = (bf16[4,2,24,512]{3,2,1,0:T(8,128)(2,1)S(1)}, bf16[4,2,24,512]{3,2,1,0:T(8,128)(2,1)S(1)}, u32[]{:S(2)}, u32[]{:S(2)}) collective-permute-start(bf16[4,2,24,512]{3,2,1,0:T(8,128)(2,1)S(1)} %shard_map.92.mine), channel_id=1, source_target_pairs={{0,2},{2,0},{4,6},{6,4},{8,10},{10,8},{12,14},{14,12},{16,18},{18,... | collective-permute-start | bytes 589832 | tf_op jit(solution)/shard_map/ppermute | solution.py:629
  36.4 3.8 %collective-permute-start.7 = (bf16[2,96,512]{2,1,0:T(8,128)(2,1)S(1)}, bf16[2,96,512]{2,1,0:T(8,128)(2,1)S(1)}, u32[]{:S(2)}, u32[]{:S(2)}) collective-permute-start(bf16[2,96,512]{2,1,0:T(8,128)(2,1)S(1)} %get-tuple-element.79), channel_id=1, source_target_pairs={{0,2},{2,0},{4,6},{6,4},{8,10},{10,8},{12,14},{14,12},{16,18},{18,... | collective-permute-start | bytes 589832 | tf_op jit(solution)/shard_map/ppermute | solution.py:629
  40.3 22.0 %collective-permute-start.8 = (bf16[2,256,512]{2,1,0:T(8,128)(2,1)S(1)}, bf16[2,256,512]{2,1,0:T(8,128)(2,1)S(1)}, u32[]{:S(2)}, u32[]{:S(2)}) collective-permute-start(bf16[2,256,512]{2,1,0:T(8,128)(2,1)S(1)} %get-tuple-element.82), channel_id=1, source_target_pairs={{0,2},{2,0},{4,6},{6,4},{8,10},{10,8},{12,14},{14,12},{16,18},{18,... | collective-permute-start | bytes 1572872 | tf_op jit(solution)/shard_map/ppermute | solution.py:629
  40.5 21.7 %collective-permute-start.9 = (bf16[2,256,512]{2,1,0:T(8,128)(2,1)S(1)}, bf16[2,256,512]{2,1,0:T(8,128)(2,1)S(1)}, u32[]{:S(2)}, u32[]{:S(2)}) collective-permute-start(bf16[2,256,512]{2,1,0:T(8,128)(2,1)S(1)} %get-tuple-element.83), channel_id=1, source_target_pairs={{2,4},{6,8},{10,12},{14,16},{18,20},{22,24},{26,28},{4,2},{8,6},{1... | collective-permute-start | bytes 1572872 | tf_op jit(solution)/shard_map/ppermute | solution.py:633
  41.5 12.5 %collective-permute-start.10 = (bf16[2,48,512]{2,1,0:T(8,128)(2,1)S(1)}, bf16[2,48,512]{2,1,0:T(8,128)(2,1)S(1)}, u32[]{:S(2)}, u32[]{:S(2)}) collective-permute-start(bf16[2,48,512]{2,1,0:T(8,128)(2,1)S(1)} %get-tuple-element.85), channel_id=1, source_target_pairs={{0,8},{2,10},{4,12},{6,14},{8,0},{10,2},{12,4},{14,6},{16,24},{18,... | collective-permute-start | bytes 294920 | tf_op jit(solution)/shard_map/ppermute | solution.py:629
  54.0 8.2 %collective-permute-start.12 = (bf16[2,4,512]{2,1,0:T(4,128)(2,1)S(1)}, bf16[2,4,512]{2,1,0:T(4,128)(2,1)S(1)}, u32[]{:S(2)}, u32[]{:S(2)}) collective-permute-start(bf16[2,4,512]{2,1,0:T(4,128)(2,1)S(1)} %get-tuple-element.88), channel_id=1, source_target_pairs={{0,16},{2,18},{4,20},{6,22},{8,24},{10,26},{12,28},{14,30},{16,0},... | collective-permute-start | bytes 24584 | tf_op jit(solution)/shard_map/ppermute | solution.py:629
  56.0 6.2 %collective-permute-start.13 = (bf16[2,4,512]{2,1,0:T(4,128)(2,1)S(1)}, bf16[2,4,512]{2,1,0:T(4,128)(2,1)S(1)}, u32[]{:S(2)}, u32[]{:S(2)}) collective-permute-start(bf16[2,4,512]{2,1,0:T(4,128)(2,1)S(1)} %get-tuple-element.89), channel_id=1, source_target_pairs={{0,20},{2,22},{4,16},{6,18},{8,28},{10,30},{12,24},{14,26},{16,4},... | collective-permute-start | bytes 24584 | tf_op jit(solution)/shard_map/ppermute | solution.py:629
  56.0 6.2 %collective-permute-start.11 = (bf16[2,20,512]{2,1,0:T(8,128)(2,1)S(1)}, bf16[2,20,512]{2,1,0:T(8,128)(2,1)S(1)}, u32[]{:S(2)}, u32[]{:S(2)}) collective-permute-start(bf16[2,20,512]{2,1,0:T(8,128)(2,1)S(1)} %get-tuple-element.87), channel_id=1, source_target_pairs={{0,4},{2,6},{4,0},{6,2},{8,12},{10,14},{12,8},{14,10},{16,20},{18,... | collective-permute-start | bytes 122888 | tf_op jit(solution)/shard_map/ppermute | solution.py:629
  58.4 3.8 %copy-start.2 = (f32[8,256]{1,0:T(8,128)S(1)}, f32[8,256]{1,0:T(8,128)}, u32[]{:S(2)}) copy-start(f32[8,256]{1,0:T(8,128)} %refs_11_.1) | copy-start | bytes 24580
  58.4 3.8 %copy-start.3 = (f32[8,64]{1,0:T(8,128)S(1)}, f32[8,64]{1,0:T(8,128)}, u32[]{:S(2)}) copy-start(f32[8,64]{1,0:T(8,128)} %refs_10_.1) | copy-start | bytes 6148
